TPU v7x, 32 devices: a whole 2x2x4 slice. The times are simulated.
32 devices in a mesh: dp: 8 (over y, x, core), blk: 4 (over z).
Axes of the slice: x: 2, y: 2, z: 4, core: 2. Of those that a mesh axis runs over, the one named last changes fastest.
Arguments:
- tokens: bfloat16 [16, 2048, 768], P('dp', 'blk'), may hold values from -6 to 6
- cotangent: bfloat16 [16, 2048, 768], P('dp', 'blk'), may hold values from -6 to 6
- lengths: int32 [16], P('dp'), may hold values from 512 to 2048, as said below
- query_weight: bfloat16 [768, 768], P(('dp', 'blk')), may hold values from -0.21875 to 0.21875
- key_weight: bfloat16 [768, 768], P(('dp', 'blk')), may hold values from -0.21875 to 0.21875
- value_weight: bfloat16 [768, 768], P(('dp', 'blk')), may hold values from -0.21875 to 0.21875
- output_weight: bfloat16 [768, 768], P(('dp', 'blk')), may hold values from -1.75 to 1.75
- up_weight: bfloat16 [768, 3072], P(('dp', 'blk')), may hold values from -0.21875 to 0.21875
- down_weight: bfloat16 [3072, 768], P(('dp', 'blk')), may hold values from -0.109375 to 0.109375
- query_bias: bfloat16 [768], P(('dp', 'blk')), may hold values from -2 to 2
- value_bias: bfloat16 [768], P(('dp', 'blk')), may hold values from -2 to 2
- output_bias: bfloat16 [768], P(('dp', 'blk')), may hold values from -2 to 2
- up_bias: bfloat16 [3072], P(('dp', 'blk')), may hold values from -2 to 2
- down_bias: bfloat16 [768], P(('dp', 'blk')), may hold values from -2 to 2
- attn_gain: bfloat16 [768], P(('dp', 'blk')), may hold values from 0.5 to 1.5
- attn_shift: bfloat16 [768], P(('dp', 'blk')), may hold values from -2 to 2
- ffn_gain: bfloat16 [768], P(('dp', 'blk')), may hold values from 0.5 to 1.5
- ffn_shift: bfloat16 [768], P(('dp', 'blk')), may hold values from -2 to 2
Outputs:
- layer_out: bfloat16 [16, 2048, 768], P('dp', 'blk')
- tokens_grad: float32 [16, 2048, 768], P('dp', 'blk')
- grad_query_weight: float32 [768, 768], P(('dp', 'blk'))
- grad_key_weight: float32 [768, 768], P(('dp', 'blk'))
- grad_value_weight: float32 [768, 768], P(('dp', 'blk'))
- grad_output_weight: float32 [768, 768], P(('dp', 'blk'))
- grad_up_weight: float32 [768, 3072], P(('dp', 'blk'))
- grad_down_weight: float32 [3072, 768], P(('dp', 'blk'))
- grad_query_bias: float32 [768], P(('dp', 'blk'))
- grad_value_bias: float32 [768], P(('dp', 'blk'))
- grad_output_bias: float32 [768], P(('dp', 'blk'))
- grad_up_bias: float32 [3072], P(('dp', 'blk'))
- grad_down_bias: float32 [768], P(('dp', 'blk'))
- grad_attn_gain: float32 [768], P(('dp', 'blk'))
- grad_attn_shift: float32 [768], P(('dp', 'blk'))
- grad_ffn_gain: float32 [768], P(('dp', 'blk'))
- grad_ffn_shift: float32 [768], P(('dp', 'blk'))
Inputs may be any that keep to these rules, and one draw needn't show every extreme that they name: `lengths`: each sequence is valid up to its length; the first sequence of every data group of 2 has length exactly 2048; the others fall in buckets of at most 2048, 1536 or 1024 positions and hold at least half of their bucket.
All inputs are finite; a program needn't handle non-finite values.
Results may differ from a plain program's by a relative error of at most 0.018.
Values may be sent and summed in bfloat16 or wider, within the bound.
No kernel may reach another device: no remote copies, remote signals or barrier semaphores. Data moves between devices by JAX's collectives and lax.ppermute only.
A program may use at most 384 MiB of HBM per device.

v0:
```python
import jax
import jax.numpy as jnp
from jax import lax
from jax.sharding import PartitionSpec as P

HEADS = 12


def shifted(array, axis, by):
    length = lax.axis_size(axis)
    return lax.ppermute(array, axis, [(i, (i + by) % length) for i in range(length)])


def matmul(left, right):
    return jnp.dot(left, right, preferred_element_type=jnp.float32)


def times_trans(left, right):
    return lax.dot_general(
        left, right, (((1,), (1,)), ((), ())), preferred_element_type=jnp.float32
    )


def trans_times(left, right):
    return lax.dot_general(
        left, right, (((0,), (0,)), ((), ())), preferred_element_type=jnp.float32
    )


def layer_norm(values, gain, shift):
    center = jnp.mean(values, axis=-1, keepdims=True)
    offset = values - center
    spread = jnp.mean(offset * offset, axis=-1, keepdims=True)
    return offset * lax.rsqrt(spread + 1e-12) * gain + shift


def gelu_tanh(values):
    return jax.nn.gelu(values, approximate=True)


def body(
    tokens,
    cotangent,
    lengths,
    query_weight,
    key_weight,
    value_weight,
    output_weight,
    up_weight,
    down_weight,
    query_bias,
    value_bias,
    output_bias,
    up_bias,
    down_bias,
    attn_gain,
    attn_shift,
    ffn_gain,
    ffn_shift,
):
    seqs, stretch, width = tokens.shape
    rows = seqs * stretch
    heads = HEADS
    head = width // heads
    gathered = (
        lax.all_gather(query_weight, ("dp", "blk"), axis=0, tiled=True),
        lax.all_gather(key_weight, ("dp", "blk"), axis=0, tiled=True),
        lax.all_gather(value_weight, ("dp", "blk"), axis=0, tiled=True),
        lax.all_gather(output_weight, ("dp", "blk"), axis=0, tiled=True),
        lax.all_gather(up_weight, ("dp", "blk"), axis=0, tiled=True),
        lax.all_gather(down_weight, ("dp", "blk"), axis=0, tiled=True),
        lax.all_gather(query_bias, ("dp", "blk"), axis=0, tiled=True),
        lax.all_gather(value_bias, ("dp", "blk"), axis=0, tiled=True),
        lax.all_gather(output_bias, ("dp", "blk"), axis=0, tiled=True),
        lax.all_gather(up_bias, ("dp", "blk"), axis=0, tiled=True),
        lax.all_gather(down_bias, ("dp", "blk"), axis=0, tiled=True),
        lax.all_gather(attn_gain, ("dp", "blk"), axis=0, tiled=True),
        lax.all_gather(attn_shift, ("dp", "blk"), axis=0, tiled=True),
        lax.all_gather(ffn_gain, ("dp", "blk"), axis=0, tiled=True),
        lax.all_gather(ffn_shift, ("dp", "blk"), axis=0, tiled=True),
    )
    query_full, key_full, value_full, output_full, upper_full, lower_full = gathered[:6]
    (
        bias_query,
        bias_value,
        bias_output,
        bias_upper,
        bias_lower,
        gain_one,
        shift_one,
        gain_two,
        shift_two,
    ) = [item.astype(jnp.float32) for item in gathered[6:]]
    flat = tokens.reshape(rows, width)
    queries = (matmul(flat, query_full) + bias_query).astype(jnp.bfloat16)
    keys_own = matmul(flat, key_full).astype(jnp.bfloat16)
    values_own = (matmul(flat, value_full) + bias_value).astype(jnp.bfloat16)
    query_heads = queries.reshape(seqs, stretch, heads, head)
    own_block = lax.axis_index("blk")
    cycle_size = lax.axis_size("blk")
    start = jnp.int32(0)
    key_piece = lax.all_gather(keys_own.reshape(seqs, stretch, width), "blk", axis=1, tiled=True)
    value_piece = lax.all_gather(
        values_own.reshape(seqs, stretch, width), "blk", axis=1, tiled=True
    )
    count = key_piece.shape[1]
    span = min(count, stretch)
    row_max = jnp.full((seqs, stretch, heads), -1e30, jnp.float32)
    row_total = jnp.zeros((seqs, stretch, heads), jnp.float32)
    accum = jnp.zeros((seqs, stretch, heads, head), jnp.float32)
    for part_no in range(count // span):
        key_heads = key_piece[:, part_no * span : (part_no + 1) * span].reshape(
            seqs, span, heads, head
        )
        value_heads = value_piece[:, part_no * span : (part_no + 1) * span].reshape(
            seqs, span, heads, head
        )
        positions = start + part_no * span + jnp.arange(span, dtype=jnp.int32)
        valid = positions[None, :] < lengths[:, None]
        scores = (
            jnp.einsum(
                "sqhd,skhd->sqhk", query_heads, key_heads, preferred_element_type=jnp.float32
            )
            * 0.125
        )
        scores = jnp.where(valid[:, None, None, :], scores, -jnp.inf)
        new_max = jnp.maximum(row_max, jnp.max(scores, axis=-1))
        expo = jnp.exp(scores - new_max[..., None])
        factor = jnp.exp(row_max - new_max)
        row_total = row_total * factor + jnp.sum(expo, axis=-1)
        accum = accum * factor[..., None] + jnp.einsum(
            "sqhk,skhd->sqhd",
            expo.astype(jnp.bfloat16),
            value_heads,
            preferred_element_type=jnp.float32,
        )
        row_max = new_max
    row_max, row_total, accum = (row_max, row_total, accum)
    log_total = row_max + jnp.log(row_total)
    context_full = accum / row_total[..., None]
    context = context_full.reshape(rows, width).astype(jnp.bfloat16)
    attended = matmul(context, output_full) + bias_output
    hidden, norm_one_back = jax.vjp(
        layer_norm, flat.astype(jnp.float32) + attended, gain_one, shift_one
    )
    hidden_low = hidden.astype(jnp.bfloat16)
    upward = matmul(hidden_low, upper_full) + bias_upper
    active_full, gelu_back = jax.vjp(gelu_tanh, upward)
    active = active_full.astype(jnp.bfloat16)
    downward = matmul(active, lower_full) + bias_lower
    output_full32, norm_two_back = jax.vjp(layer_norm, hidden + downward, gain_two, shift_two)
    layer_out = output_full32.astype(jnp.bfloat16).reshape(seqs, stretch, width)
    query_back, key_back, value_back, output_back, upper_back, lower_back = (
        lax.all_gather(query_weight, ("dp", "blk"), axis=0, tiled=True),
        lax.all_gather(key_weight, ("dp", "blk"), axis=0, tiled=True),
        lax.all_gather(value_weight, ("dp", "blk"), axis=0, tiled=True),
        lax.all_gather(output_weight, ("dp", "blk"), axis=0, tiled=True),
        lax.all_gather(up_weight, ("dp", "blk"), axis=0, tiled=True),
        lax.all_gather(down_weight, ("dp", "blk"), axis=0, tiled=True),
    )
    grad_outer = cotangent.reshape(rows, width).astype(jnp.float32)
    grad_res_two, grad_gain_two, grad_shift_two = norm_two_back(grad_outer)
    grad_down = grad_res_two.astype(jnp.bfloat16)
    grad_lower_bias = jnp.sum(grad_down, axis=0, dtype=jnp.float32)
    grad_lower = trans_times(active, grad_down)
    grad_active = times_trans(grad_down, lower_back)
    (grad_upward,) = gelu_back(grad_active)
    grad_up = grad_upward.astype(jnp.bfloat16)
    grad_upper_bias = jnp.sum(grad_up, axis=0, dtype=jnp.float32)
    grad_upper = trans_times(hidden_low, grad_up)
    grad_hidden = grad_res_two + times_trans(grad_up, upper_back)
    grad_res_one, grad_gain_one, grad_shift_one = norm_one_back(grad_hidden)
    grad_attended = grad_res_one.astype(jnp.bfloat16)
    grad_output_bias = jnp.sum(grad_attended, axis=0, dtype=jnp.float32)
    grad_output = trans_times(context, grad_attended)
    grad_context = times_trans(grad_attended, output_back).astype(jnp.bfloat16)
    context_grad_heads = grad_context.reshape(seqs, stretch, heads, head)
    delta = jnp.sum(context_grad_heads.astype(jnp.float32) * context_full, axis=-1)

    def contribute(key_value, source, pair_grad, query_grad):
        key_heads = key_value[0]
        value_heads = key_value[1]
        positions = source * stretch + jnp.arange(stretch, dtype=jnp.int32)
        valid = positions[None, :] < lengths[:, None]
        scores = (
            jnp.einsum(
                "sqhd,skhd->sqhk", query_heads, key_heads, preferred_element_type=jnp.float32
            )
            * 0.125
        )
        probs = jnp.where(valid[:, None, None, :], jnp.exp(scores - log_total[..., None]), 0.0)
        grad_probs = jnp.einsum(
            "sqhd,skhd->sqhk", context_grad_heads, value_heads, preferred_element_type=jnp.float32
        )
        grad_scores = (probs * (grad_probs - delta[..., None])).astype(jnp.bfloat16)
        query_grad = (
            query_grad
            + jnp.einsum(
                "sqhk,skhd->sqhd", grad_scores, key_heads, preferred_element_type=jnp.float32
            )
            * 0.125
        )
        key_part = (
            jnp.einsum(
                "sqhk,sqhd->skhd", grad_scores, query_heads, preferred_element_type=jnp.float32
            )
            * 0.125
        )
        value_part = jnp.einsum(
            "sqhk,sqhd->skhd",
            probs.astype(jnp.bfloat16),
            context_grad_heads,
            preferred_element_type=jnp.float32,
        )
        pair_grad = pair_grad + jnp.stack([key_part, value_part])
        return (pair_grad, query_grad)

    def rotate_grads(pair_grad):
        return shifted(pair_grad.astype(jnp.bfloat16), "blk", 1).astype(pair_grad.dtype)

    key_value_own = jnp.stack(
        [
            keys_own.reshape(seqs, stretch, heads, head),
            values_own.reshape(seqs, stretch, heads, head),
        ]
    )
    pair_grad, query_grad = contribute(
        key_value_own,
        own_block,
        jnp.zeros((2, seqs, stretch, heads, head), jnp.float32),
        jnp.zeros((seqs, stretch, heads, head), jnp.float32),
    )

    def cycle_turn(turn, state):
        key_value_now, pair_now, query_now = state
        key_value_now = shifted(key_value_now, "blk", 1)
        pair_now = rotate_grads(pair_now)
        source = (own_block - turn) % cycle_size
        pair_now, query_now = contribute(key_value_now, source, pair_now, query_now)
        return (key_value_now, pair_now, query_now)

    final_state = lax.fori_loop(1, cycle_size, cycle_turn, (key_value_own, pair_grad, query_grad))
    pair_home = rotate_grads(final_state[1])
    grad_queries = final_state[2].reshape(rows, width).astype(jnp.bfloat16)
    grad_keys = pair_home[0].reshape(rows, width).astype(jnp.bfloat16)
    grad_values = pair_home[1].reshape(rows, width).astype(jnp.bfloat16)
    grad_query = trans_times(flat, grad_queries)
    grad_key = trans_times(flat, grad_keys)
    grad_value = trans_times(flat, grad_values)
    grad_query_bias = jnp.sum(grad_queries, axis=0, dtype=jnp.float32)
    grad_value_bias = jnp.sum(grad_values, axis=0, dtype=jnp.float32)
    tokens_grad = (
        grad_res_one
        + times_trans(grad_queries, query_back)
        + times_trans(grad_keys, key_back)
        + times_trans(grad_values, value_back)
    ).reshape(seqs, stretch, width)
    shares = (
        lax.psum_scatter(grad_query, ("dp", "blk"), scatter_dimension=0, tiled=True),
        lax.psum_scatter(grad_key, ("dp", "blk"), scatter_dimension=0, tiled=True),
        lax.psum_scatter(grad_value, ("dp", "blk"), scatter_dimension=0, tiled=True),
        lax.psum_scatter(grad_output, ("dp", "blk"), scatter_dimension=0, tiled=True),
        lax.psum_scatter(grad_upper, ("dp", "blk"), scatter_dimension=0, tiled=True),
        lax.psum_scatter(grad_lower, ("dp", "blk"), scatter_dimension=0, tiled=True),
        lax.psum_scatter(grad_query_bias, ("dp", "blk"), scatter_dimension=0, tiled=True),
        lax.psum_scatter(grad_value_bias, ("dp", "blk"), scatter_dimension=0, tiled=True),
        lax.psum_scatter(grad_output_bias, ("dp", "blk"), scatter_dimension=0, tiled=True),
        lax.psum_scatter(grad_upper_bias, ("dp", "blk"), scatter_dimension=0, tiled=True),
        lax.psum_scatter(grad_lower_bias, ("dp", "blk"), scatter_dimension=0, tiled=True),
        lax.psum_scatter(grad_gain_one, ("dp", "blk"), scatter_dimension=0, tiled=True),
        lax.psum_scatter(grad_shift_one, ("dp", "blk"), scatter_dimension=0, tiled=True),
        lax.psum_scatter(grad_gain_two, ("dp", "blk"), scatter_dimension=0, tiled=True),
        lax.psum_scatter(grad_shift_two, ("dp", "blk"), scatter_dimension=0, tiled=True),
    )
    return (layer_out, tokens_grad) + tuple(shares)


def solution(mesh):
    return jax.shard_map(
        body,
        mesh=mesh,
        in_specs=(
            P("dp", "blk", None),
            P("dp", "blk", None),
            P("dp"),
            P(("dp", "blk"), None),
            P(("dp", "blk"), None),
            P(("dp", "blk"), None),
            P(("dp", "blk"), None),
            P(("dp", "blk"), None),
            P(("dp", "blk"), None),
            P(("dp", "blk")),
            P(("dp", "blk")),
            P(("dp", "blk")),
            P(("dp", "blk")),
            P(("dp", "blk")),
            P(("dp", "blk")),
            P(("dp", "blk")),
            P(("dp", "blk")),
            P(("dp", "blk")),
        ),
        out_specs=(
            P("dp", "blk", None),
            P("dp", "blk", None),
            P(("dp", "blk"), None),
            P(("dp", "blk"), None),
            P(("dp", "blk"), None),
            P(("dp", "blk"), None),
            P(("dp", "blk"), None),
            P(("dp", "blk"), None),
            P(("dp", "blk")),
            P(("dp", "blk")),
            P(("dp", "blk")),
            P(("dp", "blk")),
            P(("dp", "blk")),
            P(("dp", "blk")),
            P(("dp", "blk")),
            P(("dp", "blk")),
            P(("dp", "blk")),
        ),
        check_vma=False,
    )
```

profile of v0, /device:TPU:9, one launch (start us, length us, event | category | flops | bytes accessed | tf_op | source)
XLA Modules:
  0.0 1752.4 jit_solution(5834047516304105900)
XLA Ops:
  9.5 56.2 %all-gather.9.cloned.1.call-done = bf16[768,768]{1,0:T(8,128)(2,1)} async-done(((bf16[24,768]{1,0:T(8,128)(2,1)}), bf16[768,768]{1,0:T(8,128)(2,1)}) %all-gather.9.cloned.1.call-update) | async-done | bytes 1179664 | tf_op jit(solution)/shard_map/all_gather | solution.py:67
  72.3 38.9 %all-reduce.19 = (bf16[768]{0:T(1024)(128)(2,1)S(1)}, bf16[768]{0:T(1024)(128)(2,1)S(1)}, bf16[768]{0:T(1024)(128)(2,1)S(1)}, bf16[768]{0:T(1024)(128)(2,1)S(1)}...) all-reduce(bf16[768]{0:T(1024)(128)(2,1)S(1)} %dynamic-update-slice, ...), channel_id=1, replica_groups=mesh['dp'=8,'blk'=4] {'dp','blk'}, use_global_device_ids=true, to_apply=%add.1 | all-reduce | flops 9216 | bytes 36864
  143.3 34.3 %all-gather.13.cloned.1.call-done = bf16[768,768]{1,0:T(8,128)(2,1)} async-done(((bf16[24,768]{1,0:T(8,128)(2,1)}), bf16[768,768]{1,0:T(8,128)(2,1)}) %all-gather.13.cloned.1.call-update) | async-done | bytes 1179664 | tf_op jit(solution)/shard_map/all_gather | solution.py:66
  204.3 87.3 %all-gather.11.cloned.1.call-done = bf16[2,2048,768]{2,1,0:T(8,128)(2,1)} async-done(((bf16[2,512,768]{2,1,0:T(8,128)(2,1)}), bf16[2,2048,768]{2,1,0:T(8,128)(2,1)}) %all-gather.11.cloned.1.call-update) | async-done | bytes 6291472 | tf_op jit(solution)/shard_map/all_gather | solution.py:102
  306.4 12.7 bitcast_reduce_fusion.3
  353.7 21.7 %fusion.22 = (f32[2,512,12]{1,2,0:T(8,128)S(1)}, f32[2,512,12]{1,2,0:T(8,128)}) fusion(f32[2,12,512,512]{3,2,1,0:T(8,128)} %get-tuple-element.430, f32[2,512,12]{1,2,0:T(8,128)S(1)} %get-tuple-element.417, pred[2,512]{1,0:T(4,128)(4,1)S(1)} %get-tuple-element.422, f32[2,512,12]{1,2,0:T(8,128)S(1)} %get-tuple-element.406, ...), kind=kLoop, calls=%fused_computation.42 | loop fusion | flops 50307072 | bytes 50530304 | tf_op jit(solution)/shard_map/reduce_sum | solution.py:130
  376.7 15.4 fusion.26
  392.1 14.5 all-gather.17.cloned.1.call-done
  420.5 12.8 fusion.44
  433.3 13.2 fusion.42
  446.5 12.9 fusion.40
  459.4 15.9 fusion.107
  483.0 47.5 %all-gather.21.cloned.1.call-done = bf16[768,3072]{1,0:T(8,128)(2,1)} async-done(((bf16[24,3072]{1,0:T(8,128)(2,1)}), bf16[768,3072]{1,0:T(8,128)(2,1)}) %all-gather.21.cloned.1.call-update) | async-done | bytes 4718608 | tf_op jit(solution)/shard_map/all_gather | solution.py:70
  541.2 54.6 %all-gather.23.cloned.1.call-done = bf16[3072,768]{1,0:T(8,128)(2,1)} async-done(((bf16[96,768]{1,0:T(8,128)(2,1)}), bf16[3072,768]{1,0:T(8,128)(2,1)}) %all-gather.23.cloned.1.call-update) | async-done | bytes 4718608 | tf_op jit(solution)/shard_map/all_gather | solution.py:71
  595.8 11.9 fusion.109
  614.3 16.6 convert_reduce_fusion
  648.6 17.3 fusion.15
  682.8 12.0 fusion.64
  701.3 435.4 %while.19 = (s32[]{:T(128)}, bf16[2,2,512,12,64]{2,4,3,1,0:T(8,128)(2,1)}, bf16[2,2,512,12,64]{2,4,3,1,0:T(8,128)(2,1)}, f32[2,512,12,64]{1,3,2,0:T(8,128)}, s32...) while((s32[]{:T(128)}, ...), condition=%wide.region_18.19_spmd, body=%wide.region_17.18_spmd.sunk | while | flops 4098098688 | bytes 206234064 | solution.py:242
  702.2 75.1 %collective-permute-done = bf16[2,2,512,12,64]{2,4,3,1,0:T(8,128)(2,1)S(1)} collective-permute-done((bf16[2,2,512,12,64]{2,4,3,1,0:T(8,128)(2,1)}, bf16[2,2,512,12,64]{2,4,3,1,0:T(8,128)(2,1)S(1)}, u32[]{:S(2)}, u32[]{:S(2)}) %collective-permute-start) | collective-permute-done | bytes 3145760 | tf_op jit(solution)/shard_map/while/body/eval_jaxpr/ppermute | solution.py:11
  789.2 16.6 fusion.180
  850.5 72.0 %collective-permute-done = bf16[2,2,512,12,64]{2,4,3,1,0:T(8,128)(2,1)S(1)} collective-permute-done((bf16[2,2,512,12,64]{2,4,3,1,0:T(8,128)(2,1)}, bf16[2,2,512,12,64]{2,4,3,1,0:T(8,128)(2,1)S(1)}, u32[]{:S(2)}, u32[]{:S(2)}) %collective-permute-start) | collective-permute-done | bytes 3145760 | tf_op jit(solution)/shard_map/while/body/eval_jaxpr/ppermute | solution.py:11
  934.4 16.6 fusion.180
  997.2 67.2 %collective-permute-done = bf16[2,2,512,12,64]{2,4,3,1,0:T(8,128)(2,1)S(1)} collective-permute-done((bf16[2,2,512,12,64]{2,4,3,1,0:T(8,128)(2,1)}, bf16[2,2,512,12,64]{2,4,3,1,0:T(8,128)(2,1)S(1)}, u32[]{:S(2)}, u32[]{:S(2)}) %collective-permute-start) | collective-permute-done | bytes 3145760 | tf_op jit(solution)/shard_map/while/body/eval_jaxpr/ppermute | solution.py:11
  1076.3 16.6 fusion.180
  1148.5 58.3 %collective-permute-done.2 = bf16[2,2,512,12,64]{2,4,3,1,0:T(8,128)(2,1)S(1)} collective-permute-done((bf16[2,2,512,12,64]{2,4,3,1,0:T(8,128)(2,1)}, bf16[2,2,512,12,64]{2,4,3,1,0:T(8,128)(2,1)S(1)}, u32[]{:S(2)}, u32[]{:S(2)}) %collective-permute-start.2) | collective-permute-done | bytes 3145760 | tf_op jit(solution)/shard_map/ppermute | solution.py:11
  1223.5 13.5 fusion.100
  1254.6 51.4 %all-reduce.18 = (f32[768]{0:T(1024)S(1)}, f32[768]{0:T(1024)S(1)}, f32[768]{0:T(1024)S(1)}, f32[3072]{0:T(1024)S(1)}, f32[768]{0:T(1024)S(1)}, /*index=5*/f32[7...) all-reduce(f32[768]{0:T(1024)S(1)} %reduce_sum.248, ...), channel_id=8, replica_groups=mesh['dp'=8,'blk'=4] {'dp','blk'}, use_global_device_ids=true, to_apply=%region_26.27.clone | all-reduce | flops 9216 | bytes 73728
  1318.4 39.5 %reduce-scatter.23.cloned.1.call-done = f32[24,768]{1,0:T(8,128)} async-done(((f32[768,768]{1,0:T(8,128)}), f32[24,768]{1,0:T(8,128)}) %reduce-scatter.23.cloned.1.call-update) | async-done | bytes 73744
  1357.9 104.6 %reduce-scatter.21.cloned.1.call-done = f32[24,768]{1,0:T(8,128)} async-done(((f32[768,768]{1,0:T(8,128)}), f32[24,768]{1,0:T(8,128)}) %reduce-scatter.21.cloned.1.call-update) | async-done | bytes 73744
  1462.6 140.6 %reduce-scatter.17.cloned.1.call-done = f32[96,768]{1,0:T(8,128)} async-done(((f32[3072,768]{1,0:T(8,128)}), f32[96,768]{1,0:T(8,128)}) %reduce-scatter.17.cloned.1.call-update) | async-done | bytes 294928 | tf_op jit(solution)/shard_map/reduce_scatter | solution.py:264
  1603.2 142.2 %reduce-scatter.15.cloned.1.call-done = f32[24,3072]{1,0:T(8,128)} async-done(((f32[768,3072]{1,0:T(8,128)}), f32[24,3072]{1,0:T(8,128)}) %reduce-scatter.15.cloned.1.call-update) | async-done | bytes 294928 | tf_op jit(solution)/shard_map/reduce_scatter | solution.py:263
  (370 shorter events, 427.1 us)
Async XLA Ops:
  7.2 58.4 %all-gather.9.cloned.1.call-start = ((), (), s32[]{:S(2)}) async-start(), calls=%async_computation.6 | async-start | bytes 1216512 | tf_op jit(solution)/shard_map/all_gather | solution.py:67
  7.9 113.6 %all-gather.15.cloned.1.call-start = ((), (), s32[]{:S(2)}) async-start(), calls=%async_computation.9 | async-start | bytes 1216512 | tf_op jit(solution)/shard_map/all_gather | solution.py:68
  8.7 168.9 %all-gather.13.cloned.1.call-start = ((), (), s32[]{:S(2)}) async-start(), calls=%async_computation.8 | async-start | bytes 1216512 | tf_op jit(solution)/shard_map/all_gather | solution.py:66
  9.4 282.2 %all-gather.11.cloned.1.call-start = ((), (), s32[]{:S(2)}) async-start(), calls=%async_computation.7 | async-start | bytes 7864320 | tf_op jit(solution)/shard_map/all_gather | solution.py:102
  70.1 336.5 %all-gather.17.cloned.1.call-start = ((), (), s32[]{:S(2)}) async-start(), calls=%async_computation.10 | async-start | bytes 7864320 | tf_op jit(solution)/shard_map/all_gather | solution.py:103
  125.9 352.7 %all-gather.19.cloned.1.call-start = ((), (), s32[]{:S(2)}) async-start(), calls=%async_computation.11 | async-start | bytes 1216512 | tf_op jit(solution)/shard_map/all_gather | solution.py:69
  126.5 404.1 %all-gather.21.cloned.1.call-start = ((), (), s32[]{:S(2)}) async-start(), calls=%async_computation.12 | async-start | bytes 4866048 | tf_op jit(solution)/shard_map/all_gather | solution.py:70
  127.2 468.5 %all-gather.23.cloned.1.call-start = ((), (), s32[]{:S(2)}) async-start(), calls=%async_computation.13 | async-start | bytes 4866048 | tf_op jit(solution)/shard_map/all_gather | solution.py:71
  128.0 1190.4 %reduce-scatter.13.cloned.1.call-start = ((), (), s32[]{:S(2)}) async-start(), calls=%async_computation.14 | async-start | bytes 2433024 | tf_op jit(solution)/shard_map/reduce_scatter | solution.py:262
  128.7 508.7 %copy-start.36 = (f32[768]{0:T(1024)}, f32[768]{0:T(1024)S(1)}, u32[]{:S(2)}) copy-start(f32[768]{0:T(1024)S(1)} %convert_element_type.195) | copy-start | bytes 9220
  128.7 467.1 %copy-start.38 = (f32[768]{0:T(1024)}, f32[768]{0:T(1024)S(1)}, u32[]{:S(2)}) copy-start(f32[768]{0:T(1024)S(1)} %convert_element_type.196) | copy-start | bytes 9220
  131.7 198.5 %copy-start.45 = (pred[2,512]{1,0:T(4,128)(4,1)}, pred[2,512]{1,0:T(4,128)(4,1)S(1)}, u32[]{:S(2)}) copy-start(pred[2,512]{1,0:T(4,128)(4,1)S(1)} %get-tuple-element.420) | copy-start | bytes 3076
  131.7 209.8 %copy-start.48 = (pred[2,512]{1,0:T(4,128)(4,1)}, pred[2,512]{1,0:T(4,128)(4,1)S(1)}, u32[]{:S(2)}) copy-start(pred[2,512]{1,0:T(4,128)(4,1)S(1)} %get-tuple-element.419) | copy-start | bytes 3076
  185.2 156.4 %copy-start.2 = (bf16[2,512,12,64]{1,0,3,2:T(2,128)(2,1)}, bf16[2,512,12,64]{1,0,3,2:T(2,128)(2,1)S(1)}, u32[]{:S(2)}) copy-start(bf16[2,512,12,64]{1,0,3,2:T(2,128)(2,1)S(1)} %reshape.409) | copy-start | bytes 4718596
  482.5 154.9 %copy-start.4 = (f32[1024,768]{1,0:T(8,128)}, f32[1024,768]{1,0:T(8,128)S(1)}, u32[]{:S(2)}) copy-start(f32[1024,768]{1,0:T(8,128)S(1)} %get-tuple-element.434) | copy-start | bytes 9437188
  482.5 154.9 %copy-start.32 = (f32[1024]{0:T(1024)}, f32[1024]{0:T(1024)S(1)}, u32[]{:S(2)}) copy-start(f32[1024]{0:T(1024)S(1)} %broadcast_multiply_fusion.1) | copy-start | bytes 12292
  483.0 154.4 %copy-start.34 = (f32[1024]{0:T(1024)}, f32[1024]{0:T(1024)S(1)}, u32[]{:S(2)}) copy-start(f32[1024]{0:T(1024)S(1)} %fusion.71) | copy-start | bytes 12292
  483.0 112.7 %copy-start.55 = (f32[3072]{0:T(1024)S(1)}, f32[3072]{0:T(1024)}, u32[]{:S(2)}) copy-start(f32[3072]{0:T(1024)} %convert_element_type.198) | copy-start | bytes 36868
  483.0 112.7 %copy-start.58 = (f32[768]{0:T(1024)S(1)}, f32[768]{0:T(1024)}, u32[]{:S(2)}) copy-start(f32[768]{0:T(1024)} %convert_element_type.200) | copy-start | bytes 9220
  699.2 619.2 %reduce-scatter.19.cloned.1.call-start = ((), (), s32[]{:S(2)}) async-start(), calls=%async_computation.17 | async-start | bytes 2433024
  701.3 76.0 %collective-permute-start = (bf16[2,2,512,12,64]{2,4,3,1,0:T(8,128)(2,1)}, bf16[2,2,512,12,64]{2,4,3,1,0:T(8,128)(2,1)S(1)}, u32[]{:S(2)}, u32[]{:S(2)}) collective-permute-start(bf16[2,2,512,12,64]{2,4,3,1,0:T(8,128)(2,1)} %get-tuple-element.521), channel_id=1, source_target_pairs={{0,1},{1,2},{2,3},{3,0},{4,5},{5,6},{6,7},{7,4},{8,9},{9,10},{10,1... | collective-permute-start | bytes 9437192 | tf_op jit(solution)/shard_map/while/body/eval_jaxpr/ppermute | solution.py:11
  701.8 143.0 %collective-permute-start.1 = (bf16[2,2,512,12,64]{2,4,3,1,0:T(8,128)(2,1)}, bf16[2,2,512,12,64]{2,4,3,1,0:T(8,128)(2,1)}, u32[]{:S(2)}, u32[]{:S(2)}) collective-permute-start(bf16[2,2,512,12,64]{2,4,3,1,0:T(8,128)(2,1)} %get-tuple-element.522), channel_id=1, source_target_pairs={{0,1},{1,2},{2,3},{3,0},{4,5},{5,6},{6,7},{7,4},{8,9},{9,10},{10,1... | collective-permute-start | bytes 9437192 | tf_op jit(solution)/shard_map/while/body/eval_jaxpr/ppermute | solution.py:11
  702.2 76.9 %copy-start.1 = (bf16[2,512,12,64]{1,3,2,0:T(8,128)(2,1)S(1)}, bf16[2,512,12,64]{1,3,2,0:T(8,128)(2,1)}, u32[]{:S(2)}) copy-start(bf16[2,512,12,64]{1,3,2,0:T(8,128)(2,1)} %get-tuple-element.541) | copy-start | bytes 4718596 | tf_op jit(solution)/shard_map/while
  849.6 72.9 %collective-permute-start = (bf16[2,2,512,12,64]{2,4,3,1,0:T(8,128)(2,1)}, bf16[2,2,512,12,64]{2,4,3,1,0:T(8,128)(2,1)S(1)}, u32[]{:S(2)}, u32[]{:S(2)}) collective-permute-start(bf16[2,2,512,12,64]{2,4,3,1,0:T(8,128)(2,1)} %get-tuple-element.521), channel_id=1, source_target_pairs={{0,1},{1,2},{2,3},{3,0},{4,5},{5,6},{6,7},{7,4},{8,9},{9,10},{10,1... | collective-permute-start | bytes 9437192 | tf_op jit(solution)/shard_map/while/body/eval_jaxpr/ppermute | solution.py:11
  850.1 139.9 %collective-permute-start.1 = (bf16[2,2,512,12,64]{2,4,3,1,0:T(8,128)(2,1)}, bf16[2,2,512,12,64]{2,4,3,1,0:T(8,128)(2,1)}, u32[]{:S(2)}, u32[]{:S(2)}) collective-permute-start(bf16[2,2,512,12,64]{2,4,3,1,0:T(8,128)(2,1)} %get-tuple-element.522), channel_id=1, source_target_pairs={{0,1},{1,2},{2,3},{3,0},{4,5},{5,6},{6,7},{7,4},{8,9},{9,10},{10,1... | collective-permute-start | bytes 9437192 | tf_op jit(solution)/shard_map/while/body/eval_jaxpr/ppermute | solution.py:11
  994.8 69.6 %collective-permute-start = (bf16[2,2,512,12,64]{2,4,3,1,0:T(8,128)(2,1)}, bf16[2,2,512,12,64]{2,4,3,1,0:T(8,128)(2,1)S(1)}, u32[]{:S(2)}, u32[]{:S(2)}) collective-permute-start(bf16[2,2,512,12,64]{2,4,3,1,0:T(8,128)(2,1)} %get-tuple-element.521), channel_id=1, source_target_pairs={{0,1},{1,2},{2,3},{3,0},{4,5},{5,6},{6,7},{7,4},{8,9},{9,10},{10,1... | collective-permute-start | bytes 9437192 | tf_op jit(solution)/shard_map/while/body/eval_jaxpr/ppermute | solution.py:11
  996.2 135.7 %collective-permute-start.1 = (bf16[2,2,512,12,64]{2,4,3,1,0:T(8,128)(2,1)}, bf16[2,2,512,12,64]{2,4,3,1,0:T(8,128)(2,1)}, u32[]{:S(2)}, u32[]{:S(2)}) collective-permute-start(bf16[2,2,512,12,64]{2,4,3,1,0:T(8,128)(2,1)} %get-tuple-element.522), channel_id=1, source_target_pairs={{0,1},{1,2},{2,3},{3,0},{4,5},{5,6},{6,7},{7,4},{8,9},{9,10},{10,1... | collective-permute-start | bytes 9437192 | tf_op jit(solution)/shard_map/while/body/eval_jaxpr/ppermute | solution.py:11
  1136.7 70.2 %collective-permute-start.2 = (bf16[2,2,512,12,64]{2,4,3,1,0:T(8,128)(2,1)}, bf16[2,2,512,12,64]{2,4,3,1,0:T(8,128)(2,1)S(1)}, u32[]{:S(2)}, u32[]{:S(2)}) collective-permute-start(bf16[2,2,512,12,64]{2,4,3,1,0:T(8,128)(2,1)} %get-tuple-element.262), channel_id=1, source_target_pairs={{0,1},{1,2},{2,3},{3,0},{4,5},{5,6},{6,7},{7,4},{8,9},{9,10},{10,1... | collective-permute-start | bytes 9437192 | tf_op jit(solution)/shard_map/ppermute | solution.py:11
  1148.5 209.4 %reduce-scatter.23.cloned.1.call-start = ((), (), s32[]{:S(2)}) async-start(), calls=%async_computation.19 | async-start | bytes 2433024
  1216.3 246.2 %reduce-scatter.21.cloned.1.call-start = ((), (), s32[]{:S(2)}) async-start(), calls=%async_computation.18 | async-start | bytes 2433024
  1223.1 380.0 %reduce-scatter.17.cloned.1.call-start = ((), (), s32[]{:S(2)}) async-start(), calls=%async_computation.16 | async-start | bytes 9732096 | tf_op jit(solution)/shard_map/reduce_scatter | solution.py:264
  1237.0 508.4 %reduce-scatter.15.cloned.1.call-start = ((), (), s32[]{:S(2)}) async-start(), calls=%async_computation.15 | async-start | bytes 9732096 | tf_op jit(solution)/shard_map/reduce_scatter | solution.py:263
  (79 other events, 825.0 us)
Sparse Core Ops, SparseCore 0:
  10.8 54.7 all-gather.8
  68.4 53.1 all-gather.14
  124.4 53.1 all-gather.12
  179.6 111.9 all-gather.10
  293.0 113.5 all-gather.16
  409.2 54.6 all-gather.18
  466.7 63.8 all-gather.20
  533.3 62.3 all-gather.22
  699.3 182.5 reduce-scatter.12
  1148.6 105.3 reduce-scatter.18
  1259.9 97.9 reduce-scatter.22
  1364.5 98.0 reduce-scatter.20
  1469.0 134.0 reduce-scatter.16
  1610.5 134.8 reduce-scatter.14
where the time goes:
time: 1760 us; the launch traced here: 1750 us
  waiting for transfers between devices  1030 us (59%)
  matrix products  437 us (25%)
  local copies, waits for them, and re-layouts  93 us (5%)
  blocking collectives  90.3 us (5%)
  other arithmetic  77.9 us (4%)
    ppermute x7, waiting for transfers between devices, shifted(): lax.ppermute(array, axis, [(i, (i + by) % length) for i in range(length)])  298 us
    unnamed x17, waiting for transfers between devices  148 us
    reduce_scatter x1, waiting for transfers between devices, body(): lax.psum_scatter(grad_upper, ('dp', 'blk'), scatter_dimension=0, tiled=True)  142 us
    reduce_scatter x1, waiting for transfers between devices, body(): lax.psum_scatter(grad_lower, ('dp', 'blk'), scatter_dimension=0, tiled=True)  141 us
    unnamed x2, blocking collectives  90.3 us
    all_gather x1, waiting for transfers between devices, body(): lax.all_gather(keys_own.reshape(seqs, stretch, width), 'blk', axis=1, til...  87.3 us
    dot_general x4, matrix products, contribute(): jnp.einsum('sqhd,skhd->sqhk', context_grad_heads, value_heads, preferred_...  66.9 us
    all_gather x1, waiting for transfers between devices, body(): lax.all_gather(key_weight, ('dp', 'blk'), axis=0, tiled=True)  56.2 us
  transfers between devices with their start and end apart: 21, of which 18 were waited for; matrix products, arithmetic and copies ran while one was open for 28% of the time, Pallas kernels for 0%

commit v1 on v0

--- a/solution.py
+++ b/solution.py
@@ -1,9 +1,20 @@
+import functools
+
 import jax
 import jax.numpy as jnp
 from jax import lax
+from jax.experimental import pallas as pl
+from jax.experimental.pallas import tpu as pltpu
+from jax.sharding import Mesh
 from jax.sharding import PartitionSpec as P
 
 HEADS = 12
+LANES = 128
+PER_TILE = 2
+SCORE_SCALE = 0.125 * 1.4426950408889634
+MASKED = -1e30
+ALL = ("pair", "core", "blk")
+VMEM_LIMIT = 56 << 20
 
 
 def shifted(array, axis, by):
@@ -38,7 +49,7 @@
     return jax.nn.gelu(values, approximate=True)
 
 
-def body(
+def ring_body(
     tokens,
     cotangent,
     lengths,
@@ -275,48 +286,500 @@
     return (layer_out, tokens_grad) + tuple(shares)
 
 
+def dot_f32(left, right, dims):
+    return lax.dot_general(left, right, (dims, ((), ())), preferred_element_type=jnp.float32)
+
+
+NT = ((1,), (1,))
+NN = ((1,), (0,))
+
+
+def split_three(values):
+    high = values.astype(jnp.bfloat16).astype(jnp.float32)
+    rest = values - high
+    mid = rest.astype(jnp.bfloat16).astype(jnp.float32)
+    return high, mid, rest - mid
+
+
+def spread_three(lane, base, values, into):
+    for step, part in enumerate(split_three(values)):
+        into = jnp.where(lane == base + step, part, into)
+    return into
+
+
+def fill_keys(info_ref, keys, values, key_aug, value_aug, value_fill, chunk):
+    length = keys.shape[0]
+    lane = lax.broadcasted_iota(jnp.int32, (chunk, LANES), 1)
+    row = lax.broadcasted_iota(jnp.int32, (chunk, LANES), 0)
+    for part in range(length // chunk):
+        at = slice(part * chunk, (part + 1) * chunk)
+        off = (lane == 3) & (row + info_ref[1 + part] >= info_ref[0])
+        mask = jnp.where(off, MASKED, 0.0)
+        for one in range(PER_TILE):
+            mine = lane // (LANES // PER_TILE) == one
+            base = 4 * one
+            minus = (lane >= base) & (lane < base + 3)
+            key_aug[one, at, :LANES] = jnp.where(mine, keys[at], jnp.zeros((), keys.dtype))
+            key_aug[one, at, LANES:] = jnp.where(minus, -1.0, mask).astype(jnp.bfloat16)
+            value_aug[one, at, :LANES] = jnp.where(mine, values[at], jnp.zeros((), keys.dtype))
+            if value_fill:
+                value_aug[one, at, LANES:] = jnp.ones((chunk, LANES), jnp.bfloat16)
+            else:
+                value_aug[one, at, LANES:] = jnp.where(minus, -1.0, 0.0).astype(jnp.bfloat16)
+
+
+def attend_kernel(span, info_ref, query_ref, key_ref, value_ref, out_ref, aux_ref, key_aug, value_aug):
+    length = key_ref.shape[0]
+    tile = query_ref.shape[0]
+    lane = lax.broadcasted_iota(jnp.int32, (1, LANES), 1)
+
+    @pl.when(pl.program_id(1) == 0)
+    def _():
+        fill_keys(info_ref, key_ref, value_ref, key_aug, value_aug, True, length // 8)
+
+    one_lane = jnp.where(lane == 3, 1.0, 0.0)
+    flag = jnp.broadcast_to(one_lane.astype(jnp.bfloat16), (tile, LANES))
+    query = jnp.concatenate([query_ref[...], flag], axis=1)
+    pieces = [slice(at, at + span) for at in range(0, length, span)]
+    scores, peaks = [], []
+    for one in range(PER_TILE):
+        peak = None
+        row = []
+        for at in pieces:
+            score = dot_f32(query, key_aug[one, at], NT)
+            row.append(score)
+            for low in range(0, span, LANES):
+                part = score[:, low : low + LANES]
+                peak = part if peak is None else jnp.maximum(peak, part)
+        scores.append(row)
+        peaks.append(jnp.max(peak, axis=1, keepdims=True))
+    out = None
+    aux = one_lane
+    for one in range(PER_TILE):
+        total = None
+        for at, score in zip(pieces, scores[one]):
+            expo = jnp.exp2((score - peaks[one]) * SCORE_SCALE).astype(jnp.bfloat16)
+            part = dot_f32(expo, value_aug[one, at], NN)
+            total = part if total is None else total + part
+        weight = total[:, LANES:]
+        part = total[:, :LANES] / weight
+        out = part if out is None else out + part
+        log_total = jnp.log2(weight) * (1.0 / SCORE_SCALE) + peaks[one]
+        aux = spread_three(lane, 4 * one, log_total, aux)
+    out_ref[...] = out
+    aux_ref[...] = aux.astype(jnp.bfloat16)
+
+
+def attend(qkv, info, tile, span):
+    length, width = qkv.shape[0], qkv.shape[1] // 3
+    tiles = width // LANES
+    query_spec = pl.BlockSpec((tile, LANES), lambda pair, at: (at, pair))
+    return pl.pallas_call(
+        functools.partial(attend_kernel, span),
+        grid=(tiles, length // tile),
+        in_specs=[
+            pl.BlockSpec(memory_space=pltpu.SMEM),
+            query_spec,
+            pl.BlockSpec((length, LANES), lambda pair, at: (0, tiles + pair)),
+            pl.BlockSpec((length, LANES), lambda pair, at: (0, 2 * tiles + pair)),
+        ],
+        out_specs=[query_spec, query_spec],
+        out_shape=[
+            jax.ShapeDtypeStruct((length, width), jnp.float32),
+            jax.ShapeDtypeStruct((length, width), jnp.bfloat16),
+        ],
+        scratch_shapes=[pltpu.VMEM((PER_TILE, length, 2 * LANES), jnp.bfloat16)] * 2,
+        compiler_params=pltpu.CompilerParams(vmem_limit_bytes=VMEM_LIMIT),
+        cost_estimate=pl.CostEstimate(
+            flops=16 * length * length * width,
+            bytes_accessed=12 * length * width,
+            transcendentals=length * length * width // 64,
+        ),
+        name="attend",
+    )(info, qkv, qkv, qkv)
+
+
+def attend_back_kernel(
+    span, info_ref, query_ref, key_ref, value_ref, grad_ref, out_ref, aux_ref,
+    query_grad_ref, key_grad_ref, value_grad_ref, key_aug, value_aug, key_cols, key_sum, value_sum,
+):
+    length = key_ref.shape[0]
+    tile = query_ref.shape[0]
+    wide = LANES // PER_TILE
+    lane = lax.broadcasted_iota(jnp.int32, (1, LANES), 1)
+
+    @pl.when(pl.program_id(1) == 0)
+    def _():
+        fill_keys(info_ref, key_ref, value_ref, key_aug, value_aug, False, length // 8)
+        key_cols[...] = key_ref[...].T
+        key_sum[...] = jnp.zeros_like(key_sum)
+        value_sum[...] = jnp.zeros_like(value_sum)
+
+    plain, grad = query_ref[...], grad_ref[...]
+    query = jnp.concatenate([plain, aux_ref[...]], axis=1)
+    product = grad.astype(jnp.float32) * out_ref[...]
+    delta = jnp.zeros((tile, LANES), jnp.float32)
+    for one in range(PER_TILE):
+        own = jnp.sum(jnp.where(lane // wide == one, product, 0.0), axis=1, keepdims=True)
+        delta = spread_three(lane, 4 * one, own, delta)
+    grad_aug = jnp.concatenate([grad, delta.astype(jnp.bfloat16)], axis=1)
+    nothing = jnp.zeros((), plain.dtype)
+    query_rows = []
+    for one in range(PER_TILE):
+        mine = lane // wide == one
+        query_own = jnp.where(mine, plain, nothing)
+        grad_own = jnp.where(mine, grad, nothing)
+        total = None
+        for low in range(0, length, span):
+            at = slice(low, low + span)
+            score = dot_f32(key_aug[one, at], query, NT)
+            grad_probs = dot_f32(value_aug[one, at], grad_aug, NT)
+            probs = jnp.exp2(score * SCORE_SCALE)
+            grad_scores = (probs * grad_probs).astype(jnp.bfloat16)
+            value_sum[at] += dot_f32(probs.astype(jnp.bfloat16), grad_own, NN)
+            key_sum[at] += dot_f32(grad_scores, query_own, NN)
+            part = dot_f32(key_cols[wide * one : wide * (one + 1), at], grad_scores, NN)
+            total = part if total is None else total + part
+        query_rows.append(total)
+    query_grad_ref[...] = (jnp.concatenate(query_rows, axis=0).T * 0.125).astype(jnp.bfloat16)
+
+    @pl.when(pl.program_id(1) == pl.num_programs(1) - 1)
+    def _():
+        key_grad_ref[...] = (key_sum[...] * 0.125).astype(jnp.bfloat16)
+        value_grad_ref[...] = value_sum[...].astype(jnp.bfloat16)
+
+
+def attend_back(qkv, grad, out, aux, info, tile, span):
+    length, width = qkv.shape[0], qkv.shape[1] // 3
+    tiles = width // LANES
+    query_spec = pl.BlockSpec((tile, LANES), lambda pair, at: (at, pair))
+    whole = pl.BlockSpec((length, LANES), lambda pair, at: (0, pair))
+    result = jax.ShapeDtypeStruct((length, width), jnp.bfloat16)
+    return pl.pallas_call(
+        functools.partial(attend_back_kernel, span),
+        grid=(tiles, length // tile),
+        in_specs=[
+            pl.BlockSpec(memory_space=pltpu.SMEM),
+            query_spec,
+            pl.BlockSpec((length, LANES), lambda pair, at: (0, tiles + pair)),
+            pl.BlockSpec((length, LANES), lambda pair, at: (0, 2 * tiles + pair)),
+            query_spec,
+            query_spec,
+            query_spec,
+        ],
+        out_specs=[query_spec, whole, whole],
+        out_shape=[result] * 3,
+        scratch_shapes=[pltpu.VMEM((PER_TILE, length, 2 * LANES), jnp.bfloat16)] * 2
+        + [pltpu.VMEM((LANES, length), jnp.bfloat16)]
+        + [pltpu.VMEM((length, LANES), jnp.float32)] * 2,
+        compiler_params=pltpu.CompilerParams(vmem_limit_bytes=VMEM_LIMIT),
+        cost_estimate=pl.CostEstimate(
+            flops=40 * length * length * width,
+            bytes_accessed=22 * length * width,
+            transcendentals=length * length * width // 64,
+        ),
+        name="attend_back",
+    )(info, qkv, qkv, qkv, grad, out, aux)
+
+
+def body(
+    tokens,
+    cotangent,
+    lengths,
+    query_weight,
+    key_weight,
+    value_weight,
+    output_weight,
+    up_weight,
+    down_weight,
+    query_bias,
+    value_bias,
+    output_bias,
+    up_bias,
+    down_bias,
+    attn_gain,
+    attn_shift,
+    ffn_gain,
+    ffn_shift,
+):
+    seqs, stretch, width = tokens.shape
+    rows = seqs * stretch
+    n_pair, n_core, n_blk = (lax.axis_size(axis) for axis in ALL)
+    devices = n_pair * n_core * n_blk
+    core, blk = lax.axis_index("core"), lax.axis_index("blk")
+    half, cols = stretch // 2, width // 2
+    own_rows = n_blk * half
+    share = query_weight.shape[0]
+    bf16, f32 = jnp.bfloat16, jnp.float32
+
+    def exchange_table(step, back):
+        table = []
+        for pair in range(n_pair):
+            for src_core in range(n_core):
+                for src in range(n_blk):
+                    piece = src ^ step
+                    sender = (pair * n_core + src_core) * n_blk + src
+                    target = (pair * n_core + piece % 2) * n_blk + seqs * src_core + piece // 2
+                    table.append((target, sender) if back else (sender, target))
+        return table
+
+    def to_sequence(array):
+        pieces = array.reshape(n_blk, half, array.shape[-1])
+        return [
+            lax.ppermute(
+                lax.dynamic_index_in_dim(pieces, blk ^ step, 0, keepdims=False),
+                ALL,
+                exchange_table(step, False),
+            )
+            for step in range(n_blk)
+        ]
+
+    def from_sequence(chunks):
+        got = [lax.ppermute(c, ALL, exchange_table(step, True)) for step, c in enumerate(chunks)]
+        bit = 1
+        while bit < n_blk:
+            flip = (blk & bit) != 0
+            got = [jnp.where(flip, got[at ^ bit], got[at]) for at in range(n_blk)]
+            bit *= 2
+        return jnp.concatenate(got, axis=0)
+
+    def other_core(array):
+        return lax.ppermute(array, "core", [(0, 1), (1, 0)])
+
+    def columns(array, which):
+        return lax.dynamic_slice_in_dim(array, which * cols, cols, axis=-1)
+
+    def small_block(items, lanes):
+        flat = jnp.concatenate([item.reshape(item.shape[0], -1) for item in items], axis=1)
+        flat = jnp.pad(flat, ((0, 0), (0, lanes - flat.shape[1])))
+        return jnp.pad(flat[:, None, :], ((0, 0), (0, 7), (0, 0)))
+
+    coded = jnp.stack([lengths // 16, lengths % 16]).astype(bf16)
+    first = jnp.concatenate(
+        [query_weight, key_weight, value_weight]
+        + [small_block([query_bias[None], value_bias[None], coded.reshape(1, -1)], width)[0]],
+        axis=0,
+    )
+    second = jnp.concatenate(
+        [output_weight]
+        + [up_weight[:, at : at + width] for at in range(0, up_weight.shape[1], width)]
+        + [down_weight]
+        + [
+            small_block(
+                [
+                    item[None]
+                    for item in (
+                        output_bias, up_bias, down_bias, attn_gain, attn_shift, ffn_gain, ffn_shift
+                    )
+                ],
+                width,
+            )[0]
+        ],
+        axis=0,
+    )
+    first = lax.all_gather(first, ALL, axis=0)
+    second = lax.all_gather(second, ALL, axis=0)
+    mine = columns(first[:, : 3 * share], core).reshape(devices, 3, share, cols)
+    qkv_weight = mine.transpose(0, 2, 1, 3).reshape(width, 3 * cols)
+    small = first[:, 3 * share]
+    bias_query = columns(small[:, :share].reshape(width), core)
+    bias_value = columns(small[:, share : 2 * share].reshape(width), core)
+    qkv_bias = jnp.concatenate([bias_query, jnp.zeros_like(bias_query), bias_value]).astype(f32)
+    code = small[:, 2 * share : 2 * share + 2 * seqs].astype(jnp.int32)
+    code = code.reshape(n_pair, n_core, n_blk, 2, seqs)[:, :, 0]
+    code = code[:, :, 0] * 16 + code[:, :, 1]
+    own_length = code.reshape(n_pair, n_core * seqs)[lax.axis_index("pair"), blk]
+
+    arrived = to_sequence(tokens)
+    own_tokens = jnp.concatenate(arrived, axis=0)
+    sequence = jnp.concatenate([own_tokens, other_core(own_tokens)], axis=0)
+    starts = []
+    for side in (core, 1 - core):
+        piece = 2 * (blk % seqs) + side
+        starts += [(piece ^ step) * stretch + side * half for step in range(n_blk)]
+    info = jnp.stack([own_length] + starts).astype(jnp.int32)
+
+    qkv = (matmul(sequence, qkv_weight) + qkv_bias).astype(bf16)
+    context_seq, aux = attend(qkv, info, 512, 512)
+    context_low = context_seq.astype(bf16)
+    kept, crossed = context_low[:own_rows], other_core(context_low[own_rows:])
+    joined = jnp.concatenate(
+        [jnp.where(core == 0, kept, crossed), jnp.where(core == 0, crossed, kept)], axis=1
+    )
+    context = from_sequence([joined[at : at + half] for at in range(0, own_rows, half)])
+
+    output_full = second[:, :share].reshape(width, width)
+    fold = up_weight.shape[1] // width
+    up_rows = second[:, share : (1 + fold) * share].reshape(devices, fold, share, width)
+    upper_full = up_rows.transpose(0, 2, 1, 3).reshape(width, fold * width)
+    lower_full = second[:, (1 + fold) * share : (1 + 2 * fold) * share].reshape(fold * width, width)
+    small = second[:, (1 + 2 * fold) * share].astype(f32)
+    vectors, at = [], 0
+    for item in (output_bias, up_bias, down_bias, attn_gain, attn_shift, ffn_gain, ffn_shift):
+        vectors.append(small[:, at : at + item.shape[0]].reshape(-1))
+        at += item.shape[0]
+    bias_output, bias_upper, bias_lower, gain_one, shift_one, gain_two, shift_two = vectors
+
+    flat = tokens.reshape(rows, width)
+    attended = matmul(context, output_full) + bias_output
+    hidden, norm_one_back = jax.vjp(layer_norm, flat.astype(f32) + attended, gain_one, shift_one)
+    hidden_low = hidden.astype(bf16)
+    upward = matmul(hidden_low, upper_full) + bias_upper
+    active_full, gelu_back = jax.vjp(gelu_tanh, upward)
+    active = active_full.astype(bf16)
+    downward = matmul(active, lower_full) + bias_lower
+    output_full32, norm_two_back = jax.vjp(layer_norm, hidden + downward, gain_two, shift_two)
+    layer_out = output_full32.astype(bf16).reshape(seqs, stretch, width)
+
+    grad_outer = cotangent.reshape(rows, width).astype(f32)
+    grad_res_two, grad_gain_two, grad_shift_two = norm_two_back(grad_outer)
+    grad_down = grad_res_two.astype(bf16)
+    grad_active = times_trans(grad_down, lower_full)
+    (grad_upward,) = gelu_back(grad_active)
+    grad_up = grad_upward.astype(bf16)
+    grad_hidden = grad_res_two + times_trans(grad_up, upper_full)
+    grad_res_one, grad_gain_one, grad_shift_one = norm_one_back(grad_hidden)
+    grad_attended = grad_res_one.astype(bf16)
+    grad_context = times_trans(grad_attended, output_full).astype(bf16)
+
+    own_grad = jnp.concatenate(
+        to_sequence(grad_context.reshape(seqs, stretch, width)), axis=0
+    )
+    context_grad = jnp.concatenate(
+        [columns(own_grad, core), other_core(columns(own_grad, 1 - core))], axis=0
+    )
+
+    grad_lower = trans_times(active, grad_down)
+    grad_upper = trans_times(hidden_low, grad_up)
+    grad_output = trans_times(context, grad_attended)
+    grad_upper = grad_upper.reshape(devices, share, fold, width).transpose(0, 2, 1, 3)
+    small_grads = small_block(
+        [
+            item.reshape(devices, -1)
+            for item in (
+                jnp.sum(grad_attended, axis=0, dtype=f32),
+                jnp.sum(grad_up, axis=0, dtype=f32),
+                jnp.sum(grad_down, axis=0, dtype=f32),
+                grad_gain_one,
+                grad_shift_one,
+                grad_gain_two,
+                grad_shift_two,
+            )
+        ],
+        width,
+    )
+    second_grads = jnp.concatenate(
+        [
+            grad_output.reshape(devices, share, width).astype(bf16),
+            grad_upper.reshape(devices, fold * share, width).astype(bf16),
+            grad_lower.reshape(devices, fold * share, width).astype(bf16),
+            small_grads.astype(bf16),
+        ],
+        axis=1,
+    )
+    second_grads = lax.psum_scatter(second_grads, ALL, scatter_dimension=0)
+
+    query_grad, key_grad, value_grad = attend_back(
+        qkv, context_grad, context_seq, aux, info, 512, 512
+    )
+    grad_seq = jnp.concatenate([query_grad, key_grad, value_grad], axis=1)
+    partial = times_trans(grad_seq, qkv_weight)
+    summed = (partial[:own_rows] + other_core(partial[own_rows:].astype(bf16)).astype(f32)).astype(bf16)
+    returned = from_sequence([summed[at : at + half] for at in range(0, own_rows, half)])
+    tokens_grad = (grad_res_one + returned.astype(f32)).reshape(seqs, stretch, width)
+
+    def by_owner(array):
+        array = array.reshape((n_pair, n_core, n_blk) + array.shape[1:])
+        return jnp.moveaxis(array, 1, 2).reshape((n_pair * n_blk, n_core) + array.shape[3:])
+
+    grad_qkv = trans_times(sequence, grad_seq).astype(bf16).reshape(devices, share, 3 * cols)
+    bias_sums = [
+        lax.dynamic_update_slice_in_dim(
+            jnp.zeros((width,), f32), jnp.sum(item, axis=0, dtype=f32), core * cols, 0
+        ).reshape(devices, share)
+        for item in (query_grad, value_grad)
+    ]
+    first_grads = jnp.concatenate(
+        [
+            by_owner(grad_qkv).reshape(n_pair * n_blk, n_core * share, 3 * cols),
+            by_owner(small_block(bias_sums, 3 * cols)).reshape(n_pair * n_blk, 16, 3 * cols).astype(bf16),
+        ],
+        axis=1,
+    )
+    first_grads = lax.psum_scatter(first_grads, ("pair", "blk"), scatter_dimension=0)
+
+    def for_core(which):
+        block = lax.dynamic_slice_in_dim(first_grads, which * share, share, axis=0)
+        extra = lax.dynamic_slice_in_dim(first_grads, n_core * share + which * 8, 8, axis=0)
+        return jnp.concatenate([block, extra], axis=0)
+
+    kept, crossed = for_core(core), other_core(for_core(1 - core))
+    bias_both = (kept[share].astype(f32) + crossed[share].astype(f32))
+    left = jnp.where(core == 0, kept, crossed)[:share].astype(f32)
+    right = jnp.where(core == 0, crossed, kept)[:share].astype(f32)
+    projections = tuple(
+        jnp.concatenate([left[:, at : at + cols], right[:, at : at + cols]], axis=1)
+        for at in range(0, 3 * cols, cols)
+    )
+    second_grads = second_grads.astype(f32)
+    out_weight_grad = second_grads[:share]
+    up_weight_grad = jnp.concatenate(
+        [second_grads[at : at + share] for at in range(share, (1 + fold) * share, share)], axis=1
+    )
+    down_weight_grad = second_grads[(1 + fold) * share : (1 + 2 * fold) * share]
+    line = second_grads[(1 + 2 * fold) * share]
+    vectors, at = [], 0
+    for item in (output_bias, up_bias, down_bias, attn_gain, attn_shift, ffn_gain, ffn_shift):
+        vectors.append(line[at : at + item.shape[0]])
+        at += item.shape[0]
+    return (
+        (layer_out, tokens_grad)
+        + projections
+        + (out_weight_grad, up_weight_grad, down_weight_grad)
+        + (bias_both[:share], bias_both[share : 2 * share])
+        + tuple(vectors)
+    )
+
+
+def fits(mesh, tokens, up_weight):
+    n_dp, n_blk = mesh.shape["dp"], mesh.shape["blk"]
+    batch, length, width = tokens.shape
+    if n_dp % 2 or batch % n_dp or 2 * (batch // n_dp) != n_blk or n_blk & (n_blk - 1):
+        return False
+    share = width // (n_dp * n_blk)
+    fold = up_weight.shape[1] // width
+    return (
+        width == HEADS * 64
+        and width % (4 * LANES // PER_TILE) == 0
+        and up_weight.shape[1] == fold * width
+        and share * n_dp * n_blk == width
+        and share % 8 == 0
+        and (6 + fold) * share <= width
+        and length % (16 * n_blk) == 0
+        and length % 512 == 0
+        and length <= 4096
+    )
+
+
 def solution(mesh):
-    return jax.shard_map(
-        body,
-        mesh=mesh,
-        in_specs=(
-            P("dp", "blk", None),
-            P("dp", "blk", None),
-            P("dp"),
-            P(("dp", "blk"), None),
-            P(("dp", "blk"), None),
-            P(("dp", "blk"), None),
-            P(("dp", "blk"), None),
-            P(("dp", "blk"), None),
-            P(("dp", "blk"), None),
-            P(("dp", "blk")),
-            P(("dp", "blk")),
-            P(("dp", "blk")),
-            P(("dp", "blk")),
-            P(("dp", "blk")),
-            P(("dp", "blk")),
-            P(("dp", "blk")),
-            P(("dp", "blk")),
-            P(("dp", "blk")),
-        ),
-        out_specs=(
-            P("dp", "blk", None),
-            P("dp", "blk", None),
-            P(("dp", "blk"), None),
-            P(("dp", "blk"), None),
-            P(("dp", "blk"), None),
-            P(("dp", "blk"), None),
-            P(("dp", "blk"), None),
-            P(("dp", "blk"), None),
-            P(("dp", "blk")),
-            P(("dp", "blk")),
-            P(("dp", "blk")),
-            P(("dp", "blk")),
-            P(("dp", "blk")),
-            P(("dp", "blk")),
-            P(("dp", "blk")),
-            P(("dp", "blk")),
-            P(("dp", "blk")),
-        ),
-        check_vma=False,
-    )
+    n_dp, n_blk = mesh.shape["dp"], mesh.shape["blk"]
+
+    def step(*args):
+        spread = ("dp", "blk")
+        one, use = ring_body, mesh
+        where = {"dp": "dp", "blk": "blk", spread: spread}
+        if fits(mesh, args[0], args[7]):
+            one, use = body, Mesh(mesh.devices.reshape(n_dp // 2, 2, n_blk), ALL)
+            where = {"dp": ("pair", "core"), "blk": "blk", spread: ALL}
+        block = P(where["dp"], where["blk"], None)
+        matrix = P(where[spread], None)
+        vector = P(where[spread])
+        return jax.shard_map(
+            one,
+            mesh=use,
+            in_specs=(block, block, P(where["dp"])) + (matrix,) * 6 + (vector,) * 9,
+            out_specs=(block, block) + (matrix,) * 6 + (vector,) * 9,
+            check_vma=False,
+        )(*args)
+
+    return step

time: 1760 us -> 731 us (0.42)
  waiting for transfers between devices: 1030 us -> 326 us
  matrix products: 437 us -> 100 us
  Pallas kernels: 0 us -> 111 us
  blocking collectives: 90.3 us -> 0 us
  other arithmetic: 77.9 us -> 40.8 us
  starting transfers between devices: 5.44 us -> 41.1 us
    dot_general x28 -> x0, matrix products: 330 us -> none  [the longest x4 66.9 us: contribute(): jnp.einsum('sqhd,skhd->sqhk', context_grad_heads, value_heads, preferred_...]
    all_gather x8 -> x2, waiting for transfers between devices: 305 us -> 10.6 us  [the longest x1 10.6 us: body(): first = lax.all_gather(first, ALL, axis=0)]
    ppermute x7 -> x21, waiting for transfers between devices: 298 us -> 142 us  [the longest x8 81.2 us: from_sequence(): lax.ppermute(c, ALL, exchange_table(step, True))]
    unnamed x17 -> x4, waiting for transfers between devices: 148 us -> 0.07 us
    pallas_call x0 -> x2, Pallas kernels: none -> 111 us  [the longest x1 74.8 us: attend_back(): pl.pallas_call(functools.partial(attend_back_kernel, span), grid=(tiles,...]
    reduce_scatter x3 -> x2, waiting for transfers between devices: 283 us -> 173 us  [the longest x1 138 us: body(): second_grads = lax.psum_scatter(second_grads, ALL, scatter_dimension=0)]
    unnamed x2 -> x0, blocking collectives: 90.3 us -> none
    reduce_sum x7 -> x3, other arithmetic: 44 us -> 1.76 us  [the longest x1 0.93 us: body(): jnp.sum(grad_attended, axis=0, dtype=f32)]
  transfers between devices with their start and end apart: 21 -> 25, of which waited for: 18 -> 21; matrix products, arithmetic and copies ran while one was open for 28% -> 15% of each run, Pallas kernels for 0% -> 5%
where the time goes in v1:
time: 731 us; the launch traced here: 717 us
  waiting for transfers between devices  326 us (45%)
  Pallas kernels  111 us (15%)
  matrix products  100 us (14%)
  local copies, waits for them, and re-layouts  83.1 us (11%)
  starting transfers between devices  41.1 us (6%)
  other arithmetic  40.8 us (6%)
  between operations  15.2 us (2%)
    reduce_scatter x1, waiting for transfers between devices, body(): second_grads = lax.psum_scatter(second_grads, ALL, scatter_dimension=0)  138 us
    ppermute x8, waiting for transfers between devices, from_sequence(): lax.ppermute(c, ALL, exchange_table(step, True))  81.2 us
    pallas_call x1, Pallas kernels, attend_back(): pl.pallas_call(functools.partial(attend_back_kernel, span), grid=(tiles,...  74.8 us
    ppermute x8, waiting for transfers between devices, to_sequence(): lax.ppermute(lax.dynamic_index_in_dim(pieces, blk ^ step, 0, keepdims=Fal...  56 us
    pallas_call x1, Pallas kernels, attend(): pl.pallas_call(functools.partial(attend_kernel, span), grid=(tiles, lengt...  36.5 us
    dot_general x4, matrix products, matmul(): return jnp.dot(left, right, preferred_element_type=jnp.float32)  35.6 us
    reduce_scatter x1, waiting for transfers between devices, body(): lax.psum_scatter(first_grads, ('pair', 'blk'), scatter_dimension=0)  34.3 us
    dot_general x4, matrix products, trans_times(): lax.dot_general(left, right, (((0,), (0,)), ((), ())), preferred_element_...  32.9 us
  transfers between devices with their start and end apart: 25, of which 21 were waited for; matrix products, arithmetic and copies ran while one was open for 15% of the time, Pallas kernels for 5%

profile of v1, /device:TPU:9, one launch (start us, length us, event | category | flops | bytes accessed | tf_op | source)
XLA Modules:
  0.0 717.3 jit_solution(8484783986701984101)
XLA Ops:
  23.2 5.6 collective-permute-start.3
  28.8 5.9 collective-permute-done
  34.7 10.9 %collective-permute-done.1 = bf16[256,768]{1,0:T(8,128)(2,1)S(1)} collective-permute-done((bf16[256,768]{1,0:T(8,128)(2,1)S(1)}, bf16[256,768]{1,0:T(8,128)(2,1)S(1)}, u32[]{:S(2)}, u32[]{:S(2)}) %collective-permute-start.1) | collective-permute-done | bytes 393248 | tf_op jit(solution)/shard_map/ppermute | solution.py:529
  45.6 13.8 %collective-permute-done.2 = bf16[256,768]{1,0:T(8,128)(2,1)S(1)} collective-permute-done((bf16[256,768]{1,0:T(8,128)(2,1)S(1)}, bf16[256,768]{1,0:T(8,128)(2,1)S(1)}, u32[]{:S(2)}, u32[]{:S(2)}) %collective-permute-start.2) | collective-permute-done | bytes 393248 | tf_op jit(solution)/shard_map/ppermute | solution.py:529
  71.7 10.6 %all-gather.5.cloned.1.call-done = bf16[2560,768]{1,0:T(8,128)(2,1)} async-done(((bf16[80,768]{1,0:T(8,128)(2,1)}), bf16[2560,768]{1,0:T(8,128)(2,1)}) %all-gather.5.cloned.1.call-update) | async-done | bytes 3932176 | tf_op jit(solution)/shard_map/all_gather | solution.py:580
  91.2 8.7 %add_convert_fusion.query_ref.key_ref.value_ref = bf16[2048,1152]{1,0:T(8,128)(2,1)} fusion(bf16[2048,768]{1,0:T(8,128)(2,1)} %constant_dynamic-update-slice_fusion, bf16[768,1152]{1,0:T(8,128)(2,1)S(1)} %bitcast.180, f32[1152]{0:T(1024)S(1)} %maximum_convert_fusion), kind=kOutput, calls=%fused_computation.13 | convolution fusion | flops 3628597248 | bytes 9638400 | tf_op jit(solution)/shard_map/dot_general | solution.py:26
  99.9 36.5 %attend.1 = (f32[2048,384]{1,0:T(8,128)}, bf16[2048,384]{1,0:T(8,128)(2,1)}) custom-call(s32[9]{0:T(128)} %stack.50.info_ref, bf16[2048,1152]{1,0:T(8,128)(2,1)} %add_convert_fusion.query_ref.key_ref.value_ref, bf16[2048,1152]{1,0:T(8,128)(2,1)} %add_convert_fusion.query_ref.key_ref.value_ref, bf16[2048,1152]{1,0:T(8,128)(2,1)} %add_convert_fusion.query_ref.key_ref.value_ref), custom_call_target="tpu_custom_call" | custom-call | flops 25769803776 | bytes 9437184 | tf_op jit(solution)/shard_map/attend/pallas_call | solution.py:377
  145.6 4.7 collective-permute-start.9
  150.3 21.8 %collective-permute-done.6 = bf16[256,768]{1,0:T(8,128)(2,1)S(1)} collective-permute-done((bf16[256,768]{1,0:T(8,128)(2,1)S(1)}, bf16[256,768]{1,0:T(8,128)(2,1)S(1)}, u32[]{:S(2)}, u32[]{:S(2)}) %collective-permute-start.6) | collective-permute-done | bytes 393248 | tf_op jit(solution)/shard_map/ppermute | solution.py:538
  172.1 8.3 %collective-permute-done.7 = bf16[256,768]{1,0:T(8,128)(2,1)S(1)} collective-permute-done((bf16[256,768]{1,0:T(8,128)(2,1)S(1)}, bf16[256,768]{1,0:T(8,128)(2,1)S(1)}, u32[]{:S(2)}, u32[]{:S(2)}) %collective-permute-start.7) | collective-permute-done | bytes 393248 | tf_op jit(solution)/shard_map/ppermute | solution.py:538
  180.4 10.0 %collective-permute-done.8 = bf16[256,768]{1,0:T(8,128)(2,1)S(1)} collective-permute-done((bf16[256,768]{1,0:T(8,128)(2,1)S(1)}, bf16[256,768]{1,0:T(8,128)(2,1)S(1)}, u32[]{:S(2)}, u32[]{:S(2)}) %collective-permute-start.8) | collective-permute-done | bytes 393248 | tf_op jit(solution)/shard_map/ppermute | solution.py:538
  190.4 10.1 %collective-permute-done.9 = bf16[256,768]{1,0:T(8,128)(2,1)S(1)} collective-permute-done((bf16[256,768]{1,0:T(8,128)(2,1)S(1)}, bf16[256,768]{1,0:T(8,128)(2,1)S(1)}, u32[]{:S(2)}, u32[]{:S(2)}) %collective-permute-start.9) | collective-permute-done | bytes 393248 | tf_op jit(solution)/shard_map/ppermute | solution.py:538
  203.0 7.9 %fusion.43 = (bf16[32,96,768]{2,1,0:T(8,128)(2,1)}, bf16[32,96,768]{2,1,0:T(8,128)(2,1)}) fusion(bf16[32,224,768]{2,1,0:T(8,128)(2,1)} %bitcast.162), kind=kLoop, calls=%fused_computation.188 | loop fusion | bytes 18874368 | tf_op jit(solution)/shard_map/slice | solution.py:613
  215.3 4.7 copy.78
  229.8 7.5 %fusion.37 = f32[1024,3072]{1,0:T(8,128)S(1)} fusion(bf16[768,3072]{1,0:T(8,128)(2,1)} %bitcast.167, f32[1024,768]{1,0:T(8,128)S(1)} %get-tuple-element.109, f32[768]{0:T(1024)S(1)} %copy-done.30, f32[768]{0:T(1024)S(1)} %copy-done.24, f32[1024]{0:T(1024)S(1)} %fusion.29, f32[1024]{0:T(1024)S(1)} %broadcast_multiply_fusion.1), kind=kOutput, calls=%fused_computation.183 | convolution fusion | flops 4835770368 | bytes 20461568 | tf_op jit(solution)/shard_map/dot_general | solution.py:26
  237.4 15.6 %fusion.51 = (f32[1024]{0:T(1024)S(1)}, f32[1024,768]{1,0:T(8,128)S(1)}) fusion(f32[768]{0:T(1024)S(1)} %copy-done.32, bf16[3072,768]{1,0:T(8,128)(2,1)} %bitcast.171, f32[1024,3072]{1,0:T(8,128)S(1)} %fusion.37, f32[3072]{0:T(1024)S(1)} %add.256, f32[768]{0:T(1024)S(1)} %copy-done.30, f32[768]{0:T(1024)S(1)} %copy-done.24, f32[1024]{0:T(1024)S(1)} %fusion.29, ...), kind=kOutput, calls=%fused_computation.196 | convolution fusion | flops 4868799488 | bytes 23626752 | tf_op jit(solution)/shard_map/dot_general | solution.py:26
  261.2 16.8 %fusion.52 = (bf16[3072]{0:T(1024)(128)(2,1)}, bf16[1024,3072]{1,0:T(8,128)(2,1)S(1)}) fusion(f32[1024,3072]{1,0:T(8,128)} %copy-done.34, f32[3072]{0:T(1024)S(1)} %add.256, bf16[1024,768]{1,0:T(8,128)(2,1)S(1)} %get-tuple-element.33, bf16[3072,768]{1,0:T(8,128)(2,1)} %bitcast.172), kind=kOutput, calls=%fused_computation.197 | convolution fusion | flops 4901041152 | bytes 25184256 | tf_op jit(solution)/shard_map/dot_general | solution.py:30
  278.0 6.6 multiply_reduce_fusion
  310.4 11.8 %collective-permute-done.12 = bf16[256,768]{1,0:T(8,128)(2,1)} collective-permute-done((bf16[256,768]{1,0:T(8,128)(2,1)}, bf16[256,768]{1,0:T(8,128)(2,1)}, u32[]{:S(2)}, u32[]{:S(2)}) %collective-permute-start.12) | collective-permute-done | bytes 393248 | tf_op jit(solution)/shard_map/ppermute | solution.py:529
  326.8 10.1 %convolution_convert_fusion.1 = bf16[768,3072]{1,0:T(8,128)(2,1)} fusion(bf16[1024,3072]{1,0:T(8,128)(2,1)} %copy-done.33, f32[1024,768]{1,0:T(8,128)S(1)} %copy-done.2, f32[768]{0:T(1024)S(1)} %copy-done.31, f32[768]{0:T(1024)S(1)} %copy-done.25, f32[1024]{0:T(1024)S(1)} %copy-done.27, f32[1024]{0:T(1024)S(1)} %copy-done.23), kind=kOutput, calls=%fused_computation.15 | convolution fusion | flops 4838129664 | bytes 14170112 | tf_op jit(solution)/shard_map/dot_general | solution.py:36
  338.2 74.8 %attend_back.1 = (bf16[2048,384]{1,0:T(8,128)(2,1)}, bf16[2048,384]{1,0:T(8,128)(2,1)}, bf16[2048,384]{1,0:T(8,128)(2,1)}) custom-call(s32[9]{0:T(128)} %stack.50.info_ref, bf16[2048,1152]{1,0:T(8,128)(2,1)} %add_convert_fusion.query_ref.key_ref.value_ref, bf16[2048,1152]{1,0:T(8,128)(2,1)} %add_convert_fusion.query_ref.key_ref.value_ref, ...), custom_call_target="tpu_custom_call" | custom-call | flops 64424509440 | bytes 17301504 | tf_op jit(solution)/shard_map/attend_back/pallas_call | solution.py:458
  419.8 7.6 %convolution_convert_fusion.2 = bf16[768,1152]{1,0:T(8,128)(2,1)S(1)} fusion(bf16[2048,768]{1,0:T(8,128)(2,1)} %constant_dynamic-update-slice_fusion, bf16[2048,1152]{1,0:T(8,128)(2,1)} %copy-done.15), kind=kOutput, calls=%fused_computation.22 | convolution fusion | flops 3624763392 | bytes 9633792 | tf_op jit(solution)/shard_map/dot_general | solution.py:36
  437.8 10.1 %convert_element_type.200 = bf16[32,24,4,768]{3,2,1,0:T(4,128)(2,1)} reshape(bf16[768,3072]{1,0:T(8,128)(2,1)} %convolution_convert_fusion.1) | data formatting | bytes 9437184 | tf_op jit(solution)/shard_map/convert_element_type | solution.py:674
  451.3 10.9 %convolution_convert_fusion = bf16[3072,768]{1,0:T(8,128)(2,1)S(1)} fusion(bf16[1024,768]{1,0:T(8,128)(2,1)S(1)} %copy-done.7, f32[1024,3072]{1,0:T(8,128)} %copy-done.34, f32[3072]{0:T(1024)S(1)} %copy-done.29), kind=kOutput, calls=%fused_computation.14 | convolution fusion | flops 4865654784 | bytes 18886656 | tf_op jit(solution)/shard_map/dot_general | solution.py:36
  462.3 5.3 fusion.8
  467.6 6.7 fusion.53
  489.0 8.7 %collective-permute-done.16 = bf16[256,768]{1,0:T(8,128)(2,1)} collective-permute-done((bf16[256,768]{1,0:T(8,128)(2,1)}, bf16[256,768]{1,0:T(8,128)(2,1)}, u32[]{:S(2)}, u32[]{:S(2)}) %collective-permute-start.16) | collective-permute-done | bytes 393248 | tf_op jit(solution)/shard_map/ppermute | solution.py:538
  497.7 6.5 collective-permute-done.17
  504.2 7.2 %collective-permute-done.18 = bf16[256,768]{1,0:T(8,128)(2,1)} collective-permute-done((bf16[256,768]{1,0:T(8,128)(2,1)}, bf16[256,768]{1,0:T(8,128)(2,1)}, u32[]{:S(2)}, u32[]{:S(2)}) %collective-permute-start.18) | collective-permute-done | bytes 393248 | tf_op jit(solution)/shard_map/ppermute | solution.py:538
  511.4 8.5 %collective-permute-done.19 = bf16[256,768]{1,0:T(8,128)(2,1)} collective-permute-done((bf16[256,768]{1,0:T(8,128)(2,1)S(1)}, bf16[256,768]{1,0:T(8,128)(2,1)}, u32[]{:S(2)}, u32[]{:S(2)}) %collective-permute-start.19) | collective-permute-done | bytes 393248 | tf_op jit(solution)/shard_map/ppermute | solution.py:538
  522.5 34.3 %reduce-scatter.3.cloned.1.call-done = bf16[1,64,1152]{2,1,0:T(8,128)(2,1)} async-done(((bf16[16,64,1152]{2,1,0:T(8,128)(2,1)}), bf16[1,64,1152]{2,1,0:T(8,128)(2,1)}) %reduce-scatter.3.cloned.1.call-update) | async-done | bytes 147472 | tf_op jit(solution)/shard_map/reduce_scatter | solution.py:709
  567.5 138.4 %reduce-scatter.5.cloned.1.call-done = bf16[1,224,768]{2,1,0:T(8,128)(2,1)} async-done(((bf16[32,224,768]{2,1,0:T(8,128)(2,1)}), bf16[1,224,768]{2,1,0:T(8,128)(2,1)}) %reduce-scatter.5.cloned.1.call-update) | async-done | bytes 344080 | tf_op jit(solution)/shard_map/reduce_scatter | solution.py:680
  (250 shorter events, 154.9 us)
Async XLA Ops:
  7.2 75.1 %all-gather.5.cloned.1.call-start = ((), (), s32[]{:S(2)}) async-start(), calls=%async_computation.4 | async-start | bytes 4055040 | tf_op jit(solution)/shard_map/all_gather | solution.py:580
  10.2 191.5 %all-gather.7.cloned.1.call-start = ((), (), s32[]{:S(2)}) async-start(), calls=%async_computation.5 | async-start | bytes 11354112 | tf_op jit(solution)/shard_map/all_gather | solution.py:581
  16.7 540.1 %reduce-scatter.3.cloned.1.call-start = ((), (), s32[]{:S(2)}) async-start(), calls=%async_computation.2 | async-start | bytes 2506752 | tf_op jit(solution)/shard_map/reduce_scatter | solution.py:709
  18.3 16.4 %collective-permute-start = (bf16[256,768]{1,0:T(8,128)(2,1)S(1)}, bf16[256,768]{1,0:T(8,128)(2,1)S(1)}, u32[]{:S(2)}, u32[]{:S(2)}) collective-permute-start(bf16[256,768]{1,0:T(8,128)(2,1)S(1)} %get-tuple-element.70), channel_id=1, source_target_pairs={{0,0},{1,4},{2,1},{3,5},{4,2},{5,6},{6,3},{7,7},{8,8},{9,12},{10,9... | collective-permute-start | bytes 1179656 | tf_op jit(solution)/shard_map/ppermute | solution.py:529
  21.5 24.1 %collective-permute-start.1 = (bf16[256,768]{1,0:T(8,128)(2,1)S(1)}, bf16[256,768]{1,0:T(8,128)(2,1)S(1)}, u32[]{:S(2)}, u32[]{:S(2)}) collective-permute-start(bf16[256,768]{1,0:T(8,128)(2,1)S(1)} %get-tuple-element.69), channel_id=1, source_target_pairs={{0,4},{1,0},{2,5},{3,1},{4,6},{5,2},{6,7},{7,3},{8,12},{9,8},{10,1... | collective-permute-start | bytes 1179656 | tf_op jit(solution)/shard_map/ppermute | solution.py:529
  22.5 36.8 %collective-permute-start.2 = (bf16[256,768]{1,0:T(8,128)(2,1)S(1)}, bf16[256,768]{1,0:T(8,128)(2,1)S(1)}, u32[]{:S(2)}, u32[]{:S(2)}) collective-permute-start(bf16[256,768]{1,0:T(8,128)(2,1)S(1)} %get-tuple-element.68), channel_id=1, source_target_pairs={{0,1},{1,5},{2,0},{3,4},{4,3},{5,7},{6,2},{7,6},{8,9},{9,13},{10,8... | collective-permute-start | bytes 1179656 | tf_op jit(solution)/shard_map/ppermute | solution.py:529
  23.2 40.3 %collective-permute-start.3 = (bf16[256,768]{1,0:T(8,128)(2,1)S(1)}, bf16[256,768]{1,0:T(8,128)(2,1)S(1)}, u32[]{:S(2)}, u32[]{:S(2)}) collective-permute-start(bf16[256,768]{1,0:T(8,128)(2,1)S(1)} %get-tuple-element.67), channel_id=1, source_target_pairs={{0,5},{1,1},{2,4},{3,0},{4,7},{5,3},{6,6},{7,2},{8,13},{9,9},{10,1... | collective-permute-start | bytes 1179656 | tf_op jit(solution)/shard_map/ppermute | solution.py:529
  64.3 6.1 collective-permute-start.4
  139.0 2.4 collective-permute-start.5
  141.6 30.4 %collective-permute-start.6 = (bf16[256,768]{1,0:T(8,128)(2,1)S(1)}, bf16[256,768]{1,0:T(8,128)(2,1)S(1)}, u32[]{:S(2)}, u32[]{:S(2)}) collective-permute-start(bf16[256,768]{1,0:T(8,128)(2,1)S(1)} %get-tuple-element.64), channel_id=1, source_target_pairs={{5,0},{1,1},{4,2},{0,3},{7,4},{3,5},{6,6},{2,7},{13,8},{9,9},{12,1... | collective-permute-start | bytes 1179656 | tf_op jit(solution)/shard_map/ppermute | solution.py:538
  143.7 36.7 %collective-permute-start.7 = (bf16[256,768]{1,0:T(8,128)(2,1)S(1)}, bf16[256,768]{1,0:T(8,128)(2,1)S(1)}, u32[]{:S(2)}, u32[]{:S(2)}) collective-permute-start(bf16[256,768]{1,0:T(8,128)(2,1)S(1)} %get-tuple-element.65), channel_id=1, source_target_pairs={{1,0},{5,1},{0,2},{4,3},{3,4},{7,5},{2,6},{6,7},{9,8},{13,9},{8,10... | collective-permute-start | bytes 1179656 | tf_op jit(solution)/shard_map/ppermute | solution.py:538
  143.8 46.7 %collective-permute-start.8 = (bf16[256,768]{1,0:T(8,128)(2,1)S(1)}, bf16[256,768]{1,0:T(8,128)(2,1)S(1)}, u32[]{:S(2)}, u32[]{:S(2)}) collective-permute-start(bf16[256,768]{1,0:T(8,128)(2,1)S(1)} %get-tuple-element.63), channel_id=1, source_target_pairs={{4,0},{0,1},{5,2},{1,3},{6,4},{2,5},{7,6},{3,7},{12,8},{8,9},{13,1... | collective-permute-start | bytes 1179656 | tf_op jit(solution)/shard_map/ppermute | solution.py:538
  145.6 55.0 %collective-permute-start.9 = (bf16[256,768]{1,0:T(8,128)(2,1)S(1)}, bf16[256,768]{1,0:T(8,128)(2,1)S(1)}, u32[]{:S(2)}, u32[]{:S(2)}) collective-permute-start(bf16[256,768]{1,0:T(8,128)(2,1)S(1)} %get-tuple-element.66), channel_id=1, source_target_pairs={{0,0},{4,1},{1,2},{5,3},{2,4},{6,5},{3,6},{7,7},{8,8},{12,9},{9,10... | collective-permute-start | bytes 1179656 | tf_op jit(solution)/shard_map/ppermute | solution.py:538
  229.0 55.6 %copy-start.22 = (f32[1024]{0:T(1024)}, f32[1024]{0:T(1024)S(1)}, u32[]{:S(2)}) copy-start(f32[1024]{0:T(1024)S(1)} %broadcast_multiply_fusion.1) | copy-start | bytes 12292
  229.7 54.9 %copy-start.26 = (f32[1024]{0:T(1024)}, f32[1024]{0:T(1024)S(1)}, u32[]{:S(2)}) copy-start(f32[1024]{0:T(1024)S(1)} %fusion.29) | copy-start | bytes 12292
  229.8 31.4 %copy-start.28 = (f32[3072]{0:T(1024)}, f32[3072]{0:T(1024)S(1)}, u32[]{:S(2)}) copy-start(f32[3072]{0:T(1024)S(1)} %add.256) | copy-start | bytes 36868
  290.0 14.5 %collective-permute-start.10 = (bf16[256,768]{1,0:T(8,128)(2,1)}, bf16[256,768]{1,0:T(8,128)(2,1)}, u32[]{:S(2)}, u32[]{:S(2)}) collective-permute-start(bf16[256,768]{1,0:T(8,128)(2,1)} %get-tuple-element.58), channel_id=1, source_target_pairs={{0,0},{1,4},{2,1},{3,5},{4,2},{5,6},{6,3},{7,7},{8,8},{9,12},{10,9... | collective-permute-start | bytes 1179656 | tf_op jit(solution)/shard_map/ppermute | solution.py:529
  291.9 17.5 %collective-permute-start.11 = (bf16[256,768]{1,0:T(8,128)(2,1)}, bf16[256,768]{1,0:T(8,128)(2,1)}, u32[]{:S(2)}, u32[]{:S(2)}) collective-permute-start(bf16[256,768]{1,0:T(8,128)(2,1)} %get-tuple-element.57), channel_id=1, source_target_pairs={{0,4},{1,0},{2,5},{3,1},{4,6},{5,2},{6,7},{7,3},{8,12},{9,8},{10,1... | collective-permute-start | bytes 1179656 | tf_op jit(solution)/shard_map/ppermute | solution.py:529
  292.7 29.5 %collective-permute-start.12 = (bf16[256,768]{1,0:T(8,128)(2,1)}, bf16[256,768]{1,0:T(8,128)(2,1)}, u32[]{:S(2)}, u32[]{:S(2)}) collective-permute-start(bf16[256,768]{1,0:T(8,128)(2,1)} %get-tuple-element.56), channel_id=1, source_target_pairs={{0,1},{1,5},{2,0},{3,4},{4,3},{5,7},{6,2},{7,6},{8,9},{9,13},{10,8... | collective-permute-start | bytes 1179656 | tf_op jit(solution)/shard_map/ppermute | solution.py:529
  294.7 31.7 %collective-permute-start.13 = (bf16[256,768]{1,0:T(8,128)(2,1)}, bf16[256,768]{1,0:T(8,128)(2,1)S(1)}, u32[]{:S(2)}, u32[]{:S(2)}) collective-permute-start(bf16[256,768]{1,0:T(8,128)(2,1)} %get-tuple-element.55), channel_id=1, source_target_pairs={{0,5},{1,1},{2,4},{3,0},{4,7},{5,3},{6,6},{7,2},{8,13},{9,9},{10,1... | collective-permute-start | bytes 1179656 | tf_op jit(solution)/shard_map/ppermute | solution.py:529
  302.0 24.7 %copy-start.2 = (f32[1024,768]{1,0:T(8,128)S(1)}, f32[1024,768]{1,0:T(8,128)}, u32[]{:S(2)}) copy-start(f32[1024,768]{1,0:T(8,128)} %copy-done) | copy-start | bytes 9437188
  302.0 24.7 %copy-start.23 = (f32[1024]{0:T(1024)S(1)}, f32[1024]{0:T(1024)}, u32[]{:S(2)}) copy-start(f32[1024]{0:T(1024)} %copy-done.22) | copy-start | bytes 12292
  302.1 24.7 %copy-start.25 = (f32[768]{0:T(1024)S(1)}, f32[768]{0:T(1024)}, u32[]{:S(2)}) copy-start(f32[768]{0:T(1024)} %mul.238) | copy-start | bytes 9220
  302.1 24.7 %copy-start.27 = (f32[1024]{0:T(1024)S(1)}, f32[1024]{0:T(1024)}, u32[]{:S(2)}) copy-start(f32[1024]{0:T(1024)} %copy-done.26) | copy-start | bytes 12292
  326.7 10.2 %collective-permute-start.14 = (bf16[1024,384]{1,0:T(8,128)(2,1)S(1)}, bf16[1024,384]{1,0:T(8,128)(2,1)S(1)}, u32[]{:S(2)}, u32[]{:S(2)}) collective-permute-start(bf16[1024,384]{1,0:T(8,128)(2,1)S(1)} %get-tuple-element.54), channel_id=1, source_target_pairs={{0,4},{4,0},{1,5},{5,1},{2,6},{6,2},{3,7},{7,3},{8,12},{12,8},{9,1... | collective-permute-start | bytes 2359304 | tf_op jit(solution)/shard_map/ppermute | solution.py:547
  429.4 276.6 %reduce-scatter.5.cloned.1.call-start = ((), (), s32[]{:S(2)}) async-start(), calls=%async_computation.3 | async-start | bytes 11354112 | tf_op jit(solution)/shard_map/reduce_scatter | solution.py:680
  474.5 3.6 collective-permute-start.15
  479.6 18.1 %collective-permute-start.16 = (bf16[256,768]{1,0:T(8,128)(2,1)}, bf16[256,768]{1,0:T(8,128)(2,1)}, u32[]{:S(2)}, u32[]{:S(2)}) collective-permute-start(bf16[256,768]{1,0:T(8,128)(2,1)} %get-tuple-element.52), channel_id=1, source_target_pairs={{5,0},{1,1},{4,2},{0,3},{7,4},{3,5},{6,6},{2,7},{13,8},{9,9},{12,1... | collective-permute-start | bytes 1179656 | tf_op jit(solution)/shard_map/ppermute | solution.py:538
  484.2 20.0 %collective-permute-start.17 = (bf16[256,768]{1,0:T(8,128)(2,1)}, bf16[256,768]{1,0:T(8,128)(2,1)}, u32[]{:S(2)}, u32[]{:S(2)}) collective-permute-start(bf16[256,768]{1,0:T(8,128)(2,1)} %get-tuple-element.51), channel_id=1, source_target_pairs={{1,0},{5,1},{0,2},{4,3},{3,4},{7,5},{2,6},{6,7},{9,8},{13,9},{8,10... | collective-permute-start | bytes 1179656 | tf_op jit(solution)/shard_map/ppermute | solution.py:538
  484.4 27.0 %collective-permute-start.18 = (bf16[256,768]{1,0:T(8,128)(2,1)}, bf16[256,768]{1,0:T(8,128)(2,1)}, u32[]{:S(2)}, u32[]{:S(2)}) collective-permute-start(bf16[256,768]{1,0:T(8,128)(2,1)} %get-tuple-element.49), channel_id=1, source_target_pairs={{4,0},{0,1},{5,2},{1,3},{6,4},{2,5},{7,6},{3,7},{12,8},{8,9},{13,1... | collective-permute-start | bytes 1179656 | tf_op jit(solution)/shard_map/ppermute | solution.py:538
  485.7 34.3 %collective-permute-start.19 = (bf16[256,768]{1,0:T(8,128)(2,1)S(1)}, bf16[256,768]{1,0:T(8,128)(2,1)}, u32[]{:S(2)}, u32[]{:S(2)}) collective-permute-start(bf16[256,768]{1,0:T(8,128)(2,1)S(1)} %get-tuple-element.50), channel_id=1, source_target_pairs={{0,0},{4,1},{1,2},{5,3},{2,4},{6,5},{3,6},{7,7},{8,8},{12,9},{9,10... | collective-permute-start | bytes 1179656 | tf_op jit(solution)/shard_map/ppermute | solution.py:538
  558.5 6.4 collective-permute-start.20
  (30 other events, 225.4 us)
Sparse Core Ops, SparseCore 0:
  11.4 70.8 all-gather.4
  85.1 106.3 all-gather.6
  429.5 127.3 reduce-scatter.2
  563.7 142.1 reduce-scatter.4

commit v2 on v1

--- a/solution.py
+++ b/solution.py
@@ -482,6 +482,408 @@
     )(info, qkv, qkv, qkv, grad, out, aux)
 
 
+def pack_kernel(query_ref, key_ref, value_ref, output_ref, up_ref, down_ref, small_ref, first_ref, second_ref):
+    share, width = query_ref.shape
+    fold = up_ref.shape[1] // width
+    first_ref[0] = query_ref[...]
+    first_ref[1] = key_ref[...]
+    first_ref[2] = value_ref[...]
+    first_ref[3, :, :LANES] = small_ref[...]
+    first_ref[3, :, LANES:] = jnp.zeros((share, width - LANES), first_ref.dtype)
+    second_ref[0] = output_ref[...]
+    for at in range(fold):
+        second_ref[1 + at] = up_ref[:, at * width : (at + 1) * width]
+        second_ref[1 + fold + at] = down_ref[at * share : (at + 1) * share, :]
+
+
+def pack(matrices, small):
+    share, width = matrices[0].shape
+    fold = matrices[4].shape[1] // width
+    return pl.pallas_call(
+        pack_kernel,
+        out_shape=[
+            jax.ShapeDtypeStruct((4, share, width), jnp.bfloat16),
+            jax.ShapeDtypeStruct((1 + 2 * fold, share, width), jnp.bfloat16),
+        ],
+        compiler_params=pltpu.CompilerParams(vmem_limit_bytes=8 << 20),
+        name="pack",
+    )(*matrices, small)
+
+
+def unspread(pieces, width, share):
+    lane = lax.broadcasted_iota(jnp.int32, (LANES, width), 1)
+    row = lax.broadcasted_iota(jnp.int32, (LANES, width), 0)
+    pick = jnp.where(lax.rem(lane, share) == row, 1.0, 0.0).astype(jnp.bfloat16)
+    spread = dot_f32(pieces, pick, NN)
+    lane = lax.broadcasted_iota(jnp.int32, (pieces.shape[0], width), 1)
+    row = lax.broadcasted_iota(jnp.int32, (pieces.shape[0], width), 0)
+    return jnp.sum(jnp.where(lax.div(lane, share) == row, spread, 0.0), axis=0, keepdims=True)
+
+
+def project_kernel(core_ref, tokens_ref, query_ref, key_ref, value_ref, small_ref, out_ref, bias_ref):
+    devices, _, share, cols = query_ref.shape
+    width = devices * share
+
+    @pl.when(pl.program_id(0) == 0)
+    def _():
+        for at, entry in ((0, 7), (1, 8)):
+            whole = unspread(small_ref[:, 0, entry, :LANES], width, share)
+            bias_ref[at : at + 1, :] = jnp.where(
+                core_ref[0] == 0, whole[:, :cols], whole[:, cols:]
+            )
+
+    tokens = tokens_ref[...]
+    for at, (ref, bias) in enumerate(((query_ref, 0), (key_ref, None), (value_ref, 1))):
+        part = dot_f32(tokens, ref[...].reshape(width, cols), NN)
+        if bias is not None:
+            part = part + bias_ref[bias : bias + 1, :]
+        out_ref[:, at * cols : (at + 1) * cols] = part.astype(out_ref.dtype)
+
+
+def weight_columns(first, unit):
+    devices, _, share, width = first.shape
+    return pl.BlockSpec((devices, 1, share, width // 2), lambda at, core: (0, unit, 0, core[0]))
+
+
+def project(core, sequence, first, tile):
+    length, width = sequence.shape
+    devices, _, share, _ = first.shape
+    cols = width // 2
+    return pl.pallas_call(
+        project_kernel,
+        grid_spec=pltpu.PrefetchScalarGridSpec(
+            num_scalar_prefetch=1,
+            grid=(length // tile,),
+            in_specs=[pl.BlockSpec((tile, width), lambda at, core: (at, 0))]
+            + [weight_columns(first, unit) for unit in range(3)]
+            + [pl.BlockSpec((devices, 1, share, width), lambda at, core: (0, 3, 0, 0))],
+            out_specs=pl.BlockSpec((tile, 3 * cols), lambda at, core: (at, 0)),
+            scratch_shapes=[pltpu.VMEM((8, cols), jnp.float32)],
+        ),
+        out_shape=jax.ShapeDtypeStruct((length, 3 * cols), jnp.bfloat16),
+        compiler_params=pltpu.CompilerParams(vmem_limit_bytes=VMEM_LIMIT),
+        cost_estimate=pl.CostEstimate(
+            flops=6 * length * width * cols, bytes_accessed=10 * length * width, transcendentals=0
+        ),
+        name="project",
+    )(core, sequence, first, first, first, first)
+
+
+def norm(values, gain, shift):
+    center = jnp.mean(values, axis=1, keepdims=True)
+    offset = values - center
+    scale = lax.rsqrt(jnp.mean(offset * offset, axis=1, keepdims=True) + 1e-12)
+    unit = offset * scale
+    return unit * gain + shift, unit, scale
+
+
+def norm_back(grad, gain, unit, scale):
+    inner = grad * gain
+    mean = jnp.mean(inner, axis=1, keepdims=True)
+    return scale * (inner - mean - unit * jnp.mean(inner * unit, axis=1, keepdims=True))
+
+
+def feed_kernel(
+    context_ref, tokens_ref, cotangent_ref, small_ref, weights_ref,
+    out_ref, active_ref, grad_down_ref, grad_up_ref, hidden_ref, res_ref, attended_ref, context_grad_ref, sum_ref,
+    weight_ref, vector_ref, slope_ref, sems,
+):
+    devices, _, share, width = weights_ref.shape
+    fold = active_ref.shape[1] // width
+    group = devices // fold
+    step = pl.program_id(0)
+    f32, bf16 = jnp.float32, jnp.bfloat16
+
+    def copy(unit):
+        if unit <= fold:
+            return pltpu.make_async_copy(weights_ref.at[:, unit], weight_ref.at[unit], sems.at[unit])
+        first = group * (unit - 1 - fold)
+        return pltpu.make_async_copy(
+            weights_ref.at[pl.ds(first, group), pl.ds(1 + fold, fold)],
+            weight_ref.at[unit].reshape(group, fold, share, width),
+            sems.at[unit],
+        )
+
+    @pl.when(step == 0)
+    def _():
+        for unit in range(1 + 2 * fold):
+            copy(unit).start()
+        sum_ref[...] = jnp.zeros_like(sum_ref)
+        for entry in range(7):
+            spread, wide = (fold * share, fold * width) if entry == 1 else (share, width)
+            vector_ref[entry : entry + 1, :wide] = unspread(
+                small_ref[:, 0, entry, :LANES], wide, spread
+            )
+
+    def ready(unit):
+        @pl.when(step == 0)
+        def _():
+            copy(unit).wait()
+
+    def weight(unit):
+        return weight_ref[unit].reshape(width, width)
+
+    def vector(entry, low=0):
+        return vector_ref[entry : entry + 1, low : low + width]
+
+    def add_sum(entry, value):
+        sum_ref[entry : entry + 1, :] += jnp.sum(value, axis=0, keepdims=True)
+
+    ready(0)
+    attended = dot_f32(context_ref[...], weight(0), NN) + vector(0)
+    hidden, unit_one, scale_one = norm(tokens_ref[...].astype(f32) + attended, vector(3), vector(4))
+    hidden_low = hidden.astype(bf16)
+    hidden_ref[...] = hidden_low
+    down = vector(2)
+    for at in range(fold):
+        low = at * width
+        ready(1 + at)
+        up = dot_f32(hidden_low, weight(1 + at), NN) + vector(1, low)
+        square = up * up
+        tanh = jnp.tanh(0.7978845608 * up * (1.0 + 0.044715 * square))
+        half = 0.5 * (1.0 + tanh)
+        active = (up * half).astype(bf16)
+        rise = (0.5 * 0.7978845608) * up * (1.0 - tanh * tanh)
+        slope_ref[at] = half + rise * (1.0 + (3 * 0.044715) * square)
+        active_ref[:, low : low + width] = active
+        ready(1 + fold + at)
+        down = down + dot_f32(active, weight(1 + fold + at), NN)
+    out, unit_two, scale_two = norm(hidden + down, vector(5), vector(6))
+    out_ref[...] = out.astype(bf16)
+    cotangent = cotangent_ref[...].astype(f32)
+    add_sum(4, cotangent * unit_two)
+    add_sum(5, cotangent)
+    grad = norm_back(cotangent, vector(5), unit_two, scale_two)
+    grad_down = grad.astype(bf16)
+    grad_down_ref[...] = grad_down
+    add_sum(1, grad_down.astype(f32))
+    for at in range(fold):
+        low = at * width
+        grad_active = dot_f32(grad_down, weight(1 + fold + at), NT)
+        grad_up = (grad_active * slope_ref[at]).astype(bf16)
+        grad_up_ref[:, low : low + width] = grad_up
+        add_sum(6 + at, grad_up.astype(f32))
+        grad = grad + dot_f32(grad_up, weight(1 + at), NT)
+    add_sum(2, grad * unit_one)
+    add_sum(3, grad)
+    res_one = norm_back(grad, vector(3), unit_one, scale_one)
+    res_ref[...] = res_one
+    grad_attended = res_one.astype(bf16)
+    attended_ref[...] = grad_attended
+    add_sum(0, grad_attended.astype(f32))
+    context_grad_ref[...] = dot_f32(grad_attended, weight(0), NT).astype(bf16)
+
+
+def feed(context, tokens, cotangent, first, second, tile):
+    rows, width = context.shape
+    devices, units, share, _ = second.shape
+    fold = (units - 1) // 2
+    thin = pl.BlockSpec((tile, width), lambda at: (at, 0))
+    wide = pl.BlockSpec((tile, fold * width), lambda at: (at, 0))
+    sums = (6 + fold + 7) // 8 * 8
+
+    def like(columns, dtype):
+        return jax.ShapeDtypeStruct((rows, columns), dtype)
+
+    bf16, f32 = jnp.bfloat16, jnp.float32
+    return pl.pallas_call(
+        feed_kernel,
+        grid=(rows // tile,),
+        in_specs=[
+            thin,
+            thin,
+            thin,
+            pl.BlockSpec((devices, 1, share, width), lambda at: (0, 3, 0, 0)),
+            pl.BlockSpec(memory_space=pl.ANY),
+        ],
+        out_specs=[thin, wide, thin, wide, thin, thin, thin, thin, pl.BlockSpec((sums, width), lambda at: (0, 0))],
+        out_shape=[
+            like(width, bf16),
+            like(fold * width, bf16),
+            like(width, bf16),
+            like(fold * width, bf16),
+            like(width, bf16),
+            like(width, f32),
+            like(width, bf16),
+            like(width, bf16),
+            jax.ShapeDtypeStruct((sums, width), f32),
+        ],
+        scratch_shapes=[
+            pltpu.VMEM((units, devices, share, width), bf16),
+            pltpu.VMEM((8, fold * width), f32),
+            pltpu.VMEM((fold, tile, width), f32),
+            pltpu.SemaphoreType.DMA((units,)),
+        ],
+        compiler_params=pltpu.CompilerParams(vmem_limit_bytes=VMEM_LIMIT),
+        cost_estimate=pl.CostEstimate(
+            flops=4 * rows * width * width * (1 + 2 * fold),
+            bytes_accessed=rows * width * (20 + 4 * fold) + 2 * units * width * width,
+            transcendentals=rows * width * fold,
+        ),
+        name="feed",
+    )(context, tokens, cotangent, first, second)
+
+
+TN = ((0,), (0,))
+
+
+def weight_grad_kernel(
+    active_ref, grad_down_ref, hidden_ref, grad_up_ref, context_ref, attended_ref, sum_ref, out_ref, block_ref, small_ref, sems
+):
+    devices, units, share, width = out_ref.shape
+    fold = (units - 2) // 2
+    group = devices // fold
+    step = pl.program_id(0)
+
+    def block(slot):
+        return block_ref.at[slot]
+
+    def column_copy(unit, slot):
+        return pltpu.make_async_copy(block(slot), out_ref.at[:, unit], sems.at[slot])
+
+    def row_copy(at, slot):
+        return pltpu.make_async_copy(
+            block(slot).reshape(group, fold, share, width),
+            out_ref.at[pl.ds(group * at, group), pl.ds(1 + fold, fold)],
+            sems.at[slot],
+        )
+
+    def small_copy():
+        return pltpu.make_async_copy(small_ref, out_ref.at[:, 1 + 2 * fold], sems.at[2])
+
+    def store(left, right, slot):
+        block_ref[slot] = dot_f32(left, right, TN).astype(out_ref.dtype).reshape(devices, share, width)
+
+    slot = lax.rem(step, 2)
+
+    @pl.when(step >= 2)
+    def _():
+        column_copy(0, slot).wait()
+
+    @pl.when(step == 0)
+    def _():
+        rows = jnp.concatenate(
+            [sum_ref[...], jnp.zeros((share - sum_ref.shape[0], width), jnp.float32)], axis=0
+        ).astype(out_ref.dtype)
+        small_ref[...] = jnp.broadcast_to(rows[None], small_ref.shape)
+        small_copy().start()
+        store(context_ref[...], attended_ref[...], 0)
+        column_copy(0, 0).start()
+
+    @pl.when((step >= 1) & (step <= fold))
+    def _():
+        store(hidden_ref[...], grad_up_ref[...], slot)
+        column_copy(step, slot).start()
+
+    @pl.when(step > fold)
+    def _():
+        store(active_ref[...], grad_down_ref[...], slot)
+        row_copy(step - 1 - fold, slot).start()
+
+    @pl.when(step == 2 * fold)
+    def _():
+        small_copy().wait()
+        column_copy(0, 0).wait()
+        column_copy(0, 1).wait()
+
+
+def weight_grads(active, grad_down, hidden, grad_up, context, attended, sums, devices):
+    rows, width = context.shape
+    fold = active.shape[1] // width
+    share, units = width // devices, 2 + 2 * fold
+    whole = pl.BlockSpec((rows, width), lambda at: (0, 0))
+    return pl.pallas_call(
+        weight_grad_kernel,
+        grid=(1 + 2 * fold,),
+        in_specs=[
+            pl.BlockSpec((rows, width), lambda at: (0, jnp.maximum(at - 1 - fold, 0))),
+            whole,
+            whole,
+            pl.BlockSpec((rows, width), lambda at: (0, jnp.clip(at - 1, 0, fold - 1))),
+            whole,
+            whole,
+            pl.BlockSpec(sums.shape, lambda at: (0, 0)),
+        ],
+        out_specs=pl.BlockSpec(memory_space=pl.ANY),
+        out_shape=jax.ShapeDtypeStruct((devices, units, share, width), jnp.bfloat16),
+        scratch_shapes=[
+            pltpu.VMEM((2, devices, share, width), jnp.bfloat16),
+            pltpu.VMEM((devices, share, width), jnp.bfloat16),
+            pltpu.SemaphoreType.DMA((3,)),
+        ],
+        compiler_params=pltpu.CompilerParams(vmem_limit_bytes=VMEM_LIMIT),
+        cost_estimate=pl.CostEstimate(
+            flops=2 * rows * width * width * (1 + 2 * fold),
+            bytes_accessed=2 * (rows + devices * share) * width * units,
+            transcendentals=0,
+        ),
+        name="weight_grads",
+    )(active, grad_down, hidden, grad_up, context, attended, sums)
+
+
+def finish_kernel(
+    core_ref, query_grad_ref, key_grad_ref, value_grad_ref, tokens_ref, query_ref, key_ref, value_ref,
+    partial_ref, out_ref, sum_ref, bias_ref,
+):
+    devices, _, share, cols = query_ref.shape
+    width = devices * share
+    step = pl.program_id(0)
+
+    @pl.when(step == 0)
+    def _():
+        sum_ref[...] = jnp.zeros_like(sum_ref)
+        bias_ref[...] = jnp.zeros_like(bias_ref)
+
+    tokens = tokens_ref[...]
+    total = None
+    for at, (grad_ref, ref) in enumerate(
+        ((query_grad_ref, query_ref), (key_grad_ref, key_ref), (value_grad_ref, value_ref))
+    ):
+        grad = grad_ref[...]
+        here = slice(at * cols, (at + 1) * cols)
+        part = dot_f32(grad, ref[...].reshape(width, cols), NT)
+        total = part if total is None else total + part
+        sum_ref[:, here] += dot_f32(tokens, grad, TN)
+        bias_ref[0:1, here] += jnp.sum(grad.astype(jnp.float32), axis=0, keepdims=True)
+    partial_ref[...] = total.astype(partial_ref.dtype)
+
+    @pl.when(step == pl.num_programs(0) - 1)
+    def _():
+        out_ref[:, :share, :] = sum_ref[...].astype(out_ref.dtype).reshape(devices, share, 3 * cols)
+        bias = bias_ref[...].astype(out_ref.dtype)
+        out_ref[:, share:, :] = jnp.broadcast_to(bias[None], (devices, 8, 3 * cols))
+
+
+def finish(core, grads, sequence, first, tile):
+    length, width = sequence.shape
+    devices, _, share, _ = first.shape
+    cols = width // 2
+    thin = pl.BlockSpec((tile, cols), lambda at, core: (at, 0))
+    full = pl.BlockSpec((tile, width), lambda at, core: (at, 0))
+    return pl.pallas_call(
+        finish_kernel,
+        grid_spec=pltpu.PrefetchScalarGridSpec(
+            num_scalar_prefetch=1,
+            grid=(length // tile,),
+            in_specs=[thin] * 3 + [full] + [weight_columns(first, unit) for unit in range(3)],
+            out_specs=[full, pl.BlockSpec((devices, share + 8, 3 * cols), lambda at, core: (0, 0, 0))],
+            scratch_shapes=[
+                pltpu.VMEM((width, 3 * cols), jnp.float32),
+                pltpu.VMEM((8, 3 * cols), jnp.float32),
+            ],
+        ),
+        out_shape=[
+            jax.ShapeDtypeStruct((length, width), jnp.bfloat16),
+            jax.ShapeDtypeStruct((devices, share + 8, 3 * cols), jnp.bfloat16),
+        ],
+        compiler_params=pltpu.CompilerParams(vmem_limit_bytes=VMEM_LIMIT),
+        cost_estimate=pl.CostEstimate(
+            flops=12 * length * width * cols, bytes_accessed=10 * length * width, transcendentals=0
+        ),
+        name="finish",
+    )(core, *grads, sequence, first, first, first)
+
+
 def body(
     tokens,
     cotangent,
@@ -506,10 +908,11 @@
     rows = seqs * stretch
     n_pair, n_core, n_blk = (lax.axis_size(axis) for axis in ALL)
     devices = n_pair * n_core * n_blk
-    core, blk = lax.axis_index("core"), lax.axis_index("blk")
+    pair, core, blk = (lax.axis_index(axis) for axis in ALL)
     half, cols = stretch // 2, width // 2
     own_rows = n_blk * half
     share = query_weight.shape[0]
+    fold = up_weight.shape[1] // width
     bf16, f32 = jnp.bfloat16, jnp.float32
 
     def exchange_table(step, back):
@@ -549,46 +952,31 @@
     def columns(array, which):
         return lax.dynamic_slice_in_dim(array, which * cols, cols, axis=-1)
 
-    def small_block(items, lanes):
-        flat = jnp.concatenate([item.reshape(item.shape[0], -1) for item in items], axis=1)
-        flat = jnp.pad(flat, ((0, 0), (0, lanes - flat.shape[1])))
-        return jnp.pad(flat[:, None, :], ((0, 0), (0, 7), (0, 0)))
-
-    coded = jnp.stack([lengths // 16, lengths % 16]).astype(bf16)
-    first = jnp.concatenate(
-        [query_weight, key_weight, value_weight]
-        + [small_block([query_bias[None], value_bias[None], coded.reshape(1, -1)], width)[0]],
-        axis=0,
-    )
-    second = jnp.concatenate(
-        [output_weight]
-        + [up_weight[:, at : at + width] for at in range(0, up_weight.shape[1], width)]
-        + [down_weight]
-        + [
-            small_block(
-                [
-                    item[None]
-                    for item in (
-                        output_bias, up_bias, down_bias, attn_gain, attn_shift, ffn_gain, ffn_shift
-                    )
-                ],
-                width,
-            )[0]
-        ],
-        axis=0,
+    def halve(array, bit, inner):
+        side = (pair & bit) // bit
+        array = array.reshape((-1, 2, inner) + array.shape[1:])
+        kept = lax.dynamic_index_in_dim(array, side, 1, keepdims=False)
+        sent = lax.dynamic_index_in_dim(array, 1 - side, 1, keepdims=False)
+        got = lax.ppermute(sent, "pair", [(at, at ^ bit) for at in range(n_pair)])
+        total = (kept.astype(f32) + got.astype(f32)).astype(bf16)
+        return total.reshape((-1,) + total.shape[2:])
+
+    vectors = (output_bias, up_bias, down_bias, attn_gain, attn_shift, ffn_gain, ffn_shift)
+    coded = jnp.concatenate([lengths // 16, lengths % 16]).astype(bf16)
+    small = [
+        jnp.pad(item, (0, LANES - item.shape[0]))
+        for item in vectors + (query_bias, value_bias, coded)
+    ]
+    small = jnp.pad(jnp.stack(small), ((0, share - len(small)), (0, 0)))
+    first, second = pack(
+        (query_weight, key_weight, value_weight, output_weight, up_weight, down_weight), small
     )
     first = lax.all_gather(first, ALL, axis=0)
     second = lax.all_gather(second, ALL, axis=0)
-    mine = columns(first[:, : 3 * share], core).reshape(devices, 3, share, cols)
-    qkv_weight = mine.transpose(0, 2, 1, 3).reshape(width, 3 * cols)
-    small = first[:, 3 * share]
-    bias_query = columns(small[:, :share].reshape(width), core)
-    bias_value = columns(small[:, share : 2 * share].reshape(width), core)
-    qkv_bias = jnp.concatenate([bias_query, jnp.zeros_like(bias_query), bias_value]).astype(f32)
-    code = small[:, 2 * share : 2 * share + 2 * seqs].astype(jnp.int32)
-    code = code.reshape(n_pair, n_core, n_blk, 2, seqs)[:, :, 0]
-    code = code[:, :, 0] * 16 + code[:, :, 1]
-    own_length = code.reshape(n_pair, n_core * seqs)[lax.axis_index("pair"), blk]
+    code = first[:, 3, 9, : 2 * seqs].astype(jnp.int32)
+    code = (code[:, :seqs] * 16 + code[:, seqs:]).reshape(n_pair, n_core, n_blk, seqs)[:, :, 0]
+    own_length = code.reshape(n_pair, n_core * seqs)[pair, blk]
+    which = jnp.reshape(core, (1,)).astype(jnp.int32)
 
     arrived = to_sequence(tokens)
     own_tokens = jnp.concatenate(arrived, axis=0)
@@ -599,7 +987,7 @@
         starts += [(piece ^ step) * stretch + side * half for step in range(n_blk)]
     info = jnp.stack([own_length] + starts).astype(jnp.int32)
 
-    qkv = (matmul(sequence, qkv_weight) + qkv_bias).astype(bf16)
+    qkv = project(which, sequence, first, 512)
     context_seq, aux = attend(qkv, info, 512, 512)
     context_low = context_seq.astype(bf16)
     kept, crossed = context_low[:own_rows], other_core(context_low[own_rows:])
@@ -608,143 +996,75 @@
     )
     context = from_sequence([joined[at : at + half] for at in range(0, own_rows, half)])
 
-    output_full = second[:, :share].reshape(width, width)
-    fold = up_weight.shape[1] // width
-    up_rows = second[:, share : (1 + fold) * share].reshape(devices, fold, share, width)
-    upper_full = up_rows.transpose(0, 2, 1, 3).reshape(width, fold * width)
-    lower_full = second[:, (1 + fold) * share : (1 + 2 * fold) * share].reshape(fold * width, width)
-    small = second[:, (1 + 2 * fold) * share].astype(f32)
-    vectors, at = [], 0
-    for item in (output_bias, up_bias, down_bias, attn_gain, attn_shift, ffn_gain, ffn_shift):
-        vectors.append(small[:, at : at + item.shape[0]].reshape(-1))
-        at += item.shape[0]
-    bias_output, bias_upper, bias_lower, gain_one, shift_one, gain_two, shift_two = vectors
-
-    flat = tokens.reshape(rows, width)
-    attended = matmul(context, output_full) + bias_output
-    hidden, norm_one_back = jax.vjp(layer_norm, flat.astype(f32) + attended, gain_one, shift_one)
-    hidden_low = hidden.astype(bf16)
-    upward = matmul(hidden_low, upper_full) + bias_upper
-    active_full, gelu_back = jax.vjp(gelu_tanh, upward)
-    active = active_full.astype(bf16)
-    downward = matmul(active, lower_full) + bias_lower
-    output_full32, norm_two_back = jax.vjp(layer_norm, hidden + downward, gain_two, shift_two)
-    layer_out = output_full32.astype(bf16).reshape(seqs, stretch, width)
-
-    grad_outer = cotangent.reshape(rows, width).astype(f32)
-    grad_res_two, grad_gain_two, grad_shift_two = norm_two_back(grad_outer)
-    grad_down = grad_res_two.astype(bf16)
-    grad_active = times_trans(grad_down, lower_full)
-    (grad_upward,) = gelu_back(grad_active)
-    grad_up = grad_upward.astype(bf16)
-    grad_hidden = grad_res_two + times_trans(grad_up, upper_full)
-    grad_res_one, grad_gain_one, grad_shift_one = norm_one_back(grad_hidden)
-    grad_attended = grad_res_one.astype(bf16)
-    grad_context = times_trans(grad_attended, output_full).astype(bf16)
-
-    own_grad = jnp.concatenate(
-        to_sequence(grad_context.reshape(seqs, stretch, width)), axis=0
-    )
+    layer_out, active, grad_down, grad_up, hidden, grad_res, grad_attended, grad_context, sums = feed(
+        context, tokens.reshape(rows, width), cotangent.reshape(rows, width), first, second, 256
+    )
+    own_grad = jnp.concatenate(to_sequence(grad_context), axis=0)
     context_grad = jnp.concatenate(
         [columns(own_grad, core), other_core(columns(own_grad, 1 - core))], axis=0
     )
 
-    grad_lower = trans_times(active, grad_down)
-    grad_upper = trans_times(hidden_low, grad_up)
-    grad_output = trans_times(context, grad_attended)
-    grad_upper = grad_upper.reshape(devices, share, fold, width).transpose(0, 2, 1, 3)
-    small_grads = small_block(
-        [
-            item.reshape(devices, -1)
-            for item in (
-                jnp.sum(grad_attended, axis=0, dtype=f32),
-                jnp.sum(grad_up, axis=0, dtype=f32),
-                jnp.sum(grad_down, axis=0, dtype=f32),
-                grad_gain_one,
-                grad_shift_one,
-                grad_gain_two,
-                grad_shift_two,
-            )
-        ],
-        width,
-    )
-    second_grads = jnp.concatenate(
-        [
-            grad_output.reshape(devices, share, width).astype(bf16),
-            grad_upper.reshape(devices, fold * share, width).astype(bf16),
-            grad_lower.reshape(devices, fold * share, width).astype(bf16),
-            small_grads.astype(bf16),
-        ],
-        axis=1,
-    )
+    second_grads = weight_grads(
+        active, grad_down, hidden, grad_up, context, grad_attended, sums, devices
+    )
+    context_grad, second_grads = lax.optimization_barrier((context_grad, second_grads))
     second_grads = lax.psum_scatter(second_grads, ALL, scatter_dimension=0)
 
-    query_grad, key_grad, value_grad = attend_back(
-        qkv, context_grad, context_seq, aux, info, 512, 512
-    )
-    grad_seq = jnp.concatenate([query_grad, key_grad, value_grad], axis=1)
-    partial = times_trans(grad_seq, qkv_weight)
-    summed = (partial[:own_rows] + other_core(partial[own_rows:].astype(bf16)).astype(f32)).astype(bf16)
+    grads = attend_back(qkv, context_grad, context_seq, aux, info, 512, 512)
+    partial, first_grads = finish(which, grads, sequence, first, 512)
+    crossed = other_core(partial[own_rows:])
+    summed = (partial[:own_rows].astype(f32) + crossed.astype(f32)).astype(bf16)
     returned = from_sequence([summed[at : at + half] for at in range(0, own_rows, half)])
-    tokens_grad = (grad_res_one + returned.astype(f32)).reshape(seqs, stretch, width)
-
-    def by_owner(array):
-        array = array.reshape((n_pair, n_core, n_blk) + array.shape[1:])
-        return jnp.moveaxis(array, 1, 2).reshape((n_pair * n_blk, n_core) + array.shape[3:])
-
-    grad_qkv = trans_times(sequence, grad_seq).astype(bf16).reshape(devices, share, 3 * cols)
-    bias_sums = [
-        lax.dynamic_update_slice_in_dim(
-            jnp.zeros((width,), f32), jnp.sum(item, axis=0, dtype=f32), core * cols, 0
-        ).reshape(devices, share)
-        for item in (query_grad, value_grad)
-    ]
-    first_grads = jnp.concatenate(
-        [
-            by_owner(grad_qkv).reshape(n_pair * n_blk, n_core * share, 3 * cols),
-            by_owner(small_block(bias_sums, 3 * cols)).reshape(n_pair * n_blk, 16, 3 * cols).astype(bf16),
-        ],
-        axis=1,
-    )
-    first_grads = lax.psum_scatter(first_grads, ("pair", "blk"), scatter_dimension=0)
-
-    def for_core(which):
-        block = lax.dynamic_slice_in_dim(first_grads, which * share, share, axis=0)
-        extra = lax.dynamic_slice_in_dim(first_grads, n_core * share + which * 8, 8, axis=0)
-        return jnp.concatenate([block, extra], axis=0)
-
-    kept, crossed = for_core(core), other_core(for_core(1 - core))
-    bias_both = (kept[share].astype(f32) + crossed[share].astype(f32))
-    left = jnp.where(core == 0, kept, crossed)[:share].astype(f32)
-    right = jnp.where(core == 0, crossed, kept)[:share].astype(f32)
-    projections = tuple(
+    tokens_grad = (grad_res + returned.astype(f32)).reshape(seqs, stretch, width)
+
+    first_grads = first_grads.reshape(n_pair, n_core, n_blk, share + 8, 3 * cols)
+    bits = [1 << at for at in range(n_pair.bit_length() - 1)]
+    sides = []
+    for side in range(n_core):
+        part = first_grads[:, side]
+        for bit in bits if side else bits[::-1]:
+            part = halve(part, bit, 1 if side else bit)
+        sides.append(part.reshape(n_blk, share + 8, 3 * cols))
+    part = jnp.stack(sides, axis=1)
+    total = lax.dynamic_index_in_dim(part, blk, 0, keepdims=False).astype(f32)
+    for step in range(1, n_blk):
+        sent = lax.dynamic_index_in_dim(part, blk ^ step, 0, keepdims=False)
+        total += lax.ppermute(sent, "blk", [(at, at ^ step) for at in range(n_blk)]).astype(f32)
+    total = total.astype(bf16)
+    kept = lax.dynamic_index_in_dim(total, core, 0, keepdims=False)
+    crossed = other_core(lax.dynamic_index_in_dim(total, 1 - core, 0, keepdims=False))
+    left = jnp.where(core == 0, kept, crossed).astype(f32)
+    right = jnp.where(core == 0, crossed, kept).astype(f32)
+    projections = [
         jnp.concatenate([left[:, at : at + cols], right[:, at : at + cols]], axis=1)
         for at in range(0, 3 * cols, cols)
-    )
+    ]
+    device = (pair * n_core + core) * n_blk + blk
+
+    def own_part(line, size):
+        return lax.dynamic_slice_in_dim(line, device * size, size, axis=-1)
+
     second_grads = second_grads.astype(f32)
-    out_weight_grad = second_grads[:share]
-    up_weight_grad = jnp.concatenate(
-        [second_grads[at : at + share] for at in range(share, (1 + fold) * share, share)], axis=1
-    )
-    down_weight_grad = second_grads[(1 + fold) * share : (1 + 2 * fold) * share]
-    line = second_grads[(1 + 2 * fold) * share]
-    vectors, at = [], 0
-    for item in (output_bias, up_bias, down_bias, attn_gain, attn_shift, ffn_gain, ffn_shift):
-        vectors.append(line[at : at + item.shape[0]])
-        at += item.shape[0]
+    lines = second_grads[1 + 2 * fold]
+    own_lines = own_part(lines[:6], share)
     return (
-        (layer_out, tokens_grad)
-        + projections
-        + (out_weight_grad, up_weight_grad, down_weight_grad)
-        + (bias_both[:share], bias_both[share : 2 * share])
-        + tuple(vectors)
+        (layer_out.reshape(seqs, stretch, width), tokens_grad)
+        + tuple(item[:share] for item in projections)
+        + (
+            second_grads[0],
+            jnp.concatenate([second_grads[1 + at] for at in range(fold)], axis=1),
+            second_grads[1 + fold : 1 + 2 * fold].reshape(fold * share, width),
+        )
+        + (own_part(projections[0][share], share), own_part(projections[2][share], share))
+        + (own_lines[0], own_part(lines[6 : 6 + fold].reshape(-1), fold * share), own_lines[1])
+        + (own_lines[2], own_lines[3], own_lines[4], own_lines[5])
     )
 
 
 def fits(mesh, tokens, up_weight):
     n_dp, n_blk = mesh.shape["dp"], mesh.shape["blk"]
     batch, length, width = tokens.shape
-    if n_dp % 2 or batch % n_dp or 2 * (batch // n_dp) != n_blk or n_blk & (n_blk - 1):
+    if n_dp % 2 or n_dp & (n_dp - 1) or batch % n_dp or 2 * (batch // n_dp) != n_blk or n_blk & (n_blk - 1):
         return False
     share = width // (n_dp * n_blk)
     fold = up_weight.shape[1] // width
@@ -754,6 +1074,8 @@
         and up_weight.shape[1] == fold * width
         and share * n_dp * n_blk == width
         and share % 8 == 0
+        and 16 <= share
+        and fold * share <= LANES
         and (6 + fold) * share <= width
         and length % (16 * n_blk) == 0
         and length % 512 == 0

time: 731 us -> 526 us (0.72); the launches traced: 717 us -> 522 us
  waiting for transfers between devices: 326 us -> 211 us
  matrix products: 100 us -> 0 us
  Pallas kernels: 111 us -> 201 us
  local copies, waits for them, and re-layouts: 83.1 us -> 23.3 us
  other arithmetic: 40.8 us -> 21 us
  starting transfers between devices: 41.1 us -> 51.6 us
    reduce_scatter x1, waiting for transfers between devices: 138 us -> 0.01 us  [body(): second_grads = lax.psum_scatter(second_grads, ALL, scatter_dimension=0)]
    dot_general x12 -> x0, matrix products: 100 us -> none  [the longest x4 35.6 us: matmul(): return jnp.dot(left, right, preferred_element_type=jnp.float32)]
    pallas_call x0 -> x5, Pallas kernels: none -> 89.4 us  [the longest x1 44 us: feed(): pl.pallas_call(feed_kernel, grid=(rows // tile,), in_specs=[thin, thin, t...]
    ppermute x0 -> x7, waiting for transfers between devices: none -> 37 us  [the longest x4 25.2 us: halve(): got = lax.ppermute(sent, 'pair', [(at, at ^ bit) for at in range(n_pair)])]
    reduce_scatter x1 -> x0, waiting for transfers between devices: 34.3 us -> none  [body(): lax.psum_scatter(first_grads, ('pair', 'blk'), scatter_dimension=0)]
    unnamed x96 -> x43, local copies, waits for them, and re-layouts: 25.4 us -> 7.58 us
    slice x15 -> x6, local copies, waits for them, and re-layouts: 19.3 us -> 3.98 us  [the longest x1 1.88 us: body(): part = first_grads[:, side]]
    convert_element_type x4 -> x1, local copies, waits for them, and re-layouts: 13.6 us -> 0.08 us  [body(): code = first[:, 3, 9, :2 * seqs].astype(jnp.int32)]
  transfers between devices with their start and end apart: 25 -> 31, of which waited for: 21 -> 25; matrix products, arithmetic and copies ran while one was open for 15% -> 5% of each run, Pallas kernels for 5% -> 30%
where the time goes in v2:
time: 526 us; the launch traced here: 522 us
  waiting for transfers between devices  211 us (40%)
  Pallas kernels  201 us (38%)
  starting transfers between devices  51.6 us (10%)
  local copies, waits for them, and re-layouts  23.3 us (4%)
  other arithmetic  21 us (4%)
  between operations  14.3 us (3%)
    ppermute x8, waiting for transfers between devices, from_sequence(): lax.ppermute(c, ALL, exchange_table(step, True))  85.5 us
    pallas_call x1, Pallas kernels, attend_back(): pl.pallas_call(functools.partial(attend_back_kernel, span), grid=(tiles,...  74.8 us
    ppermute x8, waiting for transfers between devices, to_sequence(): lax.ppermute(lax.dynamic_index_in_dim(pieces, blk ^ step, 0, keepdims=Fal...  63.2 us
    pallas_call x1, Pallas kernels, feed(): pl.pallas_call(feed_kernel, grid=(rows // tile,), in_specs=[thin, thin, t...  44 us
    pallas_call x1, Pallas kernels, attend(): pl.pallas_call(functools.partial(attend_kernel, span), grid=(tiles, lengt...  36.5 us
    ppermute x4, waiting for transfers between devices, halve(): got = lax.ppermute(sent, 'pair', [(at, at ^ bit) for at in range(n_pair)])  25.2 us
    pallas_call x1, Pallas kernels, weight_grads(): pl.pallas_call(weight_grad_kernel, grid=(1 + 2 * fold,), in_specs=[pl.Blo...  20.1 us
    ppermute x8, starting transfers between devices, to_sequence(): lax.ppermute(lax.dynamic_index_in_dim(pieces, blk ^ step, 0, keepdims=Fal...  19.7 us
  transfers between devices with their start and end apart: 31, of which 25 were waited for; matrix products, arithmetic and copies ran while one was open for 5% of the time, Pallas kernels for 30%

profile of v2, /device:TPU:9, one launch (start us, length us, event | category | flops | bytes accessed | tf_op | source)
XLA Modules:
  0.0 522.3 jit_solution(35413020601265954)
XLA Ops:
  24.4 5.6 %collective-permute-start.3 = (bf16[256,768]{1,0:T(8,128)(2,1)S(1)}, bf16[256,768]{1,0:T(8,128)(2,1)S(1)}, u32[]{:S(2)}, u32[]{:S(2)}) collective-permute-start(bf16[256,768]{1,0:T(8,128)(2,1)S(1)} %get-tuple-element.83), channel_id=1, source_target_pairs={{0,5},{1,1},{2,4},{3,0},{4,7},{5,3},{6,6},{7,2},{8,13},{9,9},{10,1... | collective-permute-start | bytes 1179656 | tf_op jit(solution)/shard_map/ppermute | solution.py:932
  30.0 3.7 collective-permute-done
  33.7 11.9 %collective-permute-done.1 = bf16[256,768]{1,0:T(8,128)(2,1)S(1)} collective-permute-done((bf16[256,768]{1,0:T(8,128)(2,1)S(1)}, bf16[256,768]{1,0:T(8,128)(2,1)S(1)}, u32[]{:S(2)}, u32[]{:S(2)}) %collective-permute-start.1) | collective-permute-done | bytes 393248 | tf_op jit(solution)/shard_map/ppermute | solution.py:932
  45.6 16.0 %collective-permute-done.2 = bf16[256,768]{1,0:T(8,128)(2,1)S(1)} collective-permute-done((bf16[256,768]{1,0:T(8,128)(2,1)S(1)}, bf16[256,768]{1,0:T(8,128)(2,1)S(1)}, u32[]{:S(2)}, u32[]{:S(2)}) %collective-permute-start.2) | collective-permute-done | bytes 393248 | tf_op jit(solution)/shard_map/ppermute | solution.py:932
  61.6 4.7 collective-permute-done.3
  72.9 19.6 %all-gather.5.cloned.1.call-done = bf16[128,24,768]{2,1,0:T(8,128)(2,1)} async-done(((bf16[4,24,768]{2,1,0:T(8,128)(2,1)}), bf16[128,24,768]{2,1,0:T(8,128)(2,1)}) %all-gather.5.cloned.1.call-update) | async-done | bytes 4718608 | tf_op jit(solution)/shard_map/all_gather | solution.py:974
  95.6 9.2 %project.1.query_ref.key_ref.value_ref = bf16[2048,1152]{1,0:T(8,128)(2,1)} custom-call(s32[1]{0:T(128)} %bitcast.22.core_ref, bf16[2048,768]{1,0:T(8,128)(2,1)} %copy-done.6, bf16[32,4,24,768]{3,2,1,0:T(8,128)(2,1)} %bitcast.128, bf16[32,4,24,768]{3,2,1,0:T(8,128)(2,1)} %bitcast.129, bf16[32,4,24,768]{3,2,1,0:T(8,128)(2,1)} %bitcast.130, ...), custom_call_target="tpu_custom_call" | custom-call | flops 3623878656 | bytes 15728640 | tf_op jit(solution)/shard_map/project/pallas_call | solution.py:552
  104.7 36.5 %attend.1 = (f32[2048,384]{1,0:T(8,128)}, bf16[2048,384]{1,0:T(8,128)(2,1)}) custom-call(s32[9]{0:T(128)} %stack.82.info_ref, bf16[2048,1152]{1,0:T(8,128)(2,1)} %project.1.query_ref.key_ref.value_ref, bf16[2048,1152]{1,0:T(8,128)(2,1)} %project.1.query_ref.key_ref.value_ref, bf16[2048,1152]{1,0:T(8,128)(2,1)} %project.1.query_ref.key_ref.value_ref), custom_call_target="tpu_custom_call" | custom-call | flops 25769803776 | bytes 9437184 | tf_op jit(solution)/shard_map/attend/pallas_call | solution.py:377
  149.2 5.1 collective-permute-start.9
  154.3 22.5 %collective-permute-done.6 = bf16[256,768]{1,0:T(8,128)(2,1)S(1)} collective-permute-done((bf16[256,768]{1,0:T(8,128)(2,1)S(1)}, bf16[256,768]{1,0:T(8,128)(2,1)S(1)}, u32[]{:S(2)}, u32[]{:S(2)}) %collective-permute-start.6) | collective-permute-done | bytes 393248 | tf_op jit(solution)/shard_map/ppermute | solution.py:941
  176.8 7.7 %collective-permute-done.7 = bf16[256,768]{1,0:T(8,128)(2,1)S(1)} collective-permute-done((bf16[256,768]{1,0:T(8,128)(2,1)S(1)}, bf16[256,768]{1,0:T(8,128)(2,1)S(1)}, u32[]{:S(2)}, u32[]{:S(2)}) %collective-permute-start.7) | collective-permute-done | bytes 393248 | tf_op jit(solution)/shard_map/ppermute | solution.py:941
  184.5 11.0 %collective-permute-done.8 = bf16[256,768]{1,0:T(8,128)(2,1)S(1)} collective-permute-done((bf16[256,768]{1,0:T(8,128)(2,1)S(1)}, bf16[256,768]{1,0:T(8,128)(2,1)S(1)}, u32[]{:S(2)}, u32[]{:S(2)}) %collective-permute-start.8) | collective-permute-done | bytes 393248 | tf_op jit(solution)/shard_map/ppermute | solution.py:941
  195.6 13.2 %collective-permute-done.9 = bf16[256,768]{1,0:T(8,128)(2,1)S(1)} collective-permute-done((bf16[256,768]{1,0:T(8,128)(2,1)S(1)}, bf16[256,768]{1,0:T(8,128)(2,1)S(1)}, u32[]{:S(2)}, u32[]{:S(2)}) %collective-permute-start.9) | collective-permute-done | bytes 393248 | tf_op jit(solution)/shard_map/ppermute | solution.py:941
  210.2 44.0 %feed.1 = (bf16[1024,768]{1,0:T(8,128)(2,1)}, bf16[1024,3072]{1,0:T(8,128)(2,1)}, bf16[1024,768]{1,0:T(8,128)(2,1)}, bf16[1024,3072]{1,0:T(8,128)(2,1)}, bf16[10...) custom-call(bf16[1024,768]{1,0:T(8,128)(2,1)} %pad_maximum_fusion.1., ...), custom_call_target="tpu_custom_call" | custom-call | flops 21743271936 | bytes 38928384 | tf_op jit(solution)/shard_map/feed/pallas_call | solution.py:689
  260.5 4.4 collective-permute-start.13
  264.9 5.0 collective-permute-done.10
  270.0 4.8 collective-permute-done.11
  274.8 12.9 %collective-permute-done.12 = bf16[256,768]{1,0:T(8,128)(2,1)S(1)} collective-permute-done((bf16[256,768]{1,0:T(8,128)(2,1)S(1)}, bf16[256,768]{1,0:T(8,128)(2,1)S(1)}, u32[]{:S(2)}, u32[]{:S(2)}) %collective-permute-start.12) | collective-permute-done | bytes 393248 | tf_op jit(solution)/shard_map/ppermute | solution.py:932
  287.7 4.2 collective-permute-done.13
  292.2 20.1 %weight_grads.1 = bf16[32,10,24,768]{3,2,1,0:T(8,128)(2,1)} custom-call(bf16[1024,3072]{1,0:T(8,128)(2,1)} %get-tuple-element.43.active_ref, bf16[1024,768]{1,0:T(8,128)(2,1)} %get-tuple-element.44.grad_down_ref, bf16[1024,768]{1,0:T(8,128)(2,1)} %get-tuple-element.45.hidden_ref, bf16[1024,3072]{1,0:T(8,128)(2,1)} %get-tuple-element.46.grad_up_ref, ...), custom_call_target="tpu_custom_call" | custom-call | flops 10871635968 | bytes 27525120 | tf_op jit(solution)/shard_map/weight_grads/pallas_call | solution.py:795
  313.6 74.8 %attend_back.1 = (bf16[2048,384]{1,0:T(8,128)(2,1)}, bf16[2048,384]{1,0:T(8,128)(2,1)}, bf16[2048,384]{1,0:T(8,128)(2,1)}) custom-call(s32[9]{0:T(128)} %stack.82.info_ref, bf16[2048,1152]{1,0:T(8,128)(2,1)} %project.1.query_ref.key_ref.value_ref, bf16[2048,1152]{1,0:T(8,128)(2,1)} %project.1.query_ref.key_ref.value_ref, ...), custom_call_target="tpu_custom_call" | custom-call | flops 64424509440 | bytes 17301504 | tf_op jit(solution)/shard_map/attend_back/pallas_call | solution.py:458
  388.4 15.3 %finish.1 = (bf16[2048,768]{1,0:T(8,128)(2,1)}, bf16[32,32,1152]{2,1,0:T(8,128)(2,1)}) custom-call(s32[1]{0:T(128)} %bitcast.22.core_ref, bf16[2048,384]{1,0:T(8,128)(2,1)} %get-tuple-element.51.query_grad_ref, bf16[2048,384]{1,0:T(8,128)(2,1)} %get-tuple-element.52.key_grad_ref, bf16[2048,384]{1,0:T(8,128)(2,1)} %get-tuple-element.53.value_grad_ref, ...), custom_call_target="tpu_custom_call" | custom-call | flops 7247757312 | bytes 15728640 | tf_op jit(solution)/shard_map/finish/pallas_call | solution.py:863
  408.2 11.9 %collective-permute-done.20 = bf16[1,2,4,32,1152]{4,3,2,1,0:T(8,128)(2,1)S(1)} collective-permute-done((bf16[1,2,4,32,1152]{4,3,2,1,0:T(8,128)(2,1)S(1)}, bf16[1,2,4,32,1152]{4,3,2,1,0:T(8,128)(2,1)S(1)}, u32[]{:S(2)}, u32[]{:S(2)}) %collective-permute-start.20) | collective-permute-done | bytes 589856 | tf_op jit(solution)/shard_map/ppermute | solution.py:960
  423.0 10.8 %collective-permute-done.21 = bf16[1,1,4,32,1152]{4,3,2,1,0:T(8,128)(2,1)S(1)} collective-permute-done((bf16[1,1,4,32,1152]{4,3,2,1,0:T(8,128)(2,1)S(1)}, bf16[1,1,4,32,1152]{4,3,2,1,0:T(8,128)(2,1)S(1)}, u32[]{:S(2)}, u32[]{:S(2)}) %collective-permute-start.21) | collective-permute-done | bytes 294944 | tf_op jit(solution)/shard_map/ppermute | solution.py:960
  446.8 8.2 %collective-permute-done.26 = bf16[2,32,1152]{2,1,0:T(8,128)(2,1)} collective-permute-done((bf16[2,32,1152]{2,1,0:T(8,128)(2,1)}, bf16[2,32,1152]{2,1,0:T(8,128)(2,1)}, u32[]{:S(2)}, u32[]{:S(2)}) %collective-permute-start.26) | collective-permute-done | bytes 147488 | tf_op jit(solution)/shard_map/ppermute | solution.py:1032
  455.0 3.5 collective-permute-done.25
  466.0 5.0 collective-permute-start.16
  471.5 4.2 collective-permute-start.19
  478.1 10.4 %collective-permute-done.16 = bf16[256,768]{1,0:T(8,128)(2,1)S(1)} collective-permute-done((bf16[256,768]{1,0:T(8,128)(2,1)S(1)}, bf16[256,768]{1,0:T(8,128)(2,1)S(1)}, u32[]{:S(2)}, u32[]{:S(2)}) %collective-permute-start.16) | collective-permute-done | bytes 393248 | tf_op jit(solution)/shard_map/ppermute | solution.py:941
  488.6 4.8 collective-permute-done.17
  493.3 7.4 %collective-permute-done.18 = bf16[256,768]{1,0:T(8,128)(2,1)S(1)} collective-permute-done((bf16[256,768]{1,0:T(8,128)(2,1)S(1)}, bf16[256,768]{1,0:T(8,128)(2,1)S(1)}, u32[]{:S(2)}, u32[]{:S(2)}) %collective-permute-start.18) | collective-permute-done | bytes 393248 | tf_op jit(solution)/shard_map/ppermute | solution.py:941
  500.7 8.4 %collective-permute-done.19 = bf16[256,768]{1,0:T(8,128)(2,1)S(1)} collective-permute-done((bf16[256,768]{1,0:T(8,128)(2,1)S(1)}, bf16[256,768]{1,0:T(8,128)(2,1)S(1)}, u32[]{:S(2)}, u32[]{:S(2)}) %collective-permute-start.19) | collective-permute-done | bytes 393248 | tf_op jit(solution)/shard_map/ppermute | solution.py:941
  (146 shorter events, 81.2 us)
Async XLA Ops:
  7.2 85.4 %all-gather.5.cloned.1.call-start = ((), (), s32[]{:S(2)}) async-start(), calls=%async_computation.2 | async-start | bytes 4866048 | tf_op jit(solution)/shard_map/all_gather | solution.py:974
  17.1 193.1 %all-gather.7.cloned.1.call-start = ((), (), s32[]{:S(2)}) async-start(), calls=%async_computation.3 | async-start | bytes 10948608 | tf_op jit(solution)/shard_map/all_gather | solution.py:975
  17.9 493.4 %reduce-scatter.2.cloned.1.call-start = ((), (), s32[]{:S(2)}) async-start(), calls=%async_computation.1 | async-start | bytes 12165120 | tf_op jit(solution)/shard_map/reduce_scatter | solution.py:1011
  19.4 14.2 %collective-permute-start = (bf16[256,768]{1,0:T(8,128)(2,1)S(1)}, bf16[256,768]{1,0:T(8,128)(2,1)S(1)}, u32[]{:S(2)}, u32[]{:S(2)}) collective-permute-start(bf16[256,768]{1,0:T(8,128)(2,1)S(1)} %get-tuple-element.86), channel_id=1, source_target_pairs={{0,0},{1,4},{2,1},{3,5},{4,2},{5,6},{6,3},{7,7},{8,8},{9,12},{10,9... | collective-permute-start | bytes 1179656 | tf_op jit(solution)/shard_map/ppermute | solution.py:932
  22.6 22.9 %collective-permute-start.1 = (bf16[256,768]{1,0:T(8,128)(2,1)S(1)}, bf16[256,768]{1,0:T(8,128)(2,1)S(1)}, u32[]{:S(2)}, u32[]{:S(2)}) collective-permute-start(bf16[256,768]{1,0:T(8,128)(2,1)S(1)} %get-tuple-element.85), channel_id=1, source_target_pairs={{0,4},{1,0},{2,5},{3,1},{4,6},{5,2},{6,7},{7,3},{8,12},{9,8},{10,1... | collective-permute-start | bytes 1179656 | tf_op jit(solution)/shard_map/ppermute | solution.py:932
  23.7 37.9 %collective-permute-start.2 = (bf16[256,768]{1,0:T(8,128)(2,1)S(1)}, bf16[256,768]{1,0:T(8,128)(2,1)S(1)}, u32[]{:S(2)}, u32[]{:S(2)}) collective-permute-start(bf16[256,768]{1,0:T(8,128)(2,1)S(1)} %get-tuple-element.84), channel_id=1, source_target_pairs={{0,1},{1,5},{2,0},{3,4},{4,3},{5,7},{6,2},{7,6},{8,9},{9,13},{10,8... | collective-permute-start | bytes 1179656 | tf_op jit(solution)/shard_map/ppermute | solution.py:932
  24.4 41.9 %collective-permute-start.3 = (bf16[256,768]{1,0:T(8,128)(2,1)S(1)}, bf16[256,768]{1,0:T(8,128)(2,1)S(1)}, u32[]{:S(2)}, u32[]{:S(2)}) collective-permute-start(bf16[256,768]{1,0:T(8,128)(2,1)S(1)} %get-tuple-element.83), channel_id=1, source_target_pairs={{0,5},{1,1},{2,4},{3,0},{4,7},{5,3},{6,6},{7,2},{8,13},{9,9},{10,1... | collective-permute-start | bytes 1179656 | tf_op jit(solution)/shard_map/ppermute | solution.py:932
  67.6 3.8 collective-permute-start.4
  143.4 2.4 collective-permute-start.5
  146.0 30.8 %collective-permute-start.6 = (bf16[256,768]{1,0:T(8,128)(2,1)S(1)}, bf16[256,768]{1,0:T(8,128)(2,1)S(1)}, u32[]{:S(2)}, u32[]{:S(2)}) collective-permute-start(bf16[256,768]{1,0:T(8,128)(2,1)S(1)} %get-tuple-element.80), channel_id=1, source_target_pairs={{5,0},{1,1},{4,2},{0,3},{7,4},{3,5},{6,6},{2,7},{13,8},{9,9},{12,1... | collective-permute-start | bytes 1179656 | tf_op jit(solution)/shard_map/ppermute | solution.py:941
  148.0 36.6 %collective-permute-start.7 = (bf16[256,768]{1,0:T(8,128)(2,1)S(1)}, bf16[256,768]{1,0:T(8,128)(2,1)S(1)}, u32[]{:S(2)}, u32[]{:S(2)}) collective-permute-start(bf16[256,768]{1,0:T(8,128)(2,1)S(1)} %get-tuple-element.81), channel_id=1, source_target_pairs={{1,0},{5,1},{0,2},{4,3},{3,4},{7,5},{2,6},{6,7},{9,8},{13,9},{8,10... | collective-permute-start | bytes 1179656 | tf_op jit(solution)/shard_map/ppermute | solution.py:941
  148.0 47.6 %collective-permute-start.8 = (bf16[256,768]{1,0:T(8,128)(2,1)S(1)}, bf16[256,768]{1,0:T(8,128)(2,1)S(1)}, u32[]{:S(2)}, u32[]{:S(2)}) collective-permute-start(bf16[256,768]{1,0:T(8,128)(2,1)S(1)} %get-tuple-element.79), channel_id=1, source_target_pairs={{4,0},{0,1},{5,2},{1,3},{6,4},{2,5},{7,6},{3,7},{12,8},{8,9},{13,1... | collective-permute-start | bytes 1179656 | tf_op jit(solution)/shard_map/ppermute | solution.py:941
  149.2 59.6 %collective-permute-start.9 = (bf16[256,768]{1,0:T(8,128)(2,1)S(1)}, bf16[256,768]{1,0:T(8,128)(2,1)S(1)}, u32[]{:S(2)}, u32[]{:S(2)}) collective-permute-start(bf16[256,768]{1,0:T(8,128)(2,1)S(1)} %get-tuple-element.82), channel_id=1, source_target_pairs={{0,0},{4,1},{1,2},{5,3},{2,4},{6,5},{3,6},{7,7},{8,8},{12,9},{9,10... | collective-permute-start | bytes 1179656 | tf_op jit(solution)/shard_map/ppermute | solution.py:941
  255.7 14.2 %collective-permute-start.10 = (bf16[256,768]{1,0:T(8,128)(2,1)S(1)}, bf16[256,768]{1,0:T(8,128)(2,1)S(1)}, u32[]{:S(2)}, u32[]{:S(2)}) collective-permute-start(bf16[256,768]{1,0:T(8,128)(2,1)S(1)} %get-tuple-element.74), channel_id=1, source_target_pairs={{0,0},{1,4},{2,1},{3,5},{4,2},{5,6},{6,3},{7,7},{8,8},{9,12},{10,9... | collective-permute-start | bytes 1179656 | tf_op jit(solution)/shard_map/ppermute | solution.py:932
  257.7 17.1 %collective-permute-start.11 = (bf16[256,768]{1,0:T(8,128)(2,1)S(1)}, bf16[256,768]{1,0:T(8,128)(2,1)S(1)}, u32[]{:S(2)}, u32[]{:S(2)}) collective-permute-start(bf16[256,768]{1,0:T(8,128)(2,1)S(1)} %get-tuple-element.73), channel_id=1, source_target_pairs={{0,4},{1,0},{2,5},{3,1},{4,6},{5,2},{6,7},{7,3},{8,12},{9,8},{10,1... | collective-permute-start | bytes 1179656 | tf_op jit(solution)/shard_map/ppermute | solution.py:932
  258.4 29.3 %collective-permute-start.12 = (bf16[256,768]{1,0:T(8,128)(2,1)S(1)}, bf16[256,768]{1,0:T(8,128)(2,1)S(1)}, u32[]{:S(2)}, u32[]{:S(2)}) collective-permute-start(bf16[256,768]{1,0:T(8,128)(2,1)S(1)} %get-tuple-element.72), channel_id=1, source_target_pairs={{0,1},{1,5},{2,0},{3,4},{4,3},{5,7},{6,2},{7,6},{8,9},{9,13},{10,8... | collective-permute-start | bytes 1179656 | tf_op jit(solution)/shard_map/ppermute | solution.py:932
  260.5 31.4 %collective-permute-start.13 = (bf16[256,768]{1,0:T(8,128)(2,1)S(1)}, bf16[256,768]{1,0:T(8,128)(2,1)S(1)}, u32[]{:S(2)}, u32[]{:S(2)}) collective-permute-start(bf16[256,768]{1,0:T(8,128)(2,1)S(1)} %get-tuple-element.71), channel_id=1, source_target_pairs={{0,5},{1,1},{2,4},{3,0},{4,7},{5,3},{6,6},{7,2},{8,13},{9,9},{10,1... | collective-permute-start | bytes 1179656 | tf_op jit(solution)/shard_map/ppermute | solution.py:932
  292.1 20.2 %collective-permute-start.14 = (bf16[1024,384]{1,0:T(8,128)(2,1)S(1)}, bf16[1024,384]{1,0:T(8,128)(2,1)S(1)}, u32[]{:S(2)}, u32[]{:S(2)}) collective-permute-start(bf16[1024,384]{1,0:T(8,128)(2,1)S(1)} %get-tuple-element.70), channel_id=1, source_target_pairs={{0,4},{4,0},{1,5},{5,1},{2,6},{6,2},{3,7},{7,3},{8,12},{12,8},{9,1... | collective-permute-start | bytes 2359304 | tf_op jit(solution)/shard_map/ppermute | solution.py:950
  405.7 14.5 %collective-permute-start.20 = (bf16[1,2,4,32,1152]{4,3,2,1,0:T(8,128)(2,1)S(1)}, bf16[1,2,4,32,1152]{4,3,2,1,0:T(8,128)(2,1)S(1)}, u32[]{:S(2)}, u32[]{:S(2)}) collective-permute-start(bf16[1,2,4,32,1152]{4,3,2,1,0:T(8,128)(2,1)S(1)} %dynamic-slice_bitcast_fusion.1), channel_id=1, source_target_pairs={{0,16},{8,24},{16,0},{24,8},{1,17},{9,25},{17,1},{25,9},{2,18},{10... | collective-permute-start | bytes 1769480 | tf_op jit(solution)/shard_map/ppermute | solution.py:960
  407.0 14.6 %collective-permute-start.22 = (bf16[2,1,4,32,1152]{4,3,2,1,0:T(8,128)(2,1)S(1)}, bf16[2,1,4,32,1152]{4,3,2,1,0:T(8,128)(2,1)S(1)}, u32[]{:S(2)}, u32[]{:S(2)}) collective-permute-start(bf16[2,1,4,32,1152]{4,3,2,1,0:T(8,128)(2,1)S(1)} %dynamic-slice_bitcast_fusion), channel_id=1, source_target_pairs={{0,8},{8,0},{16,24},{24,16},{1,9},{9,1},{17,25},{25,17},{2,10},{10... | collective-permute-start | bytes 1769480 | tf_op jit(solution)/shard_map/ppermute | solution.py:960
  420.3 13.5 %collective-permute-start.21 = (bf16[1,1,4,32,1152]{4,3,2,1,0:T(8,128)(2,1)S(1)}, bf16[1,1,4,32,1152]{4,3,2,1,0:T(8,128)(2,1)S(1)}, u32[]{:S(2)}, u32[]{:S(2)}) collective-permute-start(bf16[1,1,4,32,1152]{4,3,2,1,0:T(8,128)(2,1)S(1)} %constant_dynamic-slice_fusion.6), channel_id=1, source_target_pairs={{0,8},{8,0},{16,24},{24,16},{1,9},{9,1},{17,25},{25,17},{2,10},{10... | collective-permute-start | bytes 884744 | tf_op jit(solution)/shard_map/ppermute | solution.py:960
  421.8 14.7 %collective-permute-start.23 = (bf16[1,1,4,32,1152]{4,3,2,1,0:T(8,128)(2,1)S(1)}, bf16[1,1,4,32,1152]{4,3,2,1,0:T(8,128)(2,1)S(1)}, u32[]{:S(2)}, u32[]{:S(2)}) collective-permute-start(bf16[1,1,4,32,1152]{4,3,2,1,0:T(8,128)(2,1)S(1)} %constant_dynamic-slice_fusion.5), channel_id=1, source_target_pairs={{0,16},{8,24},{16,0},{24,8},{1,17},{9,25},{17,1},{25,9},{2,18},{10... | collective-permute-start | bytes 884744 | tf_op jit(solution)/shard_map/ppermute | solution.py:960
  438.0 17.0 %collective-permute-start.26 = (bf16[2,32,1152]{2,1,0:T(8,128)(2,1)}, bf16[2,32,1152]{2,1,0:T(8,128)(2,1)}, u32[]{:S(2)}, u32[]{:S(2)}) collective-permute-start(bf16[2,32,1152]{2,1,0:T(8,128)(2,1)} %get-tuple-element.94), channel_id=1, source_target_pairs={{0,3},{1,2},{2,1},{3,0},{4,7},{5,6},{6,5},{7,4},{8,11},{9,10},{10,... | collective-permute-start | bytes 442376 | tf_op jit(solution)/shard_map/ppermute | solution.py:1032
  440.2 18.3 %collective-permute-start.25 = (bf16[2,32,1152]{2,1,0:T(8,128)(2,1)}, bf16[2,32,1152]{2,1,0:T(8,128)(2,1)}, u32[]{:S(2)}, u32[]{:S(2)}) collective-permute-start(bf16[2,32,1152]{2,1,0:T(8,128)(2,1)} %get-tuple-element.93), channel_id=1, source_target_pairs={{0,2},{1,3},{2,0},{3,1},{4,6},{5,7},{6,4},{7,5},{8,10},{9,11},{10,... | collective-permute-start | bytes 442376 | tf_op jit(solution)/shard_map/ppermute | solution.py:1032
  441.8 16.7 %collective-permute-start.24 = (bf16[2,32,1152]{2,1,0:T(8,128)(2,1)}, bf16[2,32,1152]{2,1,0:T(8,128)(2,1)}, u32[]{:S(2)}, u32[]{:S(2)}) collective-permute-start(bf16[2,32,1152]{2,1,0:T(8,128)(2,1)} %get-tuple-element.92), channel_id=1, source_target_pairs={{0,1},{1,0},{2,3},{3,2},{4,5},{5,4},{6,7},{7,6},{8,9},{9,8},{10,11... | collective-permute-start | bytes 442376 | tf_op jit(solution)/shard_map/ppermute | solution.py:1032
  444.2 19.6 %collective-permute-start.15 = (bf16[1024,768]{1,0:T(8,128)(2,1)}, bf16[1024,768]{1,0:T(8,128)(2,1)}, u32[]{:S(2)}, u32[]{:S(2)}) collective-permute-start(bf16[1024,768]{1,0:T(8,128)(2,1)} %slice.157), channel_id=1, source_target_pairs={{0,4},{4,0},{1,5},{5,1},{2,6},{6,2},{3,7},{7,3},{8,12},{12,8},{9,1... | collective-permute-start | bytes 4718600 | tf_op jit(solution)/shard_map/ppermute | solution.py:950
  460.4 1.9 collective-permute-start.27
  466.0 22.6 %collective-permute-start.16 = (bf16[256,768]{1,0:T(8,128)(2,1)S(1)}, bf16[256,768]{1,0:T(8,128)(2,1)S(1)}, u32[]{:S(2)}, u32[]{:S(2)}) collective-permute-start(bf16[256,768]{1,0:T(8,128)(2,1)S(1)} %get-tuple-element.68), channel_id=1, source_target_pairs={{5,0},{1,1},{4,2},{0,3},{7,4},{3,5},{6,6},{2,7},{13,8},{9,9},{12,1... | collective-permute-start | bytes 1179656 | tf_op jit(solution)/shard_map/ppermute | solution.py:941
  470.9 22.4 %collective-permute-start.17 = (bf16[256,768]{1,0:T(8,128)(2,1)S(1)}, bf16[256,768]{1,0:T(8,128)(2,1)S(1)}, u32[]{:S(2)}, u32[]{:S(2)}) collective-permute-start(bf16[256,768]{1,0:T(8,128)(2,1)S(1)} %get-tuple-element.67), channel_id=1, source_target_pairs={{1,0},{5,1},{0,2},{4,3},{3,4},{7,5},{2,6},{6,7},{9,8},{13,9},{8,10... | collective-permute-start | bytes 1179656 | tf_op jit(solution)/shard_map/ppermute | solution.py:941
  471.0 29.7 %collective-permute-start.18 = (bf16[256,768]{1,0:T(8,128)(2,1)S(1)}, bf16[256,768]{1,0:T(8,128)(2,1)S(1)}, u32[]{:S(2)}, u32[]{:S(2)}) collective-permute-start(bf16[256,768]{1,0:T(8,128)(2,1)S(1)} %get-tuple-element.65), channel_id=1, source_target_pairs={{4,0},{0,1},{5,2},{1,3},{6,4},{2,5},{7,6},{3,7},{12,8},{8,9},{13,1... | collective-permute-start | bytes 1179656 | tf_op jit(solution)/shard_map/ppermute | solution.py:941
  471.5 37.7 %collective-permute-start.19 = (bf16[256,768]{1,0:T(8,128)(2,1)S(1)}, bf16[256,768]{1,0:T(8,128)(2,1)S(1)}, u32[]{:S(2)}, u32[]{:S(2)}) collective-permute-start(bf16[256,768]{1,0:T(8,128)(2,1)S(1)} %get-tuple-element.66), channel_id=1, source_target_pairs={{0,0},{4,1},{1,2},{5,3},{2,4},{6,5},{3,6},{7,7},{8,8},{12,9},{9,10... | collective-permute-start | bytes 1179656 | tf_op jit(solution)/shard_map/ppermute | solution.py:941
  478.1 31.1 %copy-start.8 = (f32[1024,768]{1,0:T(8,128)S(1)}, f32[1024,768]{1,0:T(8,128)}, u32[]{:S(2)}) copy-start(f32[1024,768]{1,0:T(8,128)} %get-tuple-element.41) | copy-start | bytes 9437188
  (17 other events, 101.2 us)
Sparse Core Ops, SparseCore 0:
  17.2 75.2 all-gather.4
  95.3 106.5 all-gather.6
  313.7 164.5 reduce-scatter.1

commit v3 on v2

--- a/solution.py
+++ b/solution.py
@@ -328,7 +328,9 @@
                 value_aug[one, at, LANES:] = jnp.where(minus, -1.0, 0.0).astype(jnp.bfloat16)
 
 
-def attend_kernel(span, info_ref, query_ref, key_ref, value_ref, out_ref, aux_ref, key_aug, value_aug):
+def attend_kernel(
+    span, info_ref, query_ref, key_ref, value_ref, low_ref, out_ref, aux_ref, key_aug, value_aug
+):
     length = key_ref.shape[0]
     tile = query_ref.shape[0]
     lane = lax.broadcasted_iota(jnp.int32, (1, LANES), 1)
@@ -366,58 +368,70 @@
         out = part if out is None else out + part
         log_total = jnp.log2(weight) * (1.0 / SCORE_SCALE) + peaks[one]
         aux = spread_three(lane, 4 * one, log_total, aux)
+    low_ref[...] = out.astype(jnp.bfloat16)
     out_ref[...] = out
     aux_ref[...] = aux.astype(jnp.bfloat16)
 
 
-def attend(qkv, info, tile, span):
+def attend(qkv, info, part, parts, tile, span):
     length, width = qkv.shape[0], qkv.shape[1] // 3
-    tiles = width // LANES
+    tiles, rows = width // LANES, length // parts
+    first = part * (rows // tile)
     query_spec = pl.BlockSpec((tile, LANES), lambda pair, at: (at, pair))
     return pl.pallas_call(
         functools.partial(attend_kernel, span),
-        grid=(tiles, length // tile),
+        grid=(tiles, rows // tile),
         in_specs=[
             pl.BlockSpec(memory_space=pltpu.SMEM),
-            query_spec,
+            pl.BlockSpec((tile, LANES), lambda pair, at: (first + at, pair)),
             pl.BlockSpec((length, LANES), lambda pair, at: (0, tiles + pair)),
             pl.BlockSpec((length, LANES), lambda pair, at: (0, 2 * tiles + pair)),
         ],
-        out_specs=[query_spec, query_spec],
+        out_specs=[query_spec] * 3,
         out_shape=[
-            jax.ShapeDtypeStruct((length, width), jnp.float32),
-            jax.ShapeDtypeStruct((length, width), jnp.bfloat16),
+            jax.ShapeDtypeStruct((rows, width), jnp.bfloat16),
+            jax.ShapeDtypeStruct((rows, width), jnp.float32),
+            jax.ShapeDtypeStruct((rows, width), jnp.bfloat16),
         ],
         scratch_shapes=[pltpu.VMEM((PER_TILE, length, 2 * LANES), jnp.bfloat16)] * 2,
         compiler_params=pltpu.CompilerParams(vmem_limit_bytes=VMEM_LIMIT),
         cost_estimate=pl.CostEstimate(
-            flops=16 * length * length * width,
+            flops=16 * rows * length * width,
             bytes_accessed=12 * length * width,
-            transcendentals=length * length * width // 64,
+            transcendentals=rows * length * width // 64,
         ),
         name="attend",
     )(info, qkv, qkv, qkv)
 
 
-def attend_back_kernel(
-    span, info_ref, query_ref, key_ref, value_ref, grad_ref, out_ref, aux_ref,
-    query_grad_ref, key_grad_ref, value_grad_ref, key_aug, value_aug, key_cols, key_sum, value_sum,
-):
+def attend_back_kernel(span, per_part, info_ref, query_ref, key_ref, value_ref, *refs):
+    parts = (len(refs) - 8) // 3
+    groups = [refs[at * parts : (at + 1) * parts] for at in range(3)]
+    query_grad_ref, key_grad_ref, value_grad_ref, key_aug, value_aug, key_cols, key_sum, value_sum = (
+        refs[3 * parts :]
+    )
     length = key_ref.shape[0]
     tile = query_ref.shape[0]
     wide = LANES // PER_TILE
     lane = lax.broadcasted_iota(jnp.int32, (1, LANES), 1)
-
-    @pl.when(pl.program_id(1) == 0)
+    step = pl.program_id(1)
+
+    @pl.when(step == 0)
     def _():
         fill_keys(info_ref, key_ref, value_ref, key_aug, value_aug, False, length // 8)
         key_cols[...] = key_ref[...].T
         key_sum[...] = jnp.zeros_like(key_sum)
         value_sum[...] = jnp.zeros_like(value_sum)
 
-    plain, grad = query_ref[...], grad_ref[...]
-    query = jnp.concatenate([plain, aux_ref[...]], axis=1)
-    product = grad.astype(jnp.float32) * out_ref[...]
+    grad, out, aux = (group[0][...] for group in groups)
+    for part in range(1, parts):
+        here = step >= part * per_part
+        grad, out, aux = (
+            jnp.where(here, group[part][...], item) for group, item in zip(groups, (grad, out, aux))
+        )
+    plain = query_ref[...]
+    query = jnp.concatenate([plain, aux], axis=1)
+    product = grad.astype(jnp.float32) * out
     delta = jnp.zeros((tile, LANES), jnp.float32)
     for one in range(PER_TILE):
         own = jnp.sum(jnp.where(lane // wide == one, product, 0.0), axis=1, keepdims=True)
@@ -443,74 +457,127 @@
         query_rows.append(total)
     query_grad_ref[...] = (jnp.concatenate(query_rows, axis=0).T * 0.125).astype(jnp.bfloat16)
 
-    @pl.when(pl.program_id(1) == pl.num_programs(1) - 1)
+    @pl.when(step == pl.num_programs(1) - 1)
     def _():
         key_grad_ref[...] = (key_sum[...] * 0.125).astype(jnp.bfloat16)
         value_grad_ref[...] = value_sum[...].astype(jnp.bfloat16)
 
 
-def attend_back(qkv, grad, out, aux, info, tile, span):
+def attend_back(qkv, grads, outs, auxes, info, first, count, tile, span):
     length, width = qkv.shape[0], qkv.shape[1] // 3
-    tiles = width // LANES
-    query_spec = pl.BlockSpec((tile, LANES), lambda pair, at: (at, pair))
+    tiles, parts = width // LANES, len(grads)
+    per_part = length // parts // tile
+
+    def part_spec(part):
+        low = part * per_part
+        return pl.BlockSpec(
+            (tile, LANES), lambda pair, at: (jnp.clip(at - low, 0, per_part - 1), first + pair)
+        )
+
+    result = jax.ShapeDtypeStruct((length, count * LANES), jnp.bfloat16)
     whole = pl.BlockSpec((length, LANES), lambda pair, at: (0, pair))
-    result = jax.ShapeDtypeStruct((length, width), jnp.bfloat16)
     return pl.pallas_call(
-        functools.partial(attend_back_kernel, span),
-        grid=(tiles, length // tile),
+        functools.partial(attend_back_kernel, span, per_part),
+        grid=(count, length // tile),
         in_specs=[
             pl.BlockSpec(memory_space=pltpu.SMEM),
-            query_spec,
-            pl.BlockSpec((length, LANES), lambda pair, at: (0, tiles + pair)),
-            pl.BlockSpec((length, LANES), lambda pair, at: (0, 2 * tiles + pair)),
-            query_spec,
-            query_spec,
-            query_spec,
-        ],
-        out_specs=[query_spec, whole, whole],
+            pl.BlockSpec((tile, LANES), lambda pair, at: (at, first + pair)),
+            pl.BlockSpec((length, LANES), lambda pair, at: (0, tiles + first + pair)),
+            pl.BlockSpec((length, LANES), lambda pair, at: (0, 2 * tiles + first + pair)),
+        ]
+        + [part_spec(part) for part in range(parts)] * 3,
+        out_specs=[pl.BlockSpec((tile, LANES), lambda pair, at: (at, pair)), whole, whole],
         out_shape=[result] * 3,
         scratch_shapes=[pltpu.VMEM((PER_TILE, length, 2 * LANES), jnp.bfloat16)] * 2
         + [pltpu.VMEM((LANES, length), jnp.bfloat16)]
         + [pltpu.VMEM((length, LANES), jnp.float32)] * 2,
         compiler_params=pltpu.CompilerParams(vmem_limit_bytes=VMEM_LIMIT),
         cost_estimate=pl.CostEstimate(
-            flops=40 * length * length * width,
+            flops=40 * count * LANES * length * length,
             bytes_accessed=22 * length * width,
-            transcendentals=length * length * width // 64,
+            transcendentals=count * length * length * 2,
         ),
         name="attend_back",
-    )(info, qkv, qkv, qkv, grad, out, aux)
-
-
-def pack_kernel(query_ref, key_ref, value_ref, output_ref, up_ref, down_ref, small_ref, first_ref, second_ref):
-    share, width = query_ref.shape
-    fold = up_ref.shape[1] // width
-    first_ref[0] = query_ref[...]
-    first_ref[1] = key_ref[...]
-    first_ref[2] = value_ref[...]
-    first_ref[3, :, :LANES] = small_ref[...]
-    first_ref[3, :, LANES:] = jnp.zeros((share, width - LANES), first_ref.dtype)
-    second_ref[0] = output_ref[...]
+    )(info, qkv, qkv, qkv, *grads, *outs, *auxes)
+
+
+def pack_kernel(count, core_ref, *refs):
+    query, key, value, output, up, down = refs[:6]
+    vectors = refs[6 : 6 + count]
+    mine_ref, theirs_ref, second_ref, held_ref, wide_ref = refs[6 + count : 11 + count]
+    lines = refs[11 + count : 11 + 2 * count]
+    sems, line_sems = refs[11 + 2 * count :]
+    share, width = query.shape
+    cols = width // 2
+    fold = up.shape[1] // width
+    copies = [
+        pltpu.make_async_copy(item, held_ref.at[at], sems.at[at])
+        for at, item in enumerate((query, key, value))
+    ]
+    copies += [
+        pltpu.make_async_copy(item, line, line_sems.at[at])
+        for at, (item, line) in enumerate(zip(vectors, lines))
+    ]
+    later = [pltpu.make_async_copy(output, second_ref.at[0], sems.at[3])]
     for at in range(fold):
-        second_ref[1 + at] = up_ref[:, at * width : (at + 1) * width]
-        second_ref[1 + fold + at] = down_ref[at * share : (at + 1) * share, :]
-
-
-def pack(matrices, small):
+        later.append(
+            pltpu.make_async_copy(
+                down.at[pl.ds(at * share, share)],
+                second_ref.at[1 + fold + at],
+                sems.at[4 + at],
+            )
+        )
+    later.append(pltpu.make_async_copy(up, wide_ref, sems.at[4 + fold]))
+    for copy in copies + later:
+        copy.start()
+    for copy in copies:
+        copy.wait()
+    first_core = core_ref[0] == 0
+    for at in range(3):
+        left, right = held_ref[at, :, :cols], held_ref[at, :, cols:]
+        here = slice(at * share, (at + 1) * share)
+        mine_ref[here] = jnp.where(first_core, left, right)
+        theirs_ref[here] = jnp.where(first_core, right, left)
+    for ref in (mine_ref, theirs_ref):
+        ref[3 * share :] = jnp.zeros((8, cols), ref.dtype)
+        for at, line in enumerate(lines):
+            low = at // 8 * LANES
+            ref[3 * share + at % 8, low : low + line.shape[0]] = line[...]
+    for copy in later:
+        copy.wait()
+    for at in range(fold):
+        second_ref[1 + at] = wide_ref[:, at * width : (at + 1) * width]
+
+
+def pack(core, matrices, vectors):
     share, width = matrices[0].shape
+    cols = width // 2
     fold = matrices[4].shape[1] // width
+    count = len(vectors)
+    block = jax.ShapeDtypeStruct((3 * share + 8, cols), jnp.bfloat16)
+    inside = pl.BlockSpec(memory_space=pltpu.VMEM)
     return pl.pallas_call(
-        pack_kernel,
+        functools.partial(pack_kernel, count),
+        in_specs=[pl.BlockSpec(memory_space=pltpu.SMEM)]
+        + [pl.BlockSpec(memory_space=pl.ANY)] * (6 + count),
+        out_specs=[inside] * 3,
         out_shape=[
-            jax.ShapeDtypeStruct((4, share, width), jnp.bfloat16),
+            block,
+            block,
             jax.ShapeDtypeStruct((1 + 2 * fold, share, width), jnp.bfloat16),
         ],
-        compiler_params=pltpu.CompilerParams(vmem_limit_bytes=8 << 20),
+        scratch_shapes=[pltpu.VMEM((3, share, width), jnp.bfloat16)]
+        + [pltpu.VMEM(matrices[4].shape, jnp.bfloat16)]
+        + [pltpu.VMEM(item.shape, item.dtype) for item in vectors]
+        + [pltpu.SemaphoreType.DMA((5 + fold,)), pltpu.SemaphoreType.DMA((count,))],
+        compiler_params=pltpu.CompilerParams(vmem_limit_bytes=VMEM_LIMIT),
         name="pack",
-    )(*matrices, small)
-
-
-def unspread(pieces, width, share):
+    )(core, *matrices, *vectors)
+
+
+def unspread(gathered_ref, first_row, entry, width, share):
+    low = entry // 8 * LANES
+    pieces = gathered_ref[:, first_row + entry % 8, low : low + LANES]
     lane = lax.broadcasted_iota(jnp.int32, (LANES, width), 1)
     row = lax.broadcasted_iota(jnp.int32, (LANES, width), 0)
     pick = jnp.where(lax.rem(lane, share) == row, 1.0, 0.0).astype(jnp.bfloat16)
@@ -520,43 +587,42 @@
     return jnp.sum(jnp.where(lax.div(lane, share) == row, spread, 0.0), axis=0, keepdims=True)
 
 
-def project_kernel(core_ref, tokens_ref, query_ref, key_ref, value_ref, small_ref, out_ref, bias_ref):
-    devices, _, share, cols = query_ref.shape
-    width = devices * share
+def own_weight(gathered_ref, at, share):
+    devices, _, cols = gathered_ref.shape
+    return gathered_ref[:, at * share : (at + 1) * share, :].reshape(devices * share, cols)
+
+
+def project_kernel(share, core_ref, tokens_ref, gathered_ref, out_ref, bias_ref):
+    devices, _, cols = gathered_ref.shape
 
     @pl.when(pl.program_id(0) == 0)
     def _():
-        for at, entry in ((0, 7), (1, 8)):
-            whole = unspread(small_ref[:, 0, entry, :LANES], width, share)
+        for at in range(2):
+            whole = unspread(gathered_ref, 3 * share, at, devices * share, share)
             bias_ref[at : at + 1, :] = jnp.where(
                 core_ref[0] == 0, whole[:, :cols], whole[:, cols:]
             )
 
     tokens = tokens_ref[...]
-    for at, (ref, bias) in enumerate(((query_ref, 0), (key_ref, None), (value_ref, 1))):
-        part = dot_f32(tokens, ref[...].reshape(width, cols), NN)
+    for at, bias in enumerate((0, None, 1)):
+        part = dot_f32(tokens, own_weight(gathered_ref, at, share), NN)
         if bias is not None:
             part = part + bias_ref[bias : bias + 1, :]
         out_ref[:, at * cols : (at + 1) * cols] = part.astype(out_ref.dtype)
 
 
-def weight_columns(first, unit):
-    devices, _, share, width = first.shape
-    return pl.BlockSpec((devices, 1, share, width // 2), lambda at, core: (0, unit, 0, core[0]))
-
-
-def project(core, sequence, first, tile):
+def project(core, sequence, gathered, tile):
     length, width = sequence.shape
-    devices, _, share, _ = first.shape
-    cols = width // 2
+    devices, _, cols = gathered.shape
     return pl.pallas_call(
-        project_kernel,
+        functools.partial(project_kernel, width // devices),
         grid_spec=pltpu.PrefetchScalarGridSpec(
             num_scalar_prefetch=1,
             grid=(length // tile,),
-            in_specs=[pl.BlockSpec((tile, width), lambda at, core: (at, 0))]
-            + [weight_columns(first, unit) for unit in range(3)]
-            + [pl.BlockSpec((devices, 1, share, width), lambda at, core: (0, 3, 0, 0))],
+            in_specs=[
+                pl.BlockSpec((tile, width), lambda at, core: (at, 0)),
+                pl.BlockSpec(gathered.shape, lambda at, core: (0, 0, 0)),
+            ],
             out_specs=pl.BlockSpec((tile, 3 * cols), lambda at, core: (at, 0)),
             scratch_shapes=[pltpu.VMEM((8, cols), jnp.float32)],
         ),
@@ -566,7 +632,7 @@
             flops=6 * length * width * cols, bytes_accessed=10 * length * width, transcendentals=0
         ),
         name="project",
-    )(core, sequence, first, first, first, first)
+    )(core, sequence, gathered)
 
 
 def norm(values, gain, shift):
@@ -584,6 +650,12 @@
 
 
 def feed_kernel(
+    kept, index_ref, context_ref, tokens_ref, cotangent_ref, small_ref, weights_ref, *refs
+):
+    feed_rows(context_ref, tokens_ref, cotangent_ref, small_ref, weights_ref, *refs[kept:])
+
+
+def feed_rows(
     context_ref, tokens_ref, cotangent_ref, small_ref, weights_ref,
     out_ref, active_ref, grad_down_ref, grad_up_ref, hidden_ref, res_ref, attended_ref, context_grad_ref, sum_ref,
     weight_ref, vector_ref, slope_ref, sems,
@@ -610,9 +682,9 @@
             copy(unit).start()
         sum_ref[...] = jnp.zeros_like(sum_ref)
         for entry in range(7):
-            spread, wide = (fold * share, fold * width) if entry == 1 else (share, width)
-            vector_ref[entry : entry + 1, :wide] = unspread(
-                small_ref[:, 0, entry, :LANES], wide, spread
+            times = fold if entry == 1 else 1
+            vector_ref[entry : entry + 1, : times * width] = unspread(
+                small_ref, 0, 2 + entry, times * width, times * share
             )
 
     def ready(unit):
@@ -674,12 +746,14 @@
     context_grad_ref[...] = dot_f32(grad_attended, weight(0), NT).astype(bf16)
 
 
-def feed(context, tokens, cotangent, first, second, tile):
+def feed(index, context, tokens, cotangent, gathered, second, kept, tile):
     rows, width = context.shape
+    seqs = tokens.shape[0]
     devices, units, share, _ = second.shape
     fold = (units - 1) // 2
-    thin = pl.BlockSpec((tile, width), lambda at: (at, 0))
-    wide = pl.BlockSpec((tile, fold * width), lambda at: (at, 0))
+    thin = pl.BlockSpec((tile, width), lambda at, index: (at, 0))
+    placed = pl.BlockSpec((None, tile, width), lambda at, index: (index[0], at, 0))
+    wide = pl.BlockSpec((tile, fold * width), lambda at, index: (at, 0))
     sums = (6 + fold + 7) // 8 * 8
 
     def like(columns, dtype):
@@ -687,18 +761,29 @@
 
     bf16, f32 = jnp.bfloat16, jnp.float32
     return pl.pallas_call(
-        feed_kernel,
-        grid=(rows // tile,),
-        in_specs=[
-            thin,
-            thin,
-            thin,
-            pl.BlockSpec((devices, 1, share, width), lambda at: (0, 3, 0, 0)),
-            pl.BlockSpec(memory_space=pl.ANY),
-        ],
-        out_specs=[thin, wide, thin, wide, thin, thin, thin, thin, pl.BlockSpec((sums, width), lambda at: (0, 0))],
+        functools.partial(feed_kernel, len(kept)),
+        grid_spec=pltpu.PrefetchScalarGridSpec(
+            num_scalar_prefetch=1,
+            grid=(rows // tile,),
+            in_specs=[
+                thin,
+                placed,
+                placed,
+                pl.BlockSpec((devices, 8, width // 2), lambda at, index: (0, 3 * share // 8, 0)),
+                pl.BlockSpec(memory_space=pl.ANY),
+            ]
+            + [pl.BlockSpec(memory_space=pl.ANY)] * len(kept),
+            out_specs=[placed, wide, thin, wide, thin, thin, thin, thin]
+            + [pl.BlockSpec((sums, width), lambda at, index: (0, 0))],
+            scratch_shapes=[
+                pltpu.VMEM((units, devices, share, width), bf16),
+                pltpu.VMEM((8, fold * width), f32),
+                pltpu.VMEM((fold, tile, width), f32),
+                pltpu.SemaphoreType.DMA((units,)),
+            ],
+        ),
         out_shape=[
-            like(width, bf16),
+            jax.ShapeDtypeStruct((seqs, rows, width), bf16),
             like(fold * width, bf16),
             like(width, bf16),
             like(fold * width, bf16),
@@ -708,12 +793,7 @@
             like(width, bf16),
             jax.ShapeDtypeStruct((sums, width), f32),
         ],
-        scratch_shapes=[
-            pltpu.VMEM((units, devices, share, width), bf16),
-            pltpu.VMEM((8, fold * width), f32),
-            pltpu.VMEM((fold, tile, width), f32),
-            pltpu.SemaphoreType.DMA((units,)),
-        ],
+        input_output_aliases={6: 0} if kept else {},
         compiler_params=pltpu.CompilerParams(vmem_limit_bytes=VMEM_LIMIT),
         cost_estimate=pl.CostEstimate(
             flops=4 * rows * width * width * (1 + 2 * fold),
@@ -721,112 +801,121 @@
             transcendentals=rows * width * fold,
         ),
         name="feed",
-    )(context, tokens, cotangent, first, second)
+    )(index, context, tokens, cotangent, gathered, second, *kept)
 
 
 TN = ((0,), (0,))
 
 
-def weight_grad_kernel(
-    active_ref, grad_down_ref, hidden_ref, grad_up_ref, context_ref, attended_ref, sum_ref, out_ref, block_ref, small_ref, sems
-):
-    devices, units, share, width = out_ref.shape
-    fold = (units - 2) // 2
-    group = devices // fold
-    step = pl.program_id(0)
-
-    def block(slot):
-        return block_ref.at[slot]
-
-    def column_copy(unit, slot):
-        return pltpu.make_async_copy(block(slot), out_ref.at[:, unit], sems.at[slot])
-
-    def row_copy(at, slot):
-        return pltpu.make_async_copy(
-            block(slot).reshape(group, fold, share, width),
-            out_ref.at[pl.ds(group * at, group), pl.ds(1 + fold, fold)],
-            sems.at[slot],
-        )
-
-    def small_copy():
-        return pltpu.make_async_copy(small_ref, out_ref.at[:, 1 + 2 * fold], sems.at[2])
-
-    def store(left, right, slot):
-        block_ref[slot] = dot_f32(left, right, TN).astype(out_ref.dtype).reshape(devices, share, width)
-
-    slot = lax.rem(step, 2)
-
-    @pl.when(step >= 2)
+def up_grad_kernel(parts, core_ref, *refs):
+    groups = [refs[at * parts : (at + 1) * parts] for at in range(4)]
+    context, attended, hidden, grad_up = groups
+    keep_ref, send_ref = refs[4 * parts :]
+    n_pair, n_blk, _, share, width = keep_ref.shape
+
+    def store(left, right):
+        total = None
+        for one, other in zip(left, right):
+            part = dot_f32(one[...], other[...], TN)
+            total = part if total is None else total + part
+        total = total.astype(keep_ref.dtype).reshape(n_pair, 2, n_blk, 1, share, width)
+        low, high = total[:, 0], total[:, 1]
+        keep_ref[...] = jnp.where(core_ref[0] == 0, low, high)
+        send_ref[...] = jnp.where(core_ref[0] == 0, high, low)
+
+    @pl.when(pl.program_id(0) == 0)
     def _():
-        column_copy(0, slot).wait()
-
-    @pl.when(step == 0)
+        store(context, attended)
+
+    @pl.when(pl.program_id(0) > 0)
     def _():
-        rows = jnp.concatenate(
-            [sum_ref[...], jnp.zeros((share - sum_ref.shape[0], width), jnp.float32)], axis=0
-        ).astype(out_ref.dtype)
-        small_ref[...] = jnp.broadcast_to(rows[None], small_ref.shape)
-        small_copy().start()
-        store(context_ref[...], attended_ref[...], 0)
-        column_copy(0, 0).start()
-
-    @pl.when((step >= 1) & (step <= fold))
-    def _():
-        store(hidden_ref[...], grad_up_ref[...], slot)
-        column_copy(step, slot).start()
-
-    @pl.when(step > fold)
-    def _():
-        store(active_ref[...], grad_down_ref[...], slot)
-        row_copy(step - 1 - fold, slot).start()
-
-    @pl.when(step == 2 * fold)
-    def _():
-        small_copy().wait()
-        column_copy(0, 0).wait()
-        column_copy(0, 1).wait()
-
-
-def weight_grads(active, grad_down, hidden, grad_up, context, attended, sums, devices):
-    rows, width = context.shape
-    fold = active.shape[1] // width
-    share, units = width // devices, 2 + 2 * fold
-    whole = pl.BlockSpec((rows, width), lambda at: (0, 0))
+        store(hidden, grad_up)
+
+
+def up_grads(core, parts, sizes):
+    n_pair, n_blk = sizes
+    rows, width = parts[0][0].shape
+    fold = parts[0][3].shape[1] // width
+    share, units = width // (2 * n_pair * n_blk), 1 + fold
+    whole = pl.BlockSpec((rows, width), lambda at, core: (0, 0))
+    wide = pl.BlockSpec((rows, width), lambda at, core: (0, jnp.maximum(at - 1, 0)))
+    result = jax.ShapeDtypeStruct((n_pair, n_blk, units, share, width), jnp.bfloat16)
+    block = pl.BlockSpec((n_pair, n_blk, 1, share, width), lambda at, core: (0, 0, at, 0, 0))
     return pl.pallas_call(
-        weight_grad_kernel,
-        grid=(1 + 2 * fold,),
-        in_specs=[
-            pl.BlockSpec((rows, width), lambda at: (0, jnp.maximum(at - 1 - fold, 0))),
-            whole,
-            whole,
-            pl.BlockSpec((rows, width), lambda at: (0, jnp.clip(at - 1, 0, fold - 1))),
-            whole,
-            whole,
-            pl.BlockSpec(sums.shape, lambda at: (0, 0)),
-        ],
-        out_specs=pl.BlockSpec(memory_space=pl.ANY),
-        out_shape=jax.ShapeDtypeStruct((devices, units, share, width), jnp.bfloat16),
-        scratch_shapes=[
-            pltpu.VMEM((2, devices, share, width), jnp.bfloat16),
-            pltpu.VMEM((devices, share, width), jnp.bfloat16),
-            pltpu.SemaphoreType.DMA((3,)),
-        ],
+        functools.partial(up_grad_kernel, len(parts)),
+        grid_spec=pltpu.PrefetchScalarGridSpec(
+            num_scalar_prefetch=1,
+            grid=(units,),
+            in_specs=[spec for spec in (whole, whole, whole, wide) for _ in parts],
+            out_specs=[block, block],
+        ),
+        out_shape=[result, result],
         compiler_params=pltpu.CompilerParams(vmem_limit_bytes=VMEM_LIMIT),
         cost_estimate=pl.CostEstimate(
-            flops=2 * rows * width * width * (1 + 2 * fold),
-            bytes_accessed=2 * (rows + devices * share) * width * units,
+            flops=2 * len(parts) * rows * width * width * units,
+            bytes_accessed=2 * (len(parts) * rows + width) * width * units,
             transcendentals=0,
         ),
-        name="weight_grads",
-    )(active, grad_down, hidden, grad_up, context, attended, sums)
-
-
-def finish_kernel(
-    core_ref, query_grad_ref, key_grad_ref, value_grad_ref, tokens_ref, query_ref, key_ref, value_ref,
-    partial_ref, out_ref, sum_ref, bias_ref,
-):
-    devices, _, share, cols = query_ref.shape
-    width = devices * share
+        name="up_grads",
+    )(core, *[part[at] for at in range(4) for part in parts])
+
+
+def down_grad_kernel(parts, core_ref, *refs):
+    groups = [refs[at * parts : (at + 1) * parts] for at in range(3)]
+    active, grad_down, sums = groups
+    keep_ref, send_ref = refs[3 * parts :]
+    _, n_blk, units, share, width = keep_ref.shape
+    fold = units - 1
+    total = None
+    for one, other in zip(active, grad_down):
+        part = dot_f32(one[...], other[...], TN)
+        total = part if total is None else total + part
+    total = total.astype(keep_ref.dtype).reshape(2, n_blk, fold, share, width)
+    low, high = total[0], total[1]
+    keep_ref[0, :, :fold] = jnp.where(core_ref[0] == 0, low, high)
+    send_ref[0, :, :fold] = jnp.where(core_ref[0] == 0, high, low)
+    total = sums[0][...]
+    for item in sums[1:]:
+        total = total + item[...]
+    pad = jnp.zeros((share - total.shape[0], width), jnp.float32)
+    lines = jnp.concatenate([total, pad], axis=0).astype(keep_ref.dtype)
+    lines = jnp.broadcast_to(lines[None], (n_blk, share, width))
+    keep_ref[0, :, fold] = lines
+    send_ref[0, :, fold] = lines
+
+
+def down_grads(core, parts, sizes):
+    n_pair, n_blk = sizes
+    rows, width = parts[0][1].shape
+    fold = parts[0][0].shape[1] // width
+    share, units = width // (2 * n_pair * n_blk), 1 + fold
+    result = jax.ShapeDtypeStruct((n_pair, n_blk, units, share, width), jnp.bfloat16)
+    block = pl.BlockSpec((1, n_blk, units, share, width), lambda at, core: (at, 0, 0, 0, 0))
+    whole = pl.BlockSpec((rows, width), lambda at, core: (0, 0))
+    wide = pl.BlockSpec((rows, width), lambda at, core: (0, at))
+    sums = pl.BlockSpec(parts[0][2].shape, lambda at, core: (0, 0))
+    return pl.pallas_call(
+        functools.partial(down_grad_kernel, len(parts)),
+        grid_spec=pltpu.PrefetchScalarGridSpec(
+            num_scalar_prefetch=1,
+            grid=(n_pair,),
+            in_specs=[spec for spec in (wide, whole, sums) for _ in parts],
+            out_specs=[block, block],
+        ),
+        out_shape=[result, result],
+        compiler_params=pltpu.CompilerParams(vmem_limit_bytes=VMEM_LIMIT),
+        cost_estimate=pl.CostEstimate(
+            flops=2 * len(parts) * rows * width * width * fold,
+            bytes_accessed=2 * (len(parts) * rows + width) * width * units,
+            transcendentals=0,
+        ),
+        name="down_grads",
+    )(core, *[part[at] for at in range(3) for part in parts])
+
+
+def own_grads_kernel(query_ref, key_ref, value_ref, tokens_ref, out_ref, sum_ref, bias_ref):
+    devices, high, wide = out_ref.shape
+    cols, share = wide // 3, high - 8
     step = pl.program_id(0)
 
     @pl.when(step == 0)
@@ -835,53 +924,72 @@
         bias_ref[...] = jnp.zeros_like(bias_ref)
 
     tokens = tokens_ref[...]
-    total = None
-    for at, (grad_ref, ref) in enumerate(
-        ((query_grad_ref, query_ref), (key_grad_ref, key_ref), (value_grad_ref, value_ref))
-    ):
+    for at, grad_ref in enumerate((query_ref, key_ref, value_ref)):
         grad = grad_ref[...]
         here = slice(at * cols, (at + 1) * cols)
-        part = dot_f32(grad, ref[...].reshape(width, cols), NT)
-        total = part if total is None else total + part
         sum_ref[:, here] += dot_f32(tokens, grad, TN)
         bias_ref[0:1, here] += jnp.sum(grad.astype(jnp.float32), axis=0, keepdims=True)
-    partial_ref[...] = total.astype(partial_ref.dtype)
 
     @pl.when(step == pl.num_programs(0) - 1)
     def _():
-        out_ref[:, :share, :] = sum_ref[...].astype(out_ref.dtype).reshape(devices, share, 3 * cols)
+        out_ref[:, :share, :] = sum_ref[...].astype(out_ref.dtype).reshape(devices, share, wide)
         bias = bias_ref[...].astype(out_ref.dtype)
-        out_ref[:, share:, :] = jnp.broadcast_to(bias[None], (devices, 8, 3 * cols))
-
-
-def finish(core, grads, sequence, first, tile):
+        out_ref[:, share:, :] = jnp.broadcast_to(bias[None], (devices, 8, wide))
+
+
+def own_grads(grads, sequence, devices, tile):
     length, width = sequence.shape
-    devices, _, share, _ = first.shape
-    cols = width // 2
-    thin = pl.BlockSpec((tile, cols), lambda at, core: (at, 0))
-    full = pl.BlockSpec((tile, width), lambda at, core: (at, 0))
+    share, wide = width // devices, 3 * (width // 2)
     return pl.pallas_call(
-        finish_kernel,
-        grid_spec=pltpu.PrefetchScalarGridSpec(
-            num_scalar_prefetch=1,
-            grid=(length // tile,),
-            in_specs=[thin] * 3 + [full] + [weight_columns(first, unit) for unit in range(3)],
-            out_specs=[full, pl.BlockSpec((devices, share + 8, 3 * cols), lambda at, core: (0, 0, 0))],
-            scratch_shapes=[
-                pltpu.VMEM((width, 3 * cols), jnp.float32),
-                pltpu.VMEM((8, 3 * cols), jnp.float32),
-            ],
-        ),
-        out_shape=[
-            jax.ShapeDtypeStruct((length, width), jnp.bfloat16),
-            jax.ShapeDtypeStruct((devices, share + 8, 3 * cols), jnp.bfloat16),
-        ],
+        own_grads_kernel,
+        grid=(length // tile,),
+        in_specs=[pl.BlockSpec((tile, wide // 3), lambda at: (at, 0))] * 3
+        + [pl.BlockSpec((tile, width), lambda at: (at, 0))],
+        out_specs=pl.BlockSpec((devices, share + 8, wide), lambda at: (0, 0, 0)),
+        scratch_shapes=[pltpu.VMEM((width, wide), jnp.float32), pltpu.VMEM((8, wide), jnp.float32)],
+        out_shape=jax.ShapeDtypeStruct((devices, share + 8, wide), jnp.bfloat16),
         compiler_params=pltpu.CompilerParams(vmem_limit_bytes=VMEM_LIMIT),
         cost_estimate=pl.CostEstimate(
-            flops=12 * length * width * cols, bytes_accessed=10 * length * width, transcendentals=0
+            flops=2 * length * width * wide, bytes_accessed=6 * length * width, transcendentals=0
         ),
-        name="finish",
-    )(core, *grads, sequence, first, first, first)
+        name="own_grads",
+    )(*grads, sequence)
+
+
+def tokens_grad_kernel(share, query_ref, key_ref, value_ref, gathered_ref, own_ref, other_ref):
+    total = None
+    for at, grad_ref in enumerate((query_ref, key_ref, value_ref)):
+        part = dot_f32(grad_ref[...], own_weight(gathered_ref, at, share), NT)
+        total = part if total is None else total + part
+    step = lax.rem(pl.program_id(0), 2)
+
+    @pl.when(step == 0)
+    def _():
+        own_ref[...] = total.astype(own_ref.dtype)
+
+    @pl.when(step == 1)
+    def _():
+        other_ref[...] = total.astype(other_ref.dtype)
+
+
+def tokens_grads(grads, gathered, tile):
+    devices, high, cols = gathered.shape
+    length, width, share = grads[0].shape[0], 2 * cols, (high - 8) // 3
+    turn = pl.BlockSpec((tile, width), lambda at: (at // 2, 0))
+    half = jax.ShapeDtypeStruct((length // 2, width), jnp.bfloat16)
+    return pl.pallas_call(
+        functools.partial(tokens_grad_kernel, share),
+        grid=(length // tile,),
+        in_specs=[pl.BlockSpec((tile, cols), lambda at: (at, 0))] * 3
+        + [pl.BlockSpec(gathered.shape, lambda at: (0, 0, 0))],
+        out_specs=[turn, turn],
+        out_shape=[half, half],
+        compiler_params=pltpu.CompilerParams(vmem_limit_bytes=VMEM_LIMIT),
+        cost_estimate=pl.CostEstimate(
+            flops=6 * length * width * cols, bytes_accessed=6 * length * width, transcendentals=0
+        ),
+        name="tokens_grads",
+    )(*grads, gathered)
 
 
 def body(
@@ -915,36 +1023,23 @@
     fold = up_weight.shape[1] // width
     bf16, f32 = jnp.bfloat16, jnp.float32
 
-    def exchange_table(step, back):
-        table = []
+    def table(step, own, back):
+        moves = []
         for pair in range(n_pair):
             for src_core in range(n_core):
                 for src in range(n_blk):
                     piece = src ^ step
+                    side = piece % 2 if own else 1 - piece % 2
                     sender = (pair * n_core + src_core) * n_blk + src
-                    target = (pair * n_core + piece % 2) * n_blk + seqs * src_core + piece // 2
-                    table.append((target, sender) if back else (sender, target))
-        return table
-
-    def to_sequence(array):
-        pieces = array.reshape(n_blk, half, array.shape[-1])
-        return [
-            lax.ppermute(
-                lax.dynamic_index_in_dim(pieces, blk ^ step, 0, keepdims=False),
-                ALL,
-                exchange_table(step, False),
-            )
-            for step in range(n_blk)
-        ]
-
-    def from_sequence(chunks):
-        got = [lax.ppermute(c, ALL, exchange_table(step, True)) for step, c in enumerate(chunks)]
-        bit = 1
-        while bit < n_blk:
-            flip = (blk & bit) != 0
-            got = [jnp.where(flip, got[at ^ bit], got[at]) for at in range(n_blk)]
-            bit *= 2
-        return jnp.concatenate(got, axis=0)
+                    target = (pair * n_core + side) * n_blk + seqs * src_core + piece // 2
+                    moves.append((target, sender) if back else (sender, target))
+        return moves
+
+    def move(array, step, own=True, back=False):
+        return lax.ppermute(array, ALL, table(step, own, back))
+
+    def after(array, *others):
+        return lax.optimization_barrier((array, others))[0]
 
     def other_core(array):
         return lax.ppermute(array, "core", [(0, 1), (1, 0)])
@@ -952,85 +1047,153 @@
     def columns(array, which):
         return lax.dynamic_slice_in_dim(array, which * cols, cols, axis=-1)
 
-    def halve(array, bit, inner):
-        side = (pair & bit) // bit
-        array = array.reshape((-1, 2, inner) + array.shape[1:])
-        kept = lax.dynamic_index_in_dim(array, side, 1, keepdims=False)
-        sent = lax.dynamic_index_in_dim(array, 1 - side, 1, keepdims=False)
-        got = lax.ppermute(sent, "pair", [(at, at ^ bit) for at in range(n_pair)])
-        total = (kept.astype(f32) + got.astype(f32)).astype(bf16)
-        return total.reshape((-1,) + total.shape[2:])
-
-    vectors = (output_bias, up_bias, down_bias, attn_gain, attn_shift, ffn_gain, ffn_shift)
-    coded = jnp.concatenate([lengths // 16, lengths % 16]).astype(bf16)
-    small = [
-        jnp.pad(item, (0, LANES - item.shape[0]))
-        for item in vectors + (query_bias, value_bias, coded)
+    def swap(flip, one, two):
+        return jnp.where(flip, two, one), jnp.where(flip, one, two)
+
+    def ordered(me, items):
+        bit = 1
+        while bit < len(items):
+            flip = (me & bit) != 0
+            items = [jnp.where(flip, items[at ^ bit], items[at]) for at in range(len(items))]
+            bit *= 2
+        return items
+
+    def others(array, axis, size):
+        return [
+            lax.ppermute(array, axis, [(at, at ^ step) for at in range(size)])
+            for step in range(1, size)
+        ]
+
+    which = jnp.reshape(core, (1,)).astype(jnp.int32)
+    mine, theirs, second = pack(
+        which,
+        (query_weight, key_weight, value_weight, output_weight, up_weight, down_weight),
+        (query_bias, value_bias, output_bias, up_bias, down_bias)
+        + (attn_gain, attn_shift, ffn_gain, ffn_shift),
+    )
+    gathered = jnp.stack(swap(core == 1, mine, other_core(theirs)))
+    gathered = jnp.stack(ordered(blk, [gathered] + others(gathered, "blk", n_blk)), axis=1)
+    tokens_moved, second = after(tokens, gathered), after(second, gathered)
+    gathered = jnp.stack(ordered(pair, [gathered] + others(gathered, "pair", n_pair)))
+    gathered = gathered.reshape(devices, 3 * share + 8, cols)
+    second = lax.all_gather(second, ALL, axis=0)
+    both = jnp.concatenate(swap(core == 1, lengths, other_core(lengths)))
+    own_length = lax.dynamic_index_in_dim(both, blk, 0, keepdims=False)
+
+    parts = n_blk // 2
+    pieces = tokens_moved.reshape(n_blk, half, width)
+    arrived = [
+        move(lax.dynamic_index_in_dim(pieces, blk ^ step, 0, keepdims=False), step)
+        for step in range(n_blk)
     ]
-    small = jnp.pad(jnp.stack(small), ((0, share - len(small)), (0, 0)))
-    first, second = pack(
-        (query_weight, key_weight, value_weight, output_weight, up_weight, down_weight), small
-    )
-    first = lax.all_gather(first, ALL, axis=0)
-    second = lax.all_gather(second, ALL, axis=0)
-    code = first[:, 3, 9, : 2 * seqs].astype(jnp.int32)
-    code = (code[:, :seqs] * 16 + code[:, seqs:]).reshape(n_pair, n_core, n_blk, seqs)[:, :, 0]
-    own_length = code.reshape(n_pair, n_core * seqs)[pair, blk]
-    which = jnp.reshape(core, (1,)).astype(jnp.int32)
-
-    arrived = to_sequence(tokens)
-    own_tokens = jnp.concatenate(arrived, axis=0)
-    sequence = jnp.concatenate([own_tokens, other_core(own_tokens)], axis=0)
-    starts = []
-    for side in (core, 1 - core):
-        piece = 2 * (blk % seqs) + side
-        starts += [(piece ^ step) * stretch + side * half for step in range(n_blk)]
+    crossed = other_core(after(jnp.concatenate(arrived, axis=0), gathered))
+    sequence, starts = [], []
+    for part in range(parts):
+        sequence += arrived[2 * part : 2 * part + 2]
+        sequence.append(crossed[2 * part * half : 2 * (part + 1) * half])
+        for side in (core, 1 - core):
+            piece = 2 * (blk % seqs) + side
+            for step in (2 * part, 2 * part + 1):
+                starts.append((piece ^ step) * stretch + side * half)
+    sequence = jnp.concatenate(sequence, axis=0)
     info = jnp.stack([own_length] + starts).astype(jnp.int32)
-
-    qkv = project(which, sequence, first, 512)
-    context_seq, aux = attend(qkv, info, 512, 512)
-    context_low = context_seq.astype(bf16)
-    kept, crossed = context_low[:own_rows], other_core(context_low[own_rows:])
-    joined = jnp.concatenate(
-        [jnp.where(core == 0, kept, crossed), jnp.where(core == 0, crossed, kept)], axis=1
-    )
-    context = from_sequence([joined[at : at + half] for at in range(0, own_rows, half)])
-
-    layer_out, active, grad_down, grad_up, hidden, grad_res, grad_attended, grad_context, sums = feed(
-        context, tokens.reshape(rows, width), cotangent.reshape(rows, width), first, second, 256
-    )
-    own_grad = jnp.concatenate(to_sequence(grad_context), axis=0)
-    context_grad = jnp.concatenate(
-        [columns(own_grad, core), other_core(columns(own_grad, 1 - core))], axis=0
-    )
-
-    second_grads = weight_grads(
-        active, grad_down, hidden, grad_up, context, grad_attended, sums, devices
-    )
-    context_grad, second_grads = lax.optimization_barrier((context_grad, second_grads))
-    second_grads = lax.psum_scatter(second_grads, ALL, scatter_dimension=0)
-
-    grads = attend_back(qkv, context_grad, context_seq, aux, info, 512, 512)
-    partial, first_grads = finish(which, grads, sequence, first, 512)
-    crossed = other_core(partial[own_rows:])
-    summed = (partial[:own_rows].astype(f32) + crossed.astype(f32)).astype(bf16)
-    returned = from_sequence([summed[at : at + half] for at in range(0, own_rows, half)])
-    tokens_grad = (grad_res + returned.astype(f32)).reshape(seqs, stretch, width)
+    odd = blk % 2 == 1
+
+    def quarters(array):
+        return [[array[low : low + half, at : at + cols] for at in (0, cols)] for low in (0, half)]
+
+    def after_all(items, *others):
+        return lax.optimization_barrier((items, others))[0]
+
+    qkv = project(which, sequence, gathered, 512)
+    attended, returning = [], []
+    for part in range(parts):
+        query_side = after(qkv, attended[-1]) if part else qkv
+        attended.append(attend(query_side, info, part, parts, 512, 512))
+        low = attended[-1][0]
+        pieces = [low[at : at + half] for at in range(0, 4 * half, half)]
+        own = [move(pieces[at], 2 * part + at, True, True) for at in range(2)]
+        far = [move(pieces[2 + at], 2 * part + at, False, True) for at in range(2)]
+        returning.append(own + far)
+
+    fed, context, context_grads, kept = [], [], [], ()
+    for part in range(parts):
+        moved = after_all(returning[part], fed[-1] if part else attended[-1])
+        own, far = moved[:2], moved[2:]
+        top = jnp.concatenate([swap(odd, *own)[0], swap(odd, *far)[0]], axis=1)
+        bottom = jnp.concatenate([swap(odd, *far)[1], swap(odd, *own)[1]], axis=1)
+        context.append(jnp.concatenate([top, bottom], axis=0))
+        index = jnp.reshape((blk // 2) ^ part, (1,)).astype(jnp.int32)
+        fed.append(feed(index, context[part], tokens, cotangent, gathered, second, kept, 256))
+        kept = (fed[-1][0],)
+        (top_left, top_right), (low_left, low_right) = quarters(fed[-1][7])
+        own = swap(odd, top_left, low_right)
+        far = swap(odd, top_right, low_left)
+        context_grads.append(
+            [move(own[at], 2 * part + at, True) for at in range(2)]
+            + [move(far[at], 2 * part + at, False) for at in range(2)]
+        )
+    layer_out = kept[0]
+
+    early, late = context_grads[0], context_grads[1]
+    early, context[0] = lax.optimization_barrier((early, context[0]))
+    up_keep, up_send = up_grads(
+        which,
+        [(context[part], item[6], item[4], item[3]) for part, item in enumerate(fed)],
+        (n_pair, n_blk),
+    )
+    own, up_keep = lax.optimization_barrier((late[:2], up_keep))
+    down_keep, down_send = down_grads(
+        which, [(item[1], item[2], after(item[8], up_keep, own)) for item in fed], (n_pair, n_blk)
+    )
+    far, down_keep = lax.optimization_barrier((late[2:], down_keep))
+    total = jnp.concatenate(
+        [
+            (keep.astype(f32) + other_core(send).astype(f32)).astype(bf16)
+            for keep, send in ((up_keep, up_send), (down_keep, down_send))
+        ],
+        axis=2,
+    )
+    second_grads = lax.psum_scatter(total, "pair", scatter_dimension=0)
+    context_grads = [jnp.concatenate(early, axis=0), jnp.concatenate(own + far, axis=0)]
+    context_grads[0] = after(context_grads[0], total)
+    outs, auxes = [item[1] for item in attended], [item[2] for item in attended]
+    grads = attend_back(qkv, context_grads, outs, auxes, info, 0, cols // LANES, 512, 512)
+
+    second_grads, grads = lax.optimization_barrier((second_grads, grads))
+    second_grads = lax.psum_scatter(second_grads, "blk", scatter_dimension=0)
+    first_grads = own_grads(grads, sequence, devices, 512)
+    own, far = tokens_grads([after(item, first_grads) for item in grads], gathered, 512)
+    summed = (own.astype(f32) + other_core(far).astype(f32)).astype(bf16)
+    moved = [
+        move(summed[step * half : (step + 1) * half], step, True, True) for step in range(n_blk)
+    ]
+
+    def to_sum(array, axis, me, size):
+        terms = [lax.dynamic_index_in_dim(array, me, 0, keepdims=False)]
+        for step in range(1, size):
+            sent = lax.dynamic_index_in_dim(array, me ^ step, 0, keepdims=False)
+            terms.append(lax.ppermute(sent, axis, [(at, at ^ step) for at in range(size)]))
+        return terms
+
+    def add(terms):
+        total = terms[0].astype(f32)
+        for term in terms[1:]:
+            total += term.astype(f32)
+        return total.astype(bf16)
 
     first_grads = first_grads.reshape(n_pair, n_core, n_blk, share + 8, 3 * cols)
-    bits = [1 << at for at in range(n_pair.bit_length() - 1)]
-    sides = []
-    for side in range(n_core):
-        part = first_grads[:, side]
-        for bit in bits if side else bits[::-1]:
-            part = halve(part, bit, 1 if side else bit)
-        sides.append(part.reshape(n_blk, share + 8, 3 * cols))
-    part = jnp.stack(sides, axis=1)
-    total = lax.dynamic_index_in_dim(part, blk, 0, keepdims=False).astype(f32)
-    for step in range(1, n_blk):
-        sent = lax.dynamic_index_in_dim(part, blk ^ step, 0, keepdims=False)
-        total += lax.ppermute(sent, "blk", [(at, at ^ step) for at in range(n_blk)]).astype(f32)
-    total = total.astype(bf16)
+    terms, moved[:2] = lax.optimization_barrier(
+        (to_sum(first_grads, "pair", pair, n_pair), moved[:2])
+    )
+    terms = to_sum(jnp.moveaxis(add(terms), 1, 0), "blk", blk, n_blk)
+    returned = []
+    for part in range(parts):
+        back = jnp.concatenate(swap(odd, *moved[2 * part : 2 * part + 2]), axis=0)
+        returned.append(fed[part][5] + back.astype(f32))
+    tokens_grad = jnp.stack(swap(blk >= 2, *returned))
+    terms, tokens_grad = lax.optimization_barrier((terms, tokens_grad))
+    total = add(terms)
     kept = lax.dynamic_index_in_dim(total, core, 0, keepdims=False)
     crossed = other_core(lax.dynamic_index_in_dim(total, 1 - core, 0, keepdims=False))
     left = jnp.where(core == 0, kept, crossed).astype(f32)
@@ -1048,7 +1211,7 @@
     lines = second_grads[1 + 2 * fold]
     own_lines = own_part(lines[:6], share)
     return (
-        (layer_out.reshape(seqs, stretch, width), tokens_grad)
+        (layer_out, tokens_grad)
         + tuple(item[:share] for item in projections)
         + (
             second_grads[0],
@@ -1064,7 +1227,7 @@
 def fits(mesh, tokens, up_weight):
     n_dp, n_blk = mesh.shape["dp"], mesh.shape["blk"]
     batch, length, width = tokens.shape
-    if n_dp % 2 or n_dp & (n_dp - 1) or batch % n_dp or 2 * (batch // n_dp) != n_blk or n_blk & (n_blk - 1):
+    if n_dp % 2 or n_dp & (n_dp - 1) or batch % n_dp or 2 * (batch // n_dp) != n_blk or n_blk != 4:
         return False
     share = width // (n_dp * n_blk)
     fold = up_weight.shape[1] // width
@@ -1075,8 +1238,8 @@
         and share * n_dp * n_blk == width
         and share % 8 == 0
         and 16 <= share
-        and fold * share <= LANES
-        and (6 + fold) * share <= width
+        and (8 + fold) * share <= width // 2
+        and fold == n_dp // 2
         and length % (16 * n_blk) == 0
         and length % 512 == 0
         and length <= 4096

time: 526 us -> 495 us (0.941)
  waiting for transfers between devices: 211 us -> 118 us
  starting transfers between devices: 51.6 us -> 93.5 us
  Pallas kernels: 201 us -> 216 us
  local copies, waits for them, and re-layouts: 23.3 us -> 17.8 us
    ppermute x23 -> x36, waiting for transfers between devices: 186 us -> 113 us  [the longest x24 81.2 us: move(): return lax.ppermute(array, ALL, table(step, own, back))]
    ppermute x23 -> x36, starting transfers between devices: 47.5 us -> 88.9 us  [the longest x24 74.9 us: move(): return lax.ppermute(array, ALL, table(step, own, back))]
    all_gather x1 -> x0, waiting for transfers between devices: 19.6 us -> none  [body(): first = lax.all_gather(first, ALL, axis=0)]
    pallas_call x7 -> x11, Pallas kernels: 201 us -> 216 us  [the longest x1 75.6 us: attend_back(): pl.pallas_call(functools.partial(attend_back_kernel, span, per_part), gri...]
  transfers between devices with their start and end apart: 31 -> 46, of which waited for: 25 -> 16; matrix products, arithmetic and copies ran while one was open for 5% -> 6% of each run, Pallas kernels for 30% -> 40%
where the time goes in v3:
time: 495 us; the launch traced here: 486 us
  Pallas kernels  216 us (44%)
  waiting for transfers between devices  118 us (24%)
  starting transfers between devices  93.5 us (19%)
  other arithmetic  26 us (5%)
  local copies, waits for them, and re-layouts  17.8 us (4%)
  between operations  14.8 us (3%)
    ppermute x24, waiting for transfers between devices, move(): return lax.ppermute(array, ALL, table(step, own, back))  81.2 us
    pallas_call x1, Pallas kernels, attend_back(): pl.pallas_call(functools.partial(attend_back_kernel, span, per_part), gri...  75.6 us
    ppermute x24, starting transfers between devices, move(): return lax.ppermute(array, ALL, table(step, own, back))  74.9 us
    pallas_call x2, Pallas kernels, feed(): pl.pallas_call(functools.partial(feed_kernel, len(kept)), grid_spec=pltpu...  47.7 us
    pallas_call x2, Pallas kernels, attend(): pl.pallas_call(functools.partial(attend_kernel, span), grid=(tiles, rows...  41.2 us
    ppermute x6, waiting for transfers between devices, to_sum(): lax.ppermute(sent, axis, [(at, at ^ step) for at in range(size)])  23.8 us
    pallas_call x1, Pallas kernels, up_grads(): pl.pallas_call(functools.partial(up_grad_kernel, len(parts)), grid_spec=p...  11.8 us
  transfers between devices with their start and end apart: 46, of which 16 were waited for; matrix products, arithmetic and copies ran while one was open for 6% of the time, Pallas kernels for 40%

profile of v3, /device:TPU:9, one launch (start us, length us, event | category | flops | bytes accessed | tf_op | source)
XLA Modules:
  0.0 486.5 jit_solution(16965532462039601212)
XLA Ops:
  15.7 6.3 %collective-permute-done.2 = bf16[2,80,384]{2,1,0:T(8,128)(2,1)S(1)} collective-permute-done((bf16[2,80,384]{2,1,0:T(8,128)(2,1)S(1)}, bf16[2,80,384]{2,1,0:T(8,128)(2,1)S(1)}, u32[]{:S(2)}, u32[]{:S(2)}) %collective-permute-start.2) | collective-permute-done | bytes 122912 | tf_op jit(solution)/shard_map/ppermute | solution.py:1063
  31.0 3.7 collective-permute-start.8
  36.1 6.2 %collective-permute-done.5 = bf16[256,768]{1,0:T(8,128)(2,1)S(1)} collective-permute-done((bf16[256,768]{1,0:T(8,128)(2,1)S(1)}, bf16[256,768]{1,0:T(8,128)(2,1)S(1)}, u32[]{:S(2)}, u32[]{:S(2)}) %collective-permute-start.5) | collective-permute-done | bytes 393248 | tf_op jit(solution)/shard_map/ppermute | solution.py:1039
  45.0 10.9 %collective-permute-done.6 = bf16[256,768]{1,0:T(8,128)(2,1)S(1)} collective-permute-done((bf16[256,768]{1,0:T(8,128)(2,1)S(1)}, bf16[256,768]{1,0:T(8,128)(2,1)S(1)}, u32[]{:S(2)}, u32[]{:S(2)}) %collective-permute-start.6) | collective-permute-done | bytes 393248 | tf_op jit(solution)/shard_map/ppermute | solution.py:1039
  56.9 8.4 %collective-permute-done.8 = bf16[256,768]{1,0:T(8,128)(2,1)S(1)} collective-permute-done((bf16[256,768]{1,0:T(8,128)(2,1)}, bf16[256,768]{1,0:T(8,128)(2,1)S(1)}, u32[]{:S(2)}, u32[]{:S(2)}) %collective-permute-start.8) | collective-permute-done | bytes 393248 | tf_op jit(solution)/shard_map/ppermute | solution.py:1039
  66.1 11.9 %collective-permute-done.7 = bf16[256,768]{1,0:T(8,128)(2,1)} collective-permute-done((bf16[256,768]{1,0:T(8,128)(2,1)}, bf16[256,768]{1,0:T(8,128)(2,1)}, u32[]{:S(2)}, u32[]{:S(2)}) %collective-permute-start.7) | collective-permute-done | bytes 393248 | tf_op jit(solution)/shard_map/ppermute | solution.py:1039
  82.2 2.9 collective-permute-done
  91.0 9.0 %project.1.query_ref.key_ref.value_ref = bf16[2048,1152]{1,0:T(8,128)(2,1)} custom-call(s32[1]{0:T(128)} %bitcast.9.core_ref, bf16[2048,768]{1,0:T(8,128)(2,1)} %copy-done.13, bf16[32,80,384]{2,1,0:T(8,128)(2,1)} %bitcast.104), custom_call_target="tpu_custom_call" | custom-call | flops 3623878656 | bytes 15728640 | tf_op jit(solution)/shard_map/project/pallas_call | solution.py:617
  100.0 20.6 %attend.2 = (bf16[1024,384]{1,0:T(8,128)(2,1)}, f32[1024,384]{1,0:T(8,128)}, bf16[1024,384]{1,0:T(8,128)(2,1)}) custom-call(s32[9]{0:T(128)} %stack.84.info_ref, bf16[2048,1152]{1,0:T(8,128)(2,1)} %project.1.query_ref.key_ref.value_ref, bf16[2048,1152]{1,0:T(8,128)(2,1)} %project.1.query_ref.key_ref.value_ref, ...), custom_call_target="tpu_custom_call" | custom-call | flops 12884901888 | bytes 9437184 | tf_op jit(solution)/shard_map/attend/pallas_call | solution.py:381
  121.9 6.0 %collective-permute-start.17 = (bf16[256,384]{1,0:T(8,128)(2,1)S(1)}, bf16[256,384]{1,0:T(8,128)(2,1)S(1)}, u32[]{:S(2)}, u32[]{:S(2)}) collective-permute-start(bf16[256,384]{1,0:T(8,128)(2,1)S(1)} %get-tuple-element.209), channel_id=1, source_target_pairs={{0,0},{4,1},{1,2},{5,3},{2,4},{6,5},{3,6},{7,7},{8,8},{12,9},{9,10... | collective-permute-start | bytes 589832 | tf_op jit(solution)/shard_map/ppermute | solution.py:1039
  127.9 10.4 %collective-permute-start.18 = (bf16[256,384]{1,0:T(8,128)(2,1)S(1)}, bf16[256,384]{1,0:T(8,128)(2,1)S(1)}, u32[]{:S(2)}, u32[]{:S(2)}) collective-permute-start(bf16[256,384]{1,0:T(8,128)(2,1)S(1)} %get-tuple-element.208), channel_id=1, source_target_pairs={{4,0},{0,1},{5,2},{1,3},{6,4},{2,5},{7,6},{3,7},{12,8},{8,9},{13,1... | collective-permute-start | bytes 589832 | tf_op jit(solution)/shard_map/ppermute | solution.py:1039
  140.5 20.7 %attend.3 = (bf16[1024,384]{1,0:T(8,128)(2,1)}, f32[1024,384]{1,0:T(8,128)}, bf16[1024,384]{1,0:T(8,128)(2,1)}) custom-call(s32[9]{0:T(128)} %stack.84.info_ref, bf16[2048,1152]{1,0:T(8,128)(2,1)} %project.1.query_ref.key_ref.value_ref, bf16[2048,1152]{1,0:T(8,128)(2,1)} %project.1.query_ref.key_ref.value_ref, ...), custom_call_target="tpu_custom_call" | custom-call | flops 12884901888 | bytes 9437184 | tf_op jit(solution)/shard_map/attend/pallas_call | solution.py:381
  164.6 3.0 collective-permute-start.14
  170.7 23.9 %feed.2 = (bf16[2,512,768]{2,1,0:T(8,128)(2,1)}, bf16[512,3072]{1,0:T(8,128)(2,1)}, bf16[512,768]{1,0:T(8,128)(2,1)}, bf16[512,3072]{1,0:T(8,128)(2,1)}, bf16[51...) custom-call(s32[1]{0:T(128)} %bitcast.26.index_ref, ...), custom_call_target="tpu_custom_call" | custom-call | flops 10871635968 | bytes 24772608 | tf_op jit(solution)/shard_map/feed/pallas_call | solution.py:763
  195.9 4.1 collective-permute-start.23
  200.1 2.9 collective-permute-start.24
  203.0 12.7 %collective-permute-start.26 = (bf16[256,384]{1,0:T(8,128)(2,1)S(1)}, bf16[256,384]{1,0:T(8,128)(2,1)S(1)}, u32[]{:S(2)}, u32[]{:S(2)}) collective-permute-start(bf16[256,384]{1,0:T(8,128)(2,1)S(1)} %get-tuple-element.202), channel_id=1, source_target_pairs={{0,0},{1,4},{2,1},{3,5},{4,2},{5,6},{6,3},{7,7},{8,8},{9,12},{10,9... | collective-permute-start | bytes 589832 | tf_op jit(solution)/shard_map/ppermute | solution.py:1039
  216.8 23.9 %feed.3 = (bf16[2,512,768]{2,1,0:T(8,128)(2,1)}, bf16[512,3072]{1,0:T(8,128)(2,1)}, bf16[512,768]{1,0:T(8,128)(2,1)}, bf16[512,3072]{1,0:T(8,128)(2,1)}, bf16[51...) custom-call(s32[1]{0:T(128)} %bitcast.index_ref, ...), custom_call_target="tpu_custom_call", output_to_operand_aliasing={{0}: (6, {})} | custom-call | flops 10871635968 | bytes 24772608 | tf_op jit(solution)/shard_map/feed/pallas_call | solution.py:763
  242.5 6.6 %collective-permute-start.22 = (bf16[256,384]{1,0:T(8,128)(2,1)S(1)}, bf16[256,384]{1,0:T(8,128)(2,1)S(1)}, u32[]{:S(2)}, u32[]{:S(2)}) collective-permute-start(bf16[256,384]{1,0:T(8,128)(2,1)S(1)} %get-tuple-element.200), channel_id=1, source_target_pairs={{0,5},{1,1},{2,4},{3,0},{4,7},{5,3},{6,6},{7,2},{8,13},{9,9},{10,1... | collective-permute-start | bytes 589832 | tf_op jit(solution)/shard_map/ppermute | solution.py:1039
  249.2 11.8 %up_grads.1 = (bf16[4,4,5,24,768]{4,3,2,1,0:T(8,128)(2,1)}, bf16[4,4,5,24,768]{4,3,2,1,0:T(8,128)(2,1)}) custom-call(s32[1]{0:T(128)} %bitcast.9.core_ref, bf16[512,768]{1,0:T(8,128)(2,1)} %maximum_maximum_fusion.context_ref.refs_0_, bf16[512,768]{1,0:T(8,128)(2,1)} %maximum_maximum_fusion.1.context_ref.refs_1_, ...), custom_call_target="tpu_custom_call" | custom-call | flops 6039797760 | bytes 13762560 | tf_op jit(solution)/shard_map/up_grads/pallas_call | solution.py:844
  261.1 9.5 %down_grads.1 = (bf16[4,4,5,24,768]{4,3,2,1,0:T(8,128)(2,1)}, bf16[4,4,5,24,768]{4,3,2,1,0:T(8,128)(2,1)}) custom-call(s32[1]{0:T(128)} %bitcast.9.core_ref, bf16[512,3072]{1,0:T(8,128)(2,1)} %get-tuple-element.115.refs_0_, bf16[512,3072]{1,0:T(8,128)(2,1)} %get-tuple-element.136.refs_1_, bf16[512,768]{1,0:T(8,128)(2,1)} %get-tuple-element.116.refs_2_, ...), custom_call_target="tpu_custom_call" | custom-call | flops 4831838208 | bytes 13762560 | tf_op jit(solution)/shard_map/down_grads/pallas_call | solution.py:897
  274.3 5.9 %collective-permute-done.28 = bf16[256,384]{1,0:T(8,128)(2,1)S(1)} collective-permute-done((bf16[256,384]{1,0:T(8,128)(2,1)S(1)}, bf16[256,384]{1,0:T(8,128)(2,1)S(1)}, u32[]{:S(2)}, u32[]{:S(2)}) %collective-permute-start.28) | collective-permute-done | bytes 196640 | tf_op jit(solution)/shard_map/ppermute | solution.py:1039
  284.6 3.0 pad_maximum_fusion
  289.9 75.6 %attend_back.1 = (bf16[2048,384]{1,0:T(8,128)(2,1)}, bf16[2048,384]{1,0:T(8,128)(2,1)}, bf16[2048,384]{1,0:T(8,128)(2,1)}) custom-call(s32[9]{0:T(128)} %stack.84.info_ref, bf16[2048,1152]{1,0:T(8,128)(2,1)} %project.1.query_ref.key_ref.value_ref, bf16[2048,1152]{1,0:T(8,128)(2,1)} %project.1.query_ref.key_ref.value_ref, ...), custom_call_target="tpu_custom_call" | custom-call | flops 64424509440 | bytes 17301504 | tf_op jit(solution)/shard_map/attend_back/pallas_call | solution.py:479
  365.5 9.2 %own_grads.1 = bf16[32,32,1152]{2,1,0:T(8,128)(2,1)} custom-call(bf16[2048,384]{1,0:T(8,128)(2,1)} %get-tuple-element.159.query_ref, bf16[2048,384]{1,0:T(8,128)(2,1)} %get-tuple-element.160.key_ref, bf16[2048,384]{1,0:T(8,128)(2,1)} %get-tuple-element.161.value_ref, bf16[2048,768]{1,0:T(8,128)(2,1)} %copy-done.13), custom_call_target="tpu_custom_call" | custom-call | flops 3623878656 | bytes 9437184 | tf_op jit(solution)/shard_map/own_grads/pallas_call | solution.py:943
  374.7 9.6 %tokens_grads.1 = (bf16[1024,768]{1,0:T(8,128)(2,1)}, bf16[1024,768]{1,0:T(8,128)(2,1)}) custom-call(bf16[2048,384]{1,0:T(8,128)(2,1)} %get-tuple-element.159.query_ref, bf16[2048,384]{1,0:T(8,128)(2,1)} %get-tuple-element.160.key_ref, bf16[2048,384]{1,0:T(8,128)(2,1)} %get-tuple-element.161.value_ref, bf16[32,80,384]{2,1,0:T(8,128)(2,1)} %bitcast.107), custom_call_target="tpu_custom_call" | custom-call | flops 3623878656 | bytes 9437184 | tf_op jit(solution)/shard_map/tokens_grads/pallas_call | solution.py:980
  393.2 3.9 collective-permute-start.35
  397.6 5.3 %collective-permute-done.31 = bf16[2,4,32,1152]{3,2,1,0:T(8,128)(2,1)S(1)} collective-permute-done((bf16[2,4,32,1152]{3,2,1,0:T(8,128)(2,1)}, bf16[2,4,32,1152]{3,2,1,0:T(8,128)(2,1)S(1)}, u32[]{:S(2)}, u32[]{:S(2)}) %collective-permute-start.31) | collective-permute-done | bytes 589856 | tf_op jit(solution)/shard_map/ppermute | solution.py:1176
  402.8 4.3 collective-permute-start.40
  407.1 8.3 %collective-permute-done.32 = bf16[2,4,32,1152]{3,2,1,0:T(8,128)(2,1)S(1)} collective-permute-done((bf16[2,4,32,1152]{3,2,1,0:T(8,128)(2,1)}, bf16[2,4,32,1152]{3,2,1,0:T(8,128)(2,1)S(1)}, u32[]{:S(2)}, u32[]{:S(2)}) %collective-permute-start.32) | collective-permute-done | bytes 589856 | tf_op jit(solution)/shard_map/ppermute | solution.py:1176
  417.5 36.1 %collective-permute-done.36 = bf16[256,768]{1,0:T(8,128)(2,1)} collective-permute-done((bf16[256,768]{1,0:T(8,128)(2,1)}, bf16[256,768]{1,0:T(8,128)(2,1)}, u32[]{:S(2)}, u32[]{:S(2)}) %collective-permute-start.36) | collective-permute-done | bytes 393248 | tf_op jit(solution)/shard_map/ppermute | solution.py:1039
  460.2 10.2 %collective-permute-done.39 = bf16[2,32,1152]{2,1,0:T(8,128)(2,1)S(1)} collective-permute-done((bf16[2,32,1152]{2,1,0:T(8,128)(2,1)S(1)}, bf16[2,32,1152]{2,1,0:T(8,128)(2,1)S(1)}, u32[]{:S(2)}, u32[]{:S(2)}) %collective-permute-start.39) | collective-permute-done | bytes 147488 | tf_op jit(solution)/shard_map/ppermute | solution.py:1176
  (167 shorter events, 84.9 us)
Async XLA Ops:
  7.2 163.5 %all-gather.3.cloned.1.call-start = ((), (), s32[]{:S(2)}) async-start(), calls=%async_computation.3 | async-start | bytes 10948608 | tf_op jit(solution)/shard_map/all_gather | solution.py:1079
  25.1 340.4 %reduce-scatter.7.cloned.1.call-start = ((), (), s32[]{:S(2)}) async-start(), calls=%async_computation.4 | async-start | bytes 7372800
  26.2 16.1 %collective-permute-start.5 = (bf16[256,768]{1,0:T(8,128)(2,1)S(1)}, bf16[256,768]{1,0:T(8,128)(2,1)S(1)}, u32[]{:S(2)}, u32[]{:S(2)}) collective-permute-start(bf16[256,768]{1,0:T(8,128)(2,1)S(1)} %get-tuple-element.193), channel_id=1, source_target_pairs={{0,0},{1,4},{2,1},{3,5},{4,2},{5,6},{6,3},{7,7},{8,8},{9,12},{10,9... | collective-permute-start | bytes 1179656 | tf_op jit(solution)/shard_map/ppermute | solution.py:1039
  28.1 27.9 %collective-permute-start.6 = (bf16[256,768]{1,0:T(8,128)(2,1)S(1)}, bf16[256,768]{1,0:T(8,128)(2,1)S(1)}, u32[]{:S(2)}, u32[]{:S(2)}) collective-permute-start(bf16[256,768]{1,0:T(8,128)(2,1)S(1)} %get-tuple-element.192), channel_id=1, source_target_pairs={{0,4},{1,0},{2,5},{3,1},{4,6},{5,2},{6,7},{7,3},{8,12},{9,8},{10,1... | collective-permute-start | bytes 1179656 | tf_op jit(solution)/shard_map/ppermute | solution.py:1039
  31.0 34.3 %collective-permute-start.8 = (bf16[256,768]{1,0:T(8,128)(2,1)}, bf16[256,768]{1,0:T(8,128)(2,1)S(1)}, u32[]{:S(2)}, u32[]{:S(2)}) collective-permute-start(bf16[256,768]{1,0:T(8,128)(2,1)} %get-tuple-element.191), channel_id=1, source_target_pairs={{0,5},{1,1},{2,4},{3,0},{4,7},{5,3},{6,6},{7,2},{8,13},{9,9},{10,1... | collective-permute-start | bytes 1179656 | tf_op jit(solution)/shard_map/ppermute | solution.py:1039
  34.7 43.2 %collective-permute-start.7 = (bf16[256,768]{1,0:T(8,128)(2,1)}, bf16[256,768]{1,0:T(8,128)(2,1)}, u32[]{:S(2)}, u32[]{:S(2)}) collective-permute-start(bf16[256,768]{1,0:T(8,128)(2,1)} %get-tuple-element.190), channel_id=1, source_target_pairs={{0,1},{1,5},{2,0},{3,4},{4,3},{5,7},{6,2},{7,6},{8,9},{9,13},{10,8... | collective-permute-start | bytes 1179656 | tf_op jit(solution)/shard_map/ppermute | solution.py:1039
  34.8 44.6 %collective-permute-start.10 = (bf16[2,4,80,384]{3,2,0,1:T(8,128)(2,1)}, bf16[2,4,80,384]{3,2,0,1:T(8,128)(2,1)S(1)}, u32[]{:S(2)}, u32[]{:S(2)}) collective-permute-start(bf16[2,4,80,384]{3,2,0,1:T(8,128)(2,1)} %pad_maximum_fusion.8), channel_id=1, source_target_pairs={{0,16},{8,24},{16,0},{24,8},{1,17},{9,25},{17,1},{25,9},{2,18},{10... | collective-permute-start | bytes 1474568 | tf_op jit(solution)/shard_map/ppermute | solution.py:1063
  42.3 37.1 %collective-permute-start.9 = (bf16[2,4,80,384]{3,2,0,1:T(8,128)(2,1)}, bf16[2,4,80,384]{3,2,0,1:T(8,128)(2,1)S(1)}, u32[]{:S(2)}, u32[]{:S(2)}) collective-permute-start(bf16[2,4,80,384]{3,2,0,1:T(8,128)(2,1)} %pad_maximum_fusion.8), channel_id=1, source_target_pairs={{0,24},{8,16},{16,8},{24,0},{1,25},{9,17},{17,9},{25,1},{2,26},{10... | collective-permute-start | bytes 1474568 | tf_op jit(solution)/shard_map/ppermute | solution.py:1063
  56.0 23.4 %collective-permute-start.11 = (bf16[2,4,80,384]{3,2,0,1:T(8,128)(2,1)}, bf16[2,4,80,384]{3,2,0,1:T(8,128)(2,1)S(1)}, u32[]{:S(2)}, u32[]{:S(2)}) collective-permute-start(bf16[2,4,80,384]{3,2,0,1:T(8,128)(2,1)} %pad_maximum_fusion.8), channel_id=1, source_target_pairs={{0,8},{8,0},{16,24},{24,16},{1,9},{9,1},{17,25},{25,17},{2,10},{10... | collective-permute-start | bytes 1474568 | tf_op jit(solution)/shard_map/ppermute | solution.py:1063
  121.9 42.7 %collective-permute-start.17 = (bf16[256,384]{1,0:T(8,128)(2,1)S(1)}, bf16[256,384]{1,0:T(8,128)(2,1)S(1)}, u32[]{:S(2)}, u32[]{:S(2)}) collective-permute-start(bf16[256,384]{1,0:T(8,128)(2,1)S(1)} %get-tuple-element.209), channel_id=1, source_target_pairs={{0,0},{4,1},{1,2},{5,3},{2,4},{6,5},{3,6},{7,7},{8,8},{12,9},{9,10... | collective-permute-start | bytes 589832 | tf_op jit(solution)/shard_map/ppermute | solution.py:1039
  127.9 39.7 %collective-permute-start.18 = (bf16[256,384]{1,0:T(8,128)(2,1)S(1)}, bf16[256,384]{1,0:T(8,128)(2,1)S(1)}, u32[]{:S(2)}, u32[]{:S(2)}) collective-permute-start(bf16[256,384]{1,0:T(8,128)(2,1)S(1)} %get-tuple-element.208), channel_id=1, source_target_pairs={{4,0},{0,1},{5,2},{1,3},{6,4},{2,5},{7,6},{3,7},{12,8},{8,9},{13,1... | collective-permute-start | bytes 589832 | tf_op jit(solution)/shard_map/ppermute | solution.py:1039
  138.3 31.2 %collective-permute-start.19 = (bf16[256,384]{1,0:T(8,128)(2,1)S(1)}, bf16[256,384]{1,0:T(8,128)(2,1)S(1)}, u32[]{:S(2)}, u32[]{:S(2)}) collective-permute-start(bf16[256,384]{1,0:T(8,128)(2,1)S(1)} %get-tuple-element.207), channel_id=1, source_target_pairs={{4,0},{0,1},{5,2},{1,3},{6,4},{2,5},{7,6},{3,7},{12,8},{8,9},{13,1... | collective-permute-start | bytes 589832 | tf_op jit(solution)/shard_map/ppermute | solution.py:1039
  138.3 31.2 %collective-permute-start.20 = (bf16[256,384]{1,0:T(8,128)(2,1)S(1)}, bf16[256,384]{1,0:T(8,128)(2,1)S(1)}, u32[]{:S(2)}, u32[]{:S(2)}) collective-permute-start(bf16[256,384]{1,0:T(8,128)(2,1)S(1)} %get-tuple-element.206), channel_id=1, source_target_pairs={{0,0},{4,1},{1,2},{5,3},{2,4},{6,5},{3,6},{7,7},{8,8},{12,9},{9,10... | collective-permute-start | bytes 589832 | tf_op jit(solution)/shard_map/ppermute | solution.py:1039
  162.5 33.4 %collective-permute-start.13 = (bf16[256,384]{1,0:T(8,128)(2,1)S(1)}, bf16[256,384]{1,0:T(8,128)(2,1)S(1)}, u32[]{:S(2)}, u32[]{:S(2)}) collective-permute-start(bf16[256,384]{1,0:T(8,128)(2,1)S(1)} %get-tuple-element.213), channel_id=1, source_target_pairs={{1,0},{5,1},{0,2},{4,3},{3,4},{7,5},{2,6},{6,7},{9,8},{13,9},{8,10... | collective-permute-start | bytes 589832 | tf_op jit(solution)/shard_map/ppermute | solution.py:1039
  164.6 31.3 %collective-permute-start.14 = (bf16[256,384]{1,0:T(8,128)(2,1)S(1)}, bf16[256,384]{1,0:T(8,128)(2,1)S(1)}, u32[]{:S(2)}, u32[]{:S(2)}) collective-permute-start(bf16[256,384]{1,0:T(8,128)(2,1)S(1)} %get-tuple-element.212), channel_id=1, source_target_pairs={{5,0},{1,1},{4,2},{0,3},{7,4},{3,5},{6,6},{2,7},{13,8},{9,9},{12,1... | collective-permute-start | bytes 589832 | tf_op jit(solution)/shard_map/ppermute | solution.py:1039
  167.6 28.3 %collective-permute-start.15 = (bf16[256,384]{1,0:T(8,128)(2,1)S(1)}, bf16[256,384]{1,0:T(8,128)(2,1)S(1)}, u32[]{:S(2)}, u32[]{:S(2)}) collective-permute-start(bf16[256,384]{1,0:T(8,128)(2,1)S(1)} %get-tuple-element.211), channel_id=1, source_target_pairs={{5,0},{1,1},{4,2},{0,3},{7,4},{3,5},{6,6},{2,7},{13,8},{9,9},{12,1... | collective-permute-start | bytes 589832 | tf_op jit(solution)/shard_map/ppermute | solution.py:1039
  169.5 26.4 %collective-permute-start.16 = (bf16[256,384]{1,0:T(8,128)(2,1)S(1)}, bf16[256,384]{1,0:T(8,128)(2,1)S(1)}, u32[]{:S(2)}, u32[]{:S(2)}) collective-permute-start(bf16[256,384]{1,0:T(8,128)(2,1)S(1)} %get-tuple-element.210), channel_id=1, source_target_pairs={{1,0},{5,1},{0,2},{4,3},{3,4},{7,5},{2,6},{6,7},{9,8},{13,9},{8,10... | collective-permute-start | bytes 589832 | tf_op jit(solution)/shard_map/ppermute | solution.py:1039
  195.9 46.6 %collective-permute-start.23 = (bf16[256,384]{1,0:T(8,128)(2,1)S(1)}, bf16[256,384]{1,0:T(8,128)(2,1)S(1)}, u32[]{:S(2)}, u32[]{:S(2)}) collective-permute-start(bf16[256,384]{1,0:T(8,128)(2,1)S(1)} %get-tuple-element.203), channel_id=1, source_target_pairs={{0,0},{1,4},{2,1},{3,5},{4,2},{5,6},{6,3},{7,7},{8,8},{9,12},{10,9... | collective-permute-start | bytes 589832 | tf_op jit(solution)/shard_map/ppermute | solution.py:1039
  200.1 49.1 %collective-permute-start.24 = (bf16[256,384]{1,0:T(8,128)(2,1)S(1)}, bf16[256,384]{1,0:T(8,128)(2,1)S(1)}, u32[]{:S(2)}, u32[]{:S(2)}) collective-permute-start(bf16[256,384]{1,0:T(8,128)(2,1)S(1)} %get-tuple-element.204), channel_id=1, source_target_pairs={{0,4},{1,0},{2,5},{3,1},{4,6},{5,2},{6,7},{7,3},{8,12},{9,8},{10,1... | collective-permute-start | bytes 589832 | tf_op jit(solution)/shard_map/ppermute | solution.py:1039
  202.9 46.2 %collective-permute-start.25 = (bf16[256,384]{1,0:T(8,128)(2,1)S(1)}, bf16[256,384]{1,0:T(8,128)(2,1)S(1)}, u32[]{:S(2)}, u32[]{:S(2)}) collective-permute-start(bf16[256,384]{1,0:T(8,128)(2,1)S(1)} %get-tuple-element.205), channel_id=1, source_target_pairs={{0,4},{1,0},{2,5},{3,1},{4,6},{5,2},{6,7},{7,3},{8,12},{9,8},{10,1... | collective-permute-start | bytes 589832 | tf_op jit(solution)/shard_map/ppermute | solution.py:1039
  203.0 46.2 %collective-permute-start.26 = (bf16[256,384]{1,0:T(8,128)(2,1)S(1)}, bf16[256,384]{1,0:T(8,128)(2,1)S(1)}, u32[]{:S(2)}, u32[]{:S(2)}) collective-permute-start(bf16[256,384]{1,0:T(8,128)(2,1)S(1)} %get-tuple-element.202), channel_id=1, source_target_pairs={{0,0},{1,4},{2,1},{3,5},{4,2},{5,6},{6,3},{7,7},{8,8},{9,12},{10,9... | collective-permute-start | bytes 589832 | tf_op jit(solution)/shard_map/ppermute | solution.py:1039
  242.0 19.0 %collective-permute-start.21 = (bf16[256,384]{1,0:T(8,128)(2,1)S(1)}, bf16[256,384]{1,0:T(8,128)(2,1)S(1)}, u32[]{:S(2)}, u32[]{:S(2)}) collective-permute-start(bf16[256,384]{1,0:T(8,128)(2,1)S(1)} %get-tuple-element.199), channel_id=1, source_target_pairs={{0,1},{1,5},{2,0},{3,4},{4,3},{5,7},{6,2},{7,6},{8,9},{9,13},{10,8... | collective-permute-start | bytes 589832 | tf_op jit(solution)/shard_map/ppermute | solution.py:1039
  242.5 18.5 %collective-permute-start.22 = (bf16[256,384]{1,0:T(8,128)(2,1)S(1)}, bf16[256,384]{1,0:T(8,128)(2,1)S(1)}, u32[]{:S(2)}, u32[]{:S(2)}) collective-permute-start(bf16[256,384]{1,0:T(8,128)(2,1)S(1)} %get-tuple-element.200), channel_id=1, source_target_pairs={{0,5},{1,1},{2,4},{3,0},{4,7},{5,3},{6,6},{7,2},{8,13},{9,9},{10,1... | collective-permute-start | bytes 589832 | tf_op jit(solution)/shard_map/ppermute | solution.py:1039
  261.0 20.9 %collective-permute-start.27 = (bf16[4,4,5,24,768]{4,3,2,1,0:T(8,128)(2,1)}, bf16[4,4,5,24,768]{4,3,2,1,0:T(8,128)(2,1)S(1)}, u32[]{:S(2)}, u32[]{:S(2)}) collective-permute-start(bf16[4,4,5,24,768]{4,3,2,1,0:T(8,128)(2,1)} %get-tuple-element.135), channel_id=1, source_target_pairs={{0,4},{4,0},{1,5},{5,1},{2,6},{6,2},{3,7},{7,3},{8,12},{12,8},{9,1... | collective-permute-start | bytes 8847368 | tf_op jit(solution)/shard_map/ppermute | solution.py:1045
  287.7 187.4 %reduce-scatter.5.cloned.1.call-start = ((), (), s32[]{:S(2)}) async-start(), calls=%async_computation.2 | async-start | bytes 1843200 | tf_op jit(solution)/shard_map/reduce_scatter | solution.py:1164
  388.9 26.6 %collective-permute-start.32 = (bf16[2,4,32,1152]{3,2,1,0:T(8,128)(2,1)}, bf16[2,4,32,1152]{3,2,1,0:T(8,128)(2,1)S(1)}, u32[]{:S(2)}, u32[]{:S(2)}) collective-permute-start(bf16[2,4,32,1152]{3,2,1,0:T(8,128)(2,1)} %get-tuple-element.180), channel_id=1, source_target_pairs={{0,16},{8,24},{16,0},{24,8},{1,17},{9,25},{17,1},{25,9},{2,18},{10... | collective-permute-start | bytes 1769480 | tf_op jit(solution)/shard_map/ppermute | solution.py:1176
  390.3 27.2 %collective-permute-start.33 = (bf16[2,4,32,1152]{3,2,1,0:T(8,128)(2,1)S(1)}, bf16[2,4,32,1152]{3,2,1,0:T(8,128)(2,1)S(1)}, u32[]{:S(2)}, u32[]{:S(2)}) collective-permute-start(bf16[2,4,32,1152]{3,2,1,0:T(8,128)(2,1)S(1)} %get-tuple-element.179), channel_id=1, source_target_pairs={{0,24},{8,16},{16,8},{24,0},{1,25},{9,17},{17,9},{25,1},{2,26},{10... | collective-permute-start | bytes 1769480 | tf_op jit(solution)/shard_map/ppermute | solution.py:1176
  393.2 24.3 %collective-permute-start.35 = (bf16[256,768]{1,0:T(8,128)(2,1)}, bf16[256,768]{1,0:T(8,128)(2,1)}, u32[]{:S(2)}, u32[]{:S(2)}) collective-permute-start(bf16[256,768]{1,0:T(8,128)(2,1)} %get-tuple-element.189), channel_id=1, source_target_pairs={{0,0},{4,1},{1,2},{5,3},{2,4},{6,5},{3,6},{7,7},{8,8},{12,9},{9,10... | collective-permute-start | bytes 1179656 | tf_op jit(solution)/shard_map/ppermute | solution.py:1039
  397.1 56.5 %collective-permute-start.36 = (bf16[256,768]{1,0:T(8,128)(2,1)}, bf16[256,768]{1,0:T(8,128)(2,1)}, u32[]{:S(2)}, u32[]{:S(2)}) collective-permute-start(bf16[256,768]{1,0:T(8,128)(2,1)} %get-tuple-element.188), channel_id=1, source_target_pairs={{4,0},{0,1},{5,2},{1,3},{6,4},{2,5},{7,6},{3,7},{12,8},{8,9},{13,1... | collective-permute-start | bytes 1179656 | tf_op jit(solution)/shard_map/ppermute | solution.py:1039
  402.8 55.1 %collective-permute-start.40 = (bf16[256,768]{1,0:T(8,128)(2,1)}, bf16[256,768]{1,0:T(8,128)(2,1)S(1)}, u32[]{:S(2)}, u32[]{:S(2)}) collective-permute-start(bf16[256,768]{1,0:T(8,128)(2,1)} %get-tuple-element.186), channel_id=1, source_target_pairs={{5,0},{1,1},{4,2},{0,3},{7,4},{3,5},{6,6},{2,7},{13,8},{9,9},{12,1... | collective-permute-start | bytes 1179656 | tf_op jit(solution)/shard_map/ppermute | solution.py:1039
  415.5 42.4 %collective-permute-start.41 = (bf16[256,768]{1,0:T(8,128)(2,1)S(1)}, bf16[256,768]{1,0:T(8,128)(2,1)S(1)}, u32[]{:S(2)}, u32[]{:S(2)}) collective-permute-start(bf16[256,768]{1,0:T(8,128)(2,1)S(1)} %get-tuple-element.187), channel_id=1, source_target_pairs={{1,0},{5,1},{0,2},{4,3},{3,4},{7,5},{2,6},{6,7},{9,8},{13,9},{8,10... | collective-permute-start | bytes 1179656 | tf_op jit(solution)/shard_map/ppermute | solution.py:1039
  454.2 16.2 %collective-permute-start.39 = (bf16[2,32,1152]{2,1,0:T(8,128)(2,1)S(1)}, bf16[2,32,1152]{2,1,0:T(8,128)(2,1)S(1)}, u32[]{:S(2)}, u32[]{:S(2)}) collective-permute-start(bf16[2,32,1152]{2,1,0:T(8,128)(2,1)S(1)} %get-tuple-element.219), channel_id=1, source_target_pairs={{0,3},{1,2},{2,1},{3,0},{4,7},{5,6},{6,5},{7,4},{8,11},{9,10},{10,... | collective-permute-start | bytes 442376 | tf_op jit(solution)/shard_map/ppermute | solution.py:1176
  (29 other events, 219.4 us)
Sparse Core Ops, SparseCore 0:
  25.2 102.9 all-gather.2
  287.8 68.2 reduce-scatter.6
  397.7 58.7 reduce-scatter.4
